TPU v7x, 32 devices: a whole 2x2x4 slice. The times are simulated.
32 devices in a mesh: dp: 8 (over z, x), fsdp: 4 (over y, core).
Axes of the slice: x: 2, y: 2, z: 4, core: 2. Of those that a mesh axis runs over, the one named last changes fastest.
Arguments:
- tokens: bfloat16 [32, 169, 1024], P(('dp', 'fsdp')), may hold values from -6 to 6
- out_grad: bfloat16 [32, 169, 1024], P(('dp', 'fsdp')), may hold values from -6 to 6
- text_len: int32 [32], P(('dp', 'fsdp')), may hold values from 12 to 120
- x_bucket: int32 [32, 169], P(('dp', 'fsdp')), may hold values from 0 to 127
- y_bucket: int32 [32, 169], P(('dp', 'fsdp')), may hold values from 0 to 127
- patch_mask: int32 [32, 49], P(('dp', 'fsdp')), may hold values 0 or 1
- qkv_weight: bfloat16 [1024, 3072], P(('dp', 'fsdp')), may hold values from -0.1875 to 0.1875
- qv_bias: bfloat16 [2048], P(('dp', 'fsdp')), may hold values from -3 to 3
- proj_weight: bfloat16 [1024, 1024], P(('dp', 'fsdp')), may hold values from -1 to 1
- proj_bias: bfloat16 [1024], P(('dp', 'fsdp')), may hold values from -2 to 2
- first_gain: bfloat16 [1024], P(('dp', 'fsdp')), may hold values from 0.5 to 1.5
- first_shift: bfloat16 [1024], P(('dp', 'fsdp')), may hold values from -2 to 2
- rel_tables: bfloat16 [6144], P(('dp', 'fsdp')), may hold values from -4 to 4
- up_weight: bfloat16 [1024, 4096], P(('dp', 'fsdp')), may hold values from -0.1875 to 0.1875
- up_bias: bfloat16 [4096], P(('dp', 'fsdp')), may hold values from -3 to 3
- down_weight: bfloat16 [1024, 4096], P(('dp', 'fsdp')), may hold values from -0.09375 to 0.09375
- down_bias: bfloat16 [1024], P(('dp', 'fsdp')), may hold values from -2 to 2
- second_gain: bfloat16 [1024], P(('dp', 'fsdp')), may hold values from 0.5 to 1.5
- second_shift: bfloat16 [1024], P(('dp', 'fsdp')), may hold values from -2 to 2
Outputs:
- encoded: bfloat16 [32, 169, 1024], P(('dp', 'fsdp'))
- grad_tokens: float32 [32, 169, 1024], P(('dp', 'fsdp'))
- grad_qkv: float32 [1024, 3072], P(('dp', 'fsdp'))
- grad_qvbias: float32 [2048], P(('dp', 'fsdp'))
- grad_proj: float32 [1024, 1024], P(('dp', 'fsdp'))
- grad_projbias: float32 [1024], P(('dp', 'fsdp'))
- grad_firstgain: float32 [1024], P(('dp', 'fsdp'))
- grad_firstshift: float32 [1024], P(('dp', 'fsdp'))
- grad_tables: float32 [6144], P(('dp', 'fsdp'))
- grad_up: float32 [1024, 4096], P(('dp', 'fsdp'))
- grad_upbias: float32 [4096], P(('dp', 'fsdp'))
- grad_down: float32 [1024, 4096], P(('dp', 'fsdp'))
- grad_downbias: float32 [1024], P(('dp', 'fsdp'))
- grad_secondgain: float32 [1024], P(('dp', 'fsdp'))
- grad_secondshift: float32 [1024], P(('dp', 'fsdp'))
All inputs are finite; a program needn't handle non-finite values. No bound on the sum of `patch_mask` on one device may be relied on, other than what follows from the above.
Results may differ from a plain program's by a relative error of at most 0.015.
Values may be sent and summed in bfloat16 or wider, within the bound.
No kernel may reach another device: no remote copies, remote signals or barrier semaphores. Data moves between devices by JAX's collectives and lax.ppermute only.
A program may use at most 256 MiB of HBM per device.

v0:
```python
from functools import partial

import jax
import jax.numpy as jnp
from jax import lax
from jax.experimental import pallas as pl
from jax.experimental.pallas import tpu as pltpu
from jax.sharding import PartitionSpec as P

D = 1024
H = 16
HD = 64
FF = 4096
NB = 128
TEXT = 120
SLOTS = 169
ROWS = 176
NEGATIVE = -1e30
EPSILON = 1e-05

f32 = jnp.float32
bf16 = jnp.bfloat16


def shape_of(shape, kind):
    return jax.ShapeDtypeStruct(tuple(shape), kind)


def call(kernel, ins, outs, scratch=(), scalars=0, alias=None, vmem=16):
    spaces = [pltpu.SMEM] * scalars + [pltpu.VMEM] * (len(ins) - scalars)
    return pl.pallas_call(
        kernel,
        in_specs=[pl.BlockSpec(memory_space=m) for m in spaces],
        out_specs=[pl.BlockSpec(memory_space=pltpu.VMEM) for _ in outs],
        out_shape=list(outs),
        scratch_shapes=list(scratch),
        input_output_aliases=alias or {},
        cost_estimate=pl.CostEstimate(flops=0, bytes_accessed=0, transcendentals=0),
        compiler_params=pltpu.CompilerParams(vmem_limit_bytes=vmem * 2**20),
    )(*ins)


def glue(fn, outs, *ins, scalars=0):
    def kernel(*refs):
        made = fn(*refs[: len(ins)])
        for out, value in zip(refs[len(ins) :], made if isinstance(made, tuple) else (made,)):
            out[...] = value

    made = call(kernel, ins, outs, scalars=scalars)
    return made[0] if len(outs) == 1 else made


def axis_bits(axis):
    bits, b = [], lax.axis_size(axis) // 2
    while b >= 1:
        bits.append((axis, b))
        b //= 2
    return bits


def swap(x, bit):
    axis, b = bit
    return lax.ppermute(x, axis, [(i, i ^ b) for i in range(lax.axis_size(axis))])


def side(bit):
    axis, b = bit
    return (lax.axis_index(axis) // b) % 2


def pair_up(mine, other, bit, pos):
    one = side(bit) == 1
    return jnp.stack([jnp.where(one, other, mine), jnp.where(one, mine, other)], axis=pos)


class Order:
    def __init__(self):
        self.last = ()

    def tie(self, args):
        if not self.last:
            return args
        return lax.optimization_barrier(tuple(args) + self.last)[: len(args)]

    def wait(self, *arrays):
        self.last = self.last + arrays

    def __call__(self, fn, *args):
        out = fn(*self.tie(args))
        self.last = tuple(jax.tree.leaves(out))
        return out


def after(x, *earlier):
    return lax.optimization_barrier((x,) + earlier)[0]


def high_bits(axis, order):
    bits = axis_bits(axis)
    return [bits[i] for i in order]


class Gather:
    def __init__(self, run, x, axis, order):
        self.run, self.x = run, x
        self.bits = axis_bits(axis)[3:][::-1] + high_bits(axis, order)
        while len(self.bits) > 3:
            self.send().join()

    def send(self, *earlier):
        self.other = swap(after(self.x, *earlier), self.bits[0])
        return self

    def join(self):
        bit = self.bits.pop(0)
        if len(self.bits) >= 3:
            self.x = self.run(
                lambda m, o: pair_up(m, o, bit, 0).reshape(-1, m.shape[1]), self.x, self.other
            )
        else:
            r, c = self.x.shape

            def join(m, o, out):
                out[:r], out[r:] = m[...], o[...]

            (self.x,) = self.run(
                lambda *ins: call(join, ins, [shape_of((2 * r, c), bf16)]), self.x, self.other
            )
        return self


class Scatter:
    def __init__(self, run, arrays, axis, order, walk=None, base=None, given=None):
        self.run = run
        self.high, rest = high_bits(axis, order), axis_bits(axis)[3:]
        have = self.high[::-1] + rest
        self.order = (high_bits(axis, walk) if walk else self.high[::-1]) + rest
        self.low = len(rest)
        if given is not None:
            have = [bit for bit in have if bit != self.order[0]]
            given = given.reshape((2,) * len(have) + (-1, given.shape[-1]))
        self.given = given
        arrays = tuple(a.reshape((2,) * len(have) + (-1, a.shape[-1])) for a in arrays)
        self.terms = [(arrays, have, [], base or (lambda x: x.astype(f32)))]

    def own(self, array):
        arrays, *rest = self.terms[0]
        self.terms[0] = ((array.reshape(arrays[0].shape),), *rest)

    def flat(self):
        return [a for arrays, *unused in self.terms for a in arrays]

    def value(self, flat, extra=()):
        flat, total = list(flat), None
        for arrays, have, cuts, base in self.terms:
            chosen = dict(list(cuts) + list(extra))
            at = tuple(
                slice(None) if bit not in chosen
                else (0 if chosen[bit] else 1) if bit in self.high
                else side(bit) if chosen[bit] else 1 - side(bit)
                for bit in have
            )
            part = base(*[flat.pop(0)[at] for unused in arrays])
            total = part if total is None else total + part
        return total

    def sum(self, extra=()):
        flat = self.flat()
        fn = lambda *f: self.value(f, extra).astype(bf16)
        if self.low:
            return self.run(fn, *flat)
        out = jax.eval_shape(fn, *flat)
        return self.run(lambda *f: glue(fn, [out], *f), *flat)

    def send(self, *earlier):
        bit = self.order[0]
        out = self.given if self.given is not None else self.sum([(bit, False)])
        self.other = swap(after(out, *earlier), bit)
        return self

    def take(self):
        bit = self.order.pop(0)
        for arrays, have, cuts, base in self.terms:
            if self.given is None:
                cuts.append((bit, True))
        self.given = None
        self.terms.append(((self.other,), list(self.order_left()), [], lambda x: x.astype(f32)))
        while 0 < len(self.order) <= self.low:
            self.send().take()
        return self

    def order_left(self):
        arrays, have, cuts, base = self.terms[0]
        gone = [bit for bit, keep in cuts]
        return [bit for bit in have if bit not in gone]


class Exchange:
    def __init__(self, run, at, give, keep):
        self.run, self.at, self.keep = run, at, keep
        self.other = swap(give, axis_bits("fsdp")[1])

    def turn(self, *earlier):
        def fn(at, keep, got, give, mine):
            y, c = at[0] // 2, at[0] % 2
            give[c], give[1 - c] = keep[1 - y], got[1 - y]
            mine[c], mine[1 - c] = keep[y], got[y]

        out = shape_of(self.keep.shape, self.keep.dtype)
        give, self.mine = self.run(
            lambda *ins: call(fn, ins, [out, out], scalars=1), self.at, self.keep, self.other
        )
        self.other = swap(after(give, *earlier), axis_bits("fsdp")[0])
        return self


def source_of(at, near, n):
    y = at[0] // 2
    return (y if near else 1 - y) * 2 + n


def dot_nn(a, b):
    return jnp.dot(a, b, preferred_element_type=f32)


def dot_nt(a, b):
    return lax.dot_general(a, b, (((1,), (1,)), ((), ())), preferred_element_type=f32)


def dot_tn(a, b):
    return lax.dot_general(a, b, (((0,), (0,)), ((), ())), preferred_element_type=f32)


def call_docs(kernel, docs, ins, in_whole, outs):
    def spec(a, whole):
        n = len(a.shape)
        if whole:
            return pl.BlockSpec(tuple(a.shape), lambda d: (0,) * n)
        return pl.BlockSpec((1,) + tuple(a.shape[1:]), lambda d: (d,) + (0,) * (n - 1))

    return pl.pallas_call(
        kernel,
        grid=(docs,),
        in_specs=[spec(a, w) for a, w in zip(ins, in_whole)],
        out_specs=[spec(a, False) for a in outs],
        out_shape=list(outs),
        cost_estimate=pl.CostEstimate(flops=0, bytes_accessed=0, transcendentals=0),
        compiler_params=pltpu.CompilerParams(vmem_limit_bytes=16 * 2**20),
    )(*ins)


def at_block(ref, me, j, size):
    return pl.ds(pl.multiple_of((me ^ j) * size, size), size)


BLOCK = D // 8
Z_X = (0, 1, 2)
X_Z = (0, 2, 1)
X_FIRST = (2, 1, 0)


def far_block(place, q, order):
    away = sum(((q >> n) & 1) * (4 >> bit) for n, bit in enumerate(order))
    return pl.ds(pl.multiple_of((place ^ away) * BLOCK, BLOCK), BLOCK)


def relative(src, dst, place, order, rows):
    for q in range(8):
        dst[rows, q * BLOCK : (q + 1) * BLOCK] = src[:, far_block(place, q, order)]


def doc_at(j):
    return slice(j * ROWS, (j + 1) * ROWS)


def hot_rows(notes, flip=False):
    buckets = lax.broadcasted_iota(jnp.int32, (NB, ROWS), 0).astype(f32)
    if flip:
        buckets = (NB - 1) - buckets
    return [(notes[r : r + 1, :ROWS] == buckets).astype(f32).astype(bf16) for r in (12, 9, 10)]


ROW_QV, ROW_TABLES, ROW_UP = 6, 7, 9
TILE_ROWS = 16


def pack_kernel(*refs):
    *smalls, out_ref = refs
    rows = smalls[0].shape[1]
    tile = jnp.zeros(out_ref.shape, f32)
    row = lax.broadcasted_iota(jnp.int32, out_ref.shape, 0)
    qv, tables, up = smalls[6:]
    parts = list(smalls[:6]) + [qv] + [tables.at[:, 3 * n * rows : 3 * (n + 1) * rows] for n in range(2)]
    for n, ref in enumerate(parts + [up]):
        value = ref[...].astype(f32)
        wide = jnp.concatenate(
            [value, jnp.zeros((1, 128 - value.shape[1]), f32)], axis=1
        ) if value.shape[1] < 128 else value
        tile = jnp.where(row == n, jnp.broadcast_to(wide, out_ref.shape), tile)
    out_ref[...] = tile.astype(bf16)


def unpack_kernel(heads, count, at_ref, all_ref, ext_ref, add_ref, up_ref, one_ref, two_ref, qv_ref, tab_ref, upb_ref):
    me, place = at_ref[0], at_ref[1]
    rows, width, low = D // count, heads * HD, count // 32
    for d in range(count):
        q = place ^ (d // (4 * low))
        block = (q * low + (d // 4) % low) * 4 + (me ^ (d % 4))
        place_of = pl.ds(pl.multiple_of(block * TILE_ROWS, TILE_ROWS), TILE_ROWS)
        tile = all_ref[place_of, :].astype(f32)
        at = slice(d * rows, (d + 1) * rows)
        one_ref[:, at] = tile[0:3, :rows]
        two_ref[:, at] = tile[3:6, :rows]
        qv_ref[:, 2 * d * rows : 2 * (d + 1) * rows] = tile[ROW_QV : ROW_QV + 1, : 2 * rows]
        for n in range(2):
            start = (2 * d + n) * 3 * rows
            row = tile[ROW_TABLES + n : ROW_TABLES + n + 1, : 3 * rows]
            tab_ref[:, start : start + 3 * rows] = row
        upb_ref[:, 4 * d * rows : 4 * (d + 1) * rows] = tile[ROW_UP : ROW_UP + 1, : 4 * rows]
    start = pl.multiple_of(me * width, width)
    add_ref[:, :width] = qv_ref[:, pl.ds(start, width)]
    add_ref[:, width : 2 * width] = jnp.zeros((1, width), f32)
    add_ref[:, 2 * width :] = qv_ref[:, pl.ds(D + start, width)]
    hidden = up_ref.shape[1]
    up_ref[...] = upb_ref[:, pl.ds(pl.multiple_of(me * hidden, hidden), hidden)]
    half = NB // 2
    for k in range(3):
        for h in range(heads):
            n = k * heads + h
            row = tab_ref[:, pl.ds(pl.multiple_of((k * H + me * heads + h) * NB, NB), NB)]
            ext_ref[n : n + 1, :half] = jnp.broadcast_to(row[:, :1], (1, half))
            ext_ref[n : n + 1, half : half + NB] = row
            ext_ref[n : n + 1, half + NB :] = jnp.broadcast_to(row[:, NB - 1 :], (1, half))


PIECES = 18


def small_grads_kernel(
    heads, count, at_ref, ext_ref, sums_ref, up_ref, one_ref, two_ref, out_ref,
    qv_ref, tab_ref, upb_ref, plain_ref, order_ref,
):
    me = at_ref[0]
    rows, width = D // count, heads * HD
    for ref in (qv_ref, tab_ref, upb_ref, plain_ref):
        ref[...] = jnp.zeros_like(ref)
    start = pl.multiple_of(me * width, width)
    sums = jnp.sum(sums_ref[...], axis=0, keepdims=True)
    qv_ref[:, pl.ds(start, width)] = sums[:, :width]
    qv_ref[:, pl.ds(D + start, width)] = sums[:, 2 * width :]
    hidden = up_ref.shape[1]
    upb_ref[:, pl.ds(pl.multiple_of(me * hidden, hidden), hidden)] = jnp.sum(
        up_ref[...], axis=0, keepdims=True
    )
    half = NB // 2
    lane = lax.broadcasted_iota(jnp.int32, (1, NB), 1)
    for k in range(3):
        for h in range(heads):
            row = ext_ref[k * heads + h : k * heads + h + 1, :]
            low = jnp.sum(row[:, :half], axis=1, keepdims=True)
            high = jnp.sum(row[:, half + NB :], axis=1, keepdims=True)
            grad = row[:, half : half + NB] + jnp.where(lane == 0, low, 0.0)
            grad = grad + jnp.where(lane == NB - 1, high, 0.0)
            tab_ref[:, pl.ds(pl.multiple_of((k * H + me * heads + h) * NB, NB), NB)] = grad
    plain_ref[0:3, :] = one_ref[...]
    plain_ref[3:6, :] = two_ref[...]
    for d in range(count):
        at = slice(d * rows, (d + 1) * rows)
        row = 6
        for ref, times in ((qv_ref, 2), (tab_ref, 6), (upb_ref, 4)):
            for n in range(times):
                begin = (d * times + n) * rows
                plain_ref[row : row + 1, at] = ref[:, begin : begin + rows]
                row += 1
    relative(plain_ref, order_ref, at_ref[1], Z_X, slice(None))
    shape = (plain_ref.shape[0], 128)
    same = lax.broadcasted_iota(jnp.int32, shape, 0) == lax.broadcasted_iota(jnp.int32, shape, 1)
    out_ref[...] = dot_tn(order_ref[...].astype(bf16), same.astype(f32).astype(bf16)).astype(bf16)


def small_outs(total, outs):
    rows = total.shape[0]
    shape = (rows, rows)
    same = lax.broadcasted_iota(jnp.int32, shape, 0) == lax.broadcasted_iota(jnp.int32, shape, 1)
    turned = lax.dot_general(
        total, same.astype(f32), (((0,), (0,)), ((), ())),
        precision=lax.Precision.HIGHEST, preferred_element_type=f32,
    )
    row = 0
    for out in outs:
        for n in range(out.shape[1] // rows):
            out[:, n * rows : (n + 1) * rows] = turned[row : row + 1, :]
            row += 1


def bias_kernel(heads, notes_ref, ext_ref, out_ref):
    notes = notes_ref[0].astype(f32)
    hots = hot_rows(notes)
    every_hot = jnp.concatenate(hots, axis=0)
    live = notes[11:12, :ROWS] > 0.5
    for h in range(heads):
        codes = []
        for k in range(3):
            row = ext_ref[k * heads + h : k * heads + h + 1, :]
            spread = jnp.broadcast_to(row, (NB, 2 * NB))
            skew = pltpu.roll(spread, NB, 1, stride=1, stride_axis=0)
            codes.append(dot_tn(hots[k], skew[:, :NB].astype(bf16)).astype(bf16))
        total = dot_nn(jnp.concatenate(codes, axis=1), every_hot)
        out_ref[0, h] = jnp.where(live, total, NEGATIVE)


def softmax_rows(q, k, bias):
    s = dot_nt(q, k) * 0.125 + bias
    e = jnp.exp(s - jnp.max(s, axis=-1, keepdims=True))
    return e / jnp.sum(e, axis=-1, keepdims=True)


def attend_kernel(heads, pair, at_ref, d0, d1, near_ref, far_ref, add_ref, bias_ref, *rest):
    group_ref, qkv_ref, probs_ref, mixed_ref = rest[-4:]
    width = heads * HD
    for j, piece in zip(pair, (d0, d1)):
        relative(piece, group_ref, at_ref[1], Z_X, doc_at(j))
    both = slice(pair[0] * ROWS, (pair[1] + 1) * ROWS)
    for n in range(3):
        at = slice(n * width, (n + 1) * width)
        qkv = dot_nn(group_ref[both, : D // 2], near_ref[:, at])
        qkv = qkv + dot_nn(group_ref[both, D // 2 :], far_ref[:, at])
        qkv_ref[both, at] = (qkv + add_ref[:, at]).astype(bf16)
    for n, j in enumerate(pair):
        outs = []
        for h in range(heads):
            q = qkv_ref[doc_at(j), h * HD : (h + 1) * HD]
            k = qkv_ref[doc_at(j), width + h * HD : width + (h + 1) * HD]
            v = qkv_ref[doc_at(j), 2 * width + h * HD : 2 * width + (h + 1) * HD]
            probs = softmax_rows(q, k, bias_ref[j, h])
            probs_ref[j, h] = probs
            outs.append(dot_nn(probs.astype(bf16), v).astype(bf16))
        mixed_ref[n] = jnp.concatenate(outs, axis=1)


def norm_parts(values):
    average = jnp.mean(values, axis=-1, keepdims=True)
    centred = values - average
    spread = jnp.mean(centred * centred, axis=-1, keepdims=True)
    scale = lax.rsqrt(spread + EPSILON)
    return centred * scale, scale


def norm_back(grad, gain, hat, scale):
    scaled = grad * gain
    first = jnp.mean(scaled, axis=-1, keepdims=True)
    second = jnp.mean(scaled * hat, axis=-1, keepdims=True)
    return (scaled - first - hat * second) * scale


def first_norm_kernel(
    width, at_ref, a0, a1, a2, a3, *rest
):
    near, far = rest[:4], rest[4:8]
    tokens_ref, vec_ref, att_ref, low_ref, normed_ref, hat_ref, scale_ref, branch_ref, plain_ref = rest[8:]
    me = at_ref[0]
    for j, piece in enumerate((a0[0], a1[...], a2[0], a3[...])):
        plain_ref[:, at_block(plain_ref, me, j, width)] = piece
    relative(plain_ref, att_ref, at_ref[1], Z_X, slice(None))
    left, right = att_ref[:, : D // 2], att_ref[:, D // 2 :]
    for j in range(4):
        branch_ref[:, at_block(branch_ref, me, j, width)] = dot_nn(left, near[j][...]) + dot_nn(
            right, far[j][...]
        )
    resid = tokens_ref[...].astype(f32) + branch_ref[...] + vec_ref[0:1, :]
    hat, scale = norm_parts(resid)
    normed = hat * vec_ref[1:2, :] + vec_ref[2:3, :]
    low_ref[...] = normed.astype(bf16)
    normed_ref[...] = normed
    hat_ref[...] = hat
    scale_ref[...] = scale


def parts_back(left, near_ref, far_ref, outs, place, order):
    for q in range(0, 8, 2):
        ref = near_ref if q < 4 else far_ref
        at = slice((q % 4) * BLOCK, (q % 4 + 2) * BLOCK)
        part = dot_nt(left, ref[at, :])
        for n, out in enumerate(outs):
            for half in range(2):
                block = part[doc_at(n), half * BLOCK : (half + 1) * BLOCK]
                out[:, far_block(place, q + half, order)] = block.astype(out.dtype)


def normal_parts(u):
    density = jnp.exp(-0.5 * u * u)
    return 0.5 + 0.5 * lax.erf(u * (0.5**0.5)), u * density * ((2 * jnp.pi) ** -0.5)


TILE = 256


def up_kernel(pair, at_ref, x0, x1, up_near, up_far, down_near, down_far, add_ref, *rest):
    group_ref, slope_ref, act_ref, keep_ref, give_ref = rest[-5:]
    for j, piece in zip(pair, (x0, x1)):
        relative(piece, group_ref, at_ref[1], Z_X, doc_at(j))
    both = slice(pair[0] * ROWS, (pair[1] + 1) * ROWS)
    for n in range(act_ref.shape[1] // TILE):
        at = slice(n * TILE, (n + 1) * TILE)
        pre = dot_nn(group_ref[both, : D // 2], up_near[:, at])
        pre = pre + dot_nn(group_ref[both, D // 2 :], up_far[:, at]) + add_ref[:, at]
        below, tilt = normal_parts(pre)
        slope_ref[both, at] = below + tilt
        act_ref[both, at] = (pre * below).astype(bf16)
    parts_back(act_ref[both, :], down_near, down_far, (keep_ref, give_ref), at_ref[1], X_Z)


def down_back_kernel(pair, at_ref, g0, g1, down_near, down_far, up_near, up_far, slope_ref, *rest):
    group_ref, dpre_ref, sums_ref, keep_ref, give_ref = rest[-5:]
    for j, piece in zip(pair, (g0, g1)):
        relative(piece, group_ref, at_ref[1], X_Z, doc_at(j))
    both = slice(pair[0] * ROWS, (pair[1] + 1) * ROWS)
    for n in range(dpre_ref.shape[1] // TILE):
        at = slice(n * TILE, (n + 1) * TILE)
        d_act = dot_nn(group_ref[both, : D // 2], down_near[:, at])
        d_act = d_act + dot_nn(group_ref[both, D // 2 :], down_far[:, at])
        d_pre = (d_act * slope_ref[both, at]).astype(bf16)
        dpre_ref[both, at] = d_pre
        sums_ref[pair[0] // 2 : pair[0] // 2 + 1, at] = jnp.sum(d_pre.astype(f32), axis=0, keepdims=True)
    parts_back(dpre_ref[both, :], up_near, up_far, (keep_ref, give_ref), at_ref[1], Z_X)


def second_norm_kernel(
    keep_ref, got_c, got_y, normed_ref, grad_ref, live_ref, vec_ref,
    enc_ref, dffn_ref, dres_ref, sums_ref,
):
    ffn = keep_ref[...] + got_c[...].astype(f32) + got_y[...].astype(f32) + vec_ref[0:1, :]
    hat, scale = norm_parts(normed_ref[...] + ffn)
    ones = jnp.ones((8, 128), bf16)
    live = dot_tn(live_ref[...].astype(bf16), ones)[:, :1]
    gain = vec_ref[1:2, :]
    enc = ((hat * gain + vec_ref[2:3, :]) * live).astype(bf16)
    enc_ref[0] = enc[:SLOTS]
    grad = grad_ref[...].astype(f32) * live
    d_resid = norm_back(grad, gain, hat, scale)
    dres_ref[...] = d_resid
    low = d_resid.astype(bf16)
    dffn_ref[...] = low
    sums_ref[0:1, :] = jnp.sum(low.astype(f32), axis=0, keepdims=True)
    sums_ref[1:2, :] = jnp.sum(grad * hat, axis=0, keepdims=True)
    sums_ref[2:3, :] = jnp.sum(grad, axis=0, keepdims=True)


def first_back_kernel(width, at_ref, keep_ref, got_c, got_y, dres_ref, hat_ref, scale_ref, vec_ref, *rest):
    near, far = rest[:4], rest[4:8]
    branch_ref, done_ref, sums_ref, a0_ref, a1_ref, a2_ref, plain_ref = rest[8:]
    me = at_ref[0]
    hat = hat_ref[...]
    grad = dres_ref[...] + keep_ref[...] + got_c[...].astype(f32) + got_y[...].astype(f32)
    d_one = norm_back(grad, vec_ref[1:2, :], hat, scale_ref[...])
    done_ref[...] = d_one
    low = d_one.astype(bf16)
    branch_ref[...] = low
    sums_ref[0:1, :] = jnp.sum(low.astype(f32), axis=0, keepdims=True)
    sums_ref[1:2, :] = jnp.sum(grad * hat, axis=0, keepdims=True)
    sums_ref[2:3, :] = jnp.sum(grad, axis=0, keepdims=True)
    for n, proj in enumerate((near, far)):
        total = None
        for j in range(4):
            part = dot_nt(branch_ref[:, at_block(branch_ref, me, j, width)], proj[j][...])
            total = part if total is None else total + part
        for q in range(4):
            plain_ref[:, far_block(at_ref[1], 4 * n + q, Z_X)] = total[
                :, q * BLOCK : (q + 1) * BLOCK
            ].astype(bf16)
    for i, out in enumerate((a0_ref, a1_ref, a2_ref.at[0], a2_ref.at[1])):
        out[...] = plain_ref[:, at_block(plain_ref, me, i, width)]


def proj_grad_kernel(width, at_ref, att_ref, branch_ref, *outs):
    me = at_ref[0]
    att = att_ref[...]
    for j, out in enumerate(outs):
        out[...] = dot_tn(att, branch_ref[:, at_block(branch_ref, me, j, width)]).astype(bf16)


def attend_back_kernel(heads, pair, last, qkv_ref, probs_ref, g0, g1, notes_ref, *rest):
    dqkv_ref, sums_ref, grid_ref = rest[-4:-1] if last else rest[-3:]
    width = heads * HD
    for j, grad_ref in zip(pair, (g0.at[0] if last else g0, g1)):
        notes = notes_ref[j].astype(f32)
        hots = jnp.concatenate(hot_rows(notes), axis=0)
        flipped = hot_rows(notes, flip=True)
        for h in range(heads):
            q = qkv_ref[doc_at(j), h * HD : (h + 1) * HD]
            k = qkv_ref[doc_at(j), width + h * HD : width + (h + 1) * HD]
            v = qkv_ref[doc_at(j), 2 * width + h * HD : 2 * width + (h + 1) * HD]
            g = grad_ref[:, h * HD : (h + 1) * HD]
            p = probs_ref[j, h]
            dp = dot_nt(g, v)
            ds = (p * (dp - jnp.sum(p * dp, axis=-1, keepdims=True))).astype(bf16)
            dq = (dot_nn(ds, k) * 0.125).astype(bf16)
            dk = (dot_tn(ds, q) * 0.125).astype(bf16)
            dv = dot_tn(p.astype(bf16), g).astype(bf16)
            for c, d in enumerate((dq, dk, dv)):
                at = slice(c * width + h * HD, c * width + (h + 1) * HD)
                dqkv_ref[doc_at(j), at] = d
            part = dot_nt(ds, hots).astype(bf16)
            for n in range(3):
                term = dot_nn(flipped[n], part[:, n * NB : (n + 1) * NB])
                if j == 0:
                    grid_ref[n * heads + h] = term
                else:
                    grid_ref[n * heads + h] += term
        sums_ref[j : j + 1, :] = jnp.sum(dqkv_ref[doc_at(j), :].astype(f32), axis=0, keepdims=True)
    if last:
        ext_ref = rest[-1]
        for n in range(3 * heads):
            wide = jnp.concatenate([grid_ref[n], jnp.zeros((NB, NB), f32)], axis=1)
            skew = pltpu.roll(wide, 1, 1, stride=1, stride_axis=0)
            ext_ref[n : n + 1, :] = jnp.sum(skew, axis=0, keepdims=True)


def tokens_back_kernel(width, at_ref, d_ref, near_ref, far_ref, *outs):
    for q in range(0, 8, 2):
        ref = near_ref if q < 4 else far_ref
        at = slice((q % 4) * BLOCK, (q % 4 + 2) * BLOCK)
        part = dot_nt(d_ref[...], ref[at, : 3 * width])
        for n, out in enumerate(outs):
            for half in range(2):
                block = part[doc_at(n), half * BLOCK : (half + 1) * BLOCK]
                out[:, far_block(at_ref[1], q + half, Z_X)] = block.astype(out.dtype)


def pad_rows(x):
    return jnp.pad(x, ((0, ROWS - SLOTS), (0, 0)))


def local(
    tokens,
    out_grad,
    text_len,
    x_bucket,
    y_bucket,
    patch_mask,
    qkv_weight,
    qv_bias,
    proj_weight,
    proj_bias,
    first_gain,
    first_shift,
    rel_tables,
    up_weight,
    up_bias,
    down_weight,
    down_bias,
    second_gain,
    second_shift,
):
    inner = axis_bits("fsdp")
    outer = axis_bits("dp")
    tp = 4
    by_y, by_c = inner
    dpn = lax.axis_size("dp")
    n_dev = tp * dpn
    rows = D // n_dev
    heads = H // tp
    width = heads * HD
    hidden = FF // tp
    me = lax.axis_index("fsdp")
    place = lax.axis_index("dp") // (dpn // 8)
    at = jnp.stack([me, place]).astype(jnp.int32)
    run = Order()
    run.wait(at)
    doc_out = shape_of((ROWS, width), bf16)

    def group_of(own):
        far = swap(own, by_y)
        return own, swap(own, by_c), far, swap(far, by_c)

    def second(pair):
        return run(lambda p: glue(lambda ref: ref[1], [doc_out], p), pair)

    def trade(p1, far):
        return swap(p1, by_c), far, swap(second(far), by_c)

    class Meet:
        def near_pair(self, keep, give):
            self.keep, self.near = keep, swap(give, by_c)
            return self

        def far_pair(self, keep, give):
            self.held, self.both = keep, swap(give, by_c)
            return self

        def send(self):
            out = shape_of(self.held.shape, bf16)
            fn = lambda k, g: (k[...].astype(f32) + g[...].astype(f32)).astype(bf16)
            both = run(lambda *ins: glue(fn, [out], *ins), self.held, self.both)
            self.far = swap(both, by_y)
            return self

        def terms(self):
            return self.keep, self.near, self.far

    def column_blocks(shards, groups):
        widths = [a.shape[1] // (g * tp) for a, g in zip(shards, groups)]
        out = shape_of((2, rows, sum(w * g for w, g in zip(widths, groups))), bf16)

        def fn(at, *refs):
            for target, c in ((refs[-2], 1 - at[0] % 2), (refs[-1], at[0] % 2)):
                for y in range(2):
                    start = 0
                    for ref, w, g in zip(refs, widths, groups):
                        for n in range(g):
                            place = pl.multiple_of((n * tp + 2 * y + c) * w, w)
                            target[y, :, start : start + w] = ref[:, pl.ds(place, w)]
                            start += w

        return Exchange(
            run, at,
            *run(lambda *ins: call(fn, ins, [out, out], scalars=1), at, *shards),
        )

    def block_rows(exchanged, parts):
        cols = exchanged.mine.shape[2] // parts

        def fn(at, mine, other, *outs):
            for near, ref in ((True, mine), (False, other)):
                for n in range(2):
                    for p, out in enumerate(outs):
                        out[source_of(at, near, n)] = ref[n, :, p * cols : (p + 1) * cols]

        outs = run(
            lambda *ins: call(fn, ins, [shape_of((tp, rows, cols), bf16)] * parts, scalars=1),
            at, exchanged.mine, exchanged.other,
        )
        return [o.reshape(tp * rows, cols) for o in outs]

    ex_first = column_blocks((qkv_weight, proj_weight), (3, 1))

    smalls = [
        proj_bias, first_gain, first_shift, down_bias, second_gain, second_shift,
        qv_bias, rel_tables, up_bias,
    ]
    flats = [pltpu.VMEM((1, n), f32) for n in (2 * D, 3 * H * NB, FF)]

    places = jnp.arange(TEXT, dtype=jnp.int32)
    live_own = jnp.concatenate(
        [places[None, :] < text_len[:, None], patch_mask > 0], axis=1
    ).astype(f32)

    def document(tokens, x_bucket, y_bucket, live):
        pad_cols = ((0, 0), (0, D - SLOTS))
        positions = (jnp.arange(SLOTS, dtype=jnp.int32) * NB // SLOTS)[None]
        return jnp.concatenate(
            [
                tokens[0],
                jnp.pad(x_bucket.astype(bf16), pad_cols),
                jnp.pad(y_bucket.astype(bf16), pad_cols),
                jnp.pad(live.astype(bf16), pad_cols),
                jnp.pad(positions.astype(bf16), pad_cols),
                jnp.zeros((ROWS - SLOTS - 4, D), bf16),
            ],
            axis=0,
        )

    ex_ffn = column_blocks((up_weight, down_weight), (1, 1))
    ex_first.turn()
    ex_ffn.turn(ex_first.other)
    doc_rows = run(document, tokens, x_bucket, y_bucket, live_own)
    (packed,) = run(
        lambda *ins: call(pack_kernel, [x[None] for x in ins], [shape_of((TILE_ROWS, 128), bf16)]),
        *smalls,
    )

    def beside(m, o):
        r = m.shape[0]

        def join(m, o, out):
            out[:r], out[r:] = m[...], o[...]

        return run(lambda *ins: call(join, ins, [shape_of((2 * r, 128), bf16)]), m, o)[0]

    small_near = swap(packed, by_c)
    grad_in, live_row = run(
        lambda g, l: (pad_rows(g[0]), jnp.pad(l, ((0, 7), (0, ROWS - SLOTS)))), out_grad, live_own
    )
    pair = beside(packed, small_near)
    small_far = swap(pair, by_y)
    g_first = Gather(run, *block_rows(ex_first, 1), "dp", Z_X).send()
    g_small = Gather(run, beside(pair, small_far), "dp", X_FIRST).send()
    doc_far = swap(after(doc_rows, ex_ffn.other, small_far), by_y)
    doc_near = swap(doc_rows, by_c)
    up_own, down_own = block_rows(ex_ffn, 2)
    g_small.join().send()
    g_small.join().send()
    g_down = Gather(run, down_own, "dp", X_Z)
    g_first.join().send()
    g_down.send(g_first.x)
    doc_pieces = (doc_rows, doc_near, doc_far, swap(after(doc_far, g_first.x), by_c))

    def take_notes(*refs):
        for n in range(4):
            refs[4][n] = refs[n][ROWS - 16 :, : 2 * NB]

    (notes,) = run(
        lambda *ins: call(take_notes, ins, [shape_of((tp, 16, 2 * NB), bf16)]), *doc_pieces
    )
    run.wait(g_small.other)
    g_down.join()
    g_first.join().send()
    g_down.send()
    g_up = Gather(run, up_own, "dp", Z_X).send(g_down.x)
    ext, qkv_bias, my_upb, vec_one, vec_two = run(
        lambda *ins: call(
            partial(unpack_kernel, heads, n_dev), ins,
            [
                shape_of((3 * heads, 2 * NB), f32), shape_of((1, 3 * width), f32),
                shape_of((1, hidden), f32), shape_of((3, D), f32), shape_of((3, D), f32),
            ],
            flats, scalars=1,
        ),
        at, beside(g_small.x, g_small.other),
    )

    (bias,) = run(
        lambda *ins: call_docs(
            partial(bias_kernel, heads), tp, ins, [False, True],
            [shape_of((tp, heads, ROWS, ROWS), f32)],
        ),
        notes, ext,
    )
    g_up.join().send()
    col_out = shape_of((D, width), bf16)
    half_out = shape_of((D // 2, width), bf16)

    def proj_part(rows_of):
        return group_of(
            run(lambda w: glue(lambda ref: ref[:, 3 * width :], [half_out], w), rows_of)
        )

    proj_near = proj_part(g_first.x)
    g_up.join()
    run.wait(*proj_near)

    proj_far = proj_part(g_first.other)
    pair_out = shape_of((2, ROWS, width), bf16)
    group_out = shape_of((tp * ROWS, D), bf16)
    qkv_out = shape_of((tp * ROWS, 3 * width), bf16)
    probs_out = shape_of((tp, heads, ROWS, ROWS), f32)
    group, qkv, probs, far = run(
        lambda *ins: call(
            partial(attend_kernel, heads, (2, 3)), ins,
            [group_out, qkv_out, probs_out, pair_out], scalars=1,
        ),
        at, *doc_pieces[2:], g_first.x, g_first.other, qkv_bias, bias,
    )
    mixed_far = swap(far, by_y)
    g_up.send(g_first.other)
    g_down.join().send()
    group, qkv, probs, near = run(
        lambda *ins: call(
            partial(attend_kernel, heads, (0, 1)), ins,
            [group_out, qkv_out, probs_out, pair_out], scalars=1,
            alias={7: 0, 8: 1, 9: 2},
        ),
        at, *doc_pieces[:2], g_first.x, g_first.other, qkv_bias, bias, group, qkv, probs,
    )
    att_pieces = (near, *trade(second(near), mixed_far))

    wide_f = shape_of((ROWS, D), f32)
    wide_b = shape_of((ROWS, D), bf16)
    attended, normed_low, normed_one, hat_one, scale_one = run(
        lambda *ins: call(
            partial(first_norm_kernel, width), ins,
            [wide_b, wide_b, wide_f, wide_f, shape_of((ROWS, 1), f32)],
            [pltpu.VMEM((ROWS, D), f32), pltpu.VMEM((ROWS, D), bf16)], scalars=1,
        ),
        at, *att_pieces, *proj_near, *proj_far, doc_rows, vec_one,
    )

    normed_pieces = group_of(normed_low)
    hid_f = shape_of((tp * ROWS, hidden), f32)
    hid_b = shape_of((tp * ROWS, hidden), bf16)
    ffn_weights = (g_up.x, g_up.other, g_down.x, g_down.other)
    normed_group, slope, act_low, keep, give = run(
        lambda *ins: call(
            partial(up_kernel, (0, 1)), ins, [group_out, hid_f, hid_b, wide_f, wide_b], scalars=1,
        ),
        at, *normed_pieces[:2], *ffn_weights, my_upb,
    )
    meet = Meet().near_pair(keep, give)
    normed_group, slope, act_low, keep, give = run(
        lambda *ins: call(
            partial(up_kernel, (2, 3)), ins, [group_out, hid_f, hid_b, wide_f, wide_b], scalars=1,
            alias={8: 0, 9: 1, 10: 2},
        ),
        at, *normed_pieces[2:], *ffn_weights, my_upb, normed_group, slope, act_low,
    )
    meet.far_pair(keep, give).send()
    encoded, d_ffn, d_resid_two, sums_two = run(
        lambda *ins: call(
            second_norm_kernel, ins,
            [shape_of((1, SLOTS, D), bf16), wide_b, wide_f, shape_of((3, D), f32)],
        ),
        *meet.terms(), normed_one, grad_in, live_row, vec_two,
    )

    d_ffn_pieces = group_of(d_ffn)
    ffn_weights = (g_down.x, g_down.other, g_up.x, g_up.other)
    sums_out = shape_of((2, hidden), f32)
    d_ffn_group, d_pre, d_up_bias, keep, give = run(
        lambda *ins: call(
            partial(down_back_kernel, (0, 1)), ins,
            [group_out, hid_b, sums_out, wide_f, wide_b], scalars=1,
        ),
        at, *d_ffn_pieces[:2], *ffn_weights, slope,
    )
    meet = Meet().near_pair(keep, give)
    d_ffn_group, d_pre, d_up_bias, keep, give = run(
        lambda *ins: call(
            partial(down_back_kernel, (2, 3)), ins,
            [group_out, hid_b, sums_out, wide_f, wide_b], scalars=1,
            alias={8: 0, 9: 1, 10: 2},
        ),
        at, *d_ffn_pieces[2:], *ffn_weights, slope, d_ffn_group, d_pre, d_up_bias,
    )
    meet.far_pair(keep, give)

    def half_grad(left, right, near):
        left = left[:, : D // 2] if near else left[:, D // 2 :]
        return dot_tn(left, right).astype(bf16)

    give = run(partial(half_grad, near=False), d_ffn_group, act_low)
    s_down = Scatter(run, (give,), "dp", X_Z, given=give)
    s_down.send()
    meet.send()
    keep = run(partial(half_grad, near=True), d_ffn_group, act_low)
    s_down.own(keep)
    keep = run(partial(half_grad, near=True), normed_group, d_pre)
    give = run(partial(half_grad, near=False), normed_group, d_pre)
    s_up = Scatter(run, (keep,), "dp", Z_X, given=give).send()

    d_branch, d_resid_one, sums_one, a0, a1, a2 = run(
        lambda *ins: call(
            partial(first_back_kernel, width), ins,
            [wide_b, wide_f, shape_of((3, D), f32), doc_out, doc_out, pair_out],
            [pltpu.VMEM((ROWS, D), bf16)], scalars=1,
        ),
        at, *meet.terms(), d_resid_two, hat_one, scale_one, vec_one, *proj_near, *proj_far,
    )
    far = swap(a2, by_y)
    got_c = swap(a1, by_c)
    parts = run(
        lambda *ins: call(partial(proj_grad_kernel, width), ins, [col_out] * 4, scalars=1),
        at, attended, d_branch,
    )
    meet_proj = Meet().near_pair(parts[0], parts[1]).far_pair(parts[2], parts[3])
    grids = shape_of((3 * heads, NB, NB), f32)
    d_qkv, d_sums, d_grid = run(
        lambda *ins: call(
            partial(attend_back_kernel, heads, (0, 1), False), ins,
            [qkv_out, shape_of((tp, 3 * width), f32), grids],
        ),
        qkv, probs, a0, got_c, notes,
    )
    got_far = swap(second(far), by_c)
    meet_proj.send()
    run.wait(s_up.other, s_down.other)
    s_up.take().send()
    d_qkv, d_sums, d_grid, d_ext = run(
        lambda *ins: call(
            partial(attend_back_kernel, heads, (2, 3), True), ins,
            [qkv_out, shape_of((tp, 3 * width), f32), grids, shape_of((3 * heads, 2 * NB), f32)],
            alias={5: 0, 6: 1, 7: 2},
        ),
        qkv, probs, far, got_far, notes, d_qkv, d_sums, d_grid,
    )

    def columns_grad(group, d_qkv, near):
        left = group[:, : D // 2] if near else group[:, D // 2 :]
        return dot_tn(left, d_qkv[:, : D // 2]).astype(bf16)

    def with_proj(q, k, c, y, small):
        p = (k.astype(f32) + c.astype(f32) + y.astype(f32)).astype(bf16)
        return jnp.concatenate([q, p, small], axis=-1).astype(f32)

    keep = run(partial(columns_grad, near=True), group, d_qkv)
    grad_b = run(lambda g, d: dot_tn(g, d[:, D // 2 :]).astype(bf16), group, d_qkv)
    give = run(partial(columns_grad, near=False), group, d_qkv)
    s_first = Scatter(run, (keep,), "dp", Z_X, given=give).send()
    plains = [pltpu.VMEM((24, D), f32)] * 2
    (small_grads,) = run(
        lambda *ins: call(
            partial(small_grads_kernel, heads, n_dev), ins, [shape_of((D, 128), bf16)],
            flats + plains, scalars=1,
        ),
        at, d_ext, d_sums, d_up_bias, sums_one, sums_two,
    )
    s_second = Scatter(
        run, (grad_b, *meet_proj.terms(), small_grads), "dp", Z_X, walk=(1, 2, 0), base=with_proj
    ).send()
    parts = run(
        lambda *ins: call(
            partial(tokens_back_kernel, width), ins, [wide_f, wide_b, wide_f, wide_b], scalars=1
        ),
        at, d_qkv, g_first.x, g_first.other,
    )
    meet_tok = Meet().near_pair(parts[0], parts[1]).far_pair(parts[2], parts[3])
    s_up.take().send()
    meet_tok.send()
    s_first.take().send()
    s_down.take().send()
    run.wait(s_second.other, s_first.other, s_up.other)
    s_second.take().send()
    s_first.take().send()
    run.wait(s_down.other, s_second.other)
    s_down.take().send()
    s_second.take().send()

    def columns_back(scatters):
        sums = [x.sum().reshape(tp, rows, -1) for x in scatters]
        out = shape_of((2, rows, sum(x.shape[2] for x in sums)), bf16)

        def fn(at, *refs):
            for target, c in ((refs[-2], 1 - at[0] % 2), (refs[-1], at[0] % 2)):
                for y in range(2):
                    target[y] = jnp.concatenate([ref[2 * y + c] for ref in refs[:-2]], axis=1)

        return Exchange(run, at, *run(lambda *ins: call(fn, ins, [out, out], scalars=1), at, *sums))

    def whole_rows(exchanged, groups, widths, smalls):
        outs = [shape_of((rows, tp * g * w), f32) for g, w in zip(groups, widths)]
        ends = [shape_of((1, n * rows), f32) for n in smalls]

        def fn(at, mine, other, *refs):
            outs, ends = refs[: len(groups)], refs[len(groups) :]
            total = None
            for near, ref in ((True, mine), (False, other)):
                for n in range(2):
                    start, f = 0, source_of(at, near, n)
                    for out, g, w in zip(outs, groups, widths):
                        for i in range(g):
                            place = pl.multiple_of((i * tp + f) * w, w)
                            out[:, pl.ds(place, w)] = ref[n, :, start : start + w].astype(f32)
                            start += w
                    part = ref[n, :, start:].astype(f32)
                    total = part if total is None else total + part
            small_outs(total, ends)

        return run(
            lambda *ins: call(fn, ins, outs + ends, scalars=1), at, exchanged.mine, exchanged.other
        )

    out_f = shape_of((1, SLOTS, D), f32)
    grad_tokens = run(
        lambda *ins: glue(
            lambda d, k, c, y: (
                d[...] + k[...] + c[...].astype(f32) + y[...].astype(f32)
            )[:SLOTS][None],
            [out_f], *ins,
        ),
        d_resid_one, *meet_tok.terms(),
    )
    run.wait(s_down.other, s_first.other, s_second.other)
    s_down.take()
    s_up.take()
    s_first.take()
    s_second.take()
    back = columns_back([s_up, s_down, s_first, s_second]).turn()

    grad_up, grad_down, grad_qkv, grad_proj, *out = whole_rows(
        back, (1, 1, 3, 1), (hidden, hidden, width, width), (1,) * 6 + (2, 6, 4)
    )
    out = [x.reshape(-1) for x in out]
    return (
        encoded,
        grad_tokens,
        grad_qkv,
        out[6],
        grad_proj,
        out[0],
        out[1],
        out[2],
        out[7],
        grad_up,
        out[8],
        grad_down,
        out[3],
        out[4],
        out[5],
    )


def solution(mesh):
    split = ("dp", "fsdp")
    one, two, three = P(split), P(split, None), P(split, None, None)
    return jax.shard_map(
        local,
        mesh=mesh,
        in_specs=(
            three, three, one, two, two, two, two, one, two, one, one, one, one, two, one, two,
            one, one, one,
        ),
        out_specs=(
            three, three, two, one, two, one, one, one, one, two, one, two, one, one, one,
        ),
        check_vma=False,
    )
```

profile of v0, /device:TPU:0, one launch (start us, length us, event | category | flops | bytes accessed | tf_op | source)
XLA Modules:
  0.0 277.4 jit_solution(12410864502094271534)
XLA Ops:
  7.6 3.0 %collective-permute-start.3 = (bf16[2,32,1024]{2,1,0:T(8,128)(2,1)S(1)}, bf16[2,32,1024]{2,1,0:T(8,128)(2,1)S(1)}, u32[]{:S(2)}, u32[]{:S(2)}) collective-permute-start(bf16[2,32,1024]{2,1,0:T(8,128)(2,1)S(1)} %get-tuple-element.400), channel_id=1, source_target_pairs={{0,2},{1,3},{2,0},{3,1},{4,6},{5,7},{6,4},{7,5},{8,10},{9,11},{10,... | collective-permute-start | bytes 393224 | tf_op jit(solution)/shard_map/ppermute | solution.py:63
  11.9 2.4 collective-permute-done.3.other
  18.5 2.7 collective-permute-start.5
  21.7 3.1 %collective-permute-done.6.o = bf16[32,128]{1,0:T(8,128)(2,1)S(1)} collective-permute-done((bf16[32,128]{1,0:T(8,128)(2,1)S(1)}, bf16[32,128]{1,0:T(8,128)(2,1)S(1)}, u32[]{:S(2)}, u32[]{:S(2)}) %collective-permute-start.6) | collective-permute-done | bytes 8224 | tf_op jit(solution)/shard_map/ppermute | solution.py:63
  30.6 3.5 %collective-permute-done.9.o = bf16[128,128]{1,0:T(8,128)(2,1)S(1)} collective-permute-done((bf16[128,128]{1,0:T(8,128)(2,1)S(1)}, bf16[128,128]{1,0:T(8,128)(2,1)S(1)}, u32[]{:S(2)}, u32[]{:S(2)}) %collective-permute-start.9) | collective-permute-done | bytes 32800 | tf_op jit(solution)/shard_map/ppermute | solution.py:63
  35.2 3.3 %collective-permute-start.11 = (bf16[128,1024]{1,0:T(8,128)(2,1)S(1)}, bf16[128,1024]{1,0:T(8,128)(2,1)S(1)}, u32[]{:S(2)}, u32[]{:S(2)}) collective-permute-start(bf16[128,1024]{1,0:T(8,128)(2,1)S(1)} %bitcast.85), channel_id=1, source_target_pairs={{0,16},{4,20},{8,24},{12,28},{16,0},{20,4},{24,8},{28,12},{1,17},{... | collective-permute-start | bytes 786440 | tf_op jit(solution)/shard_map/ppermute | solution.py:63
  38.5 14.4 %collective-permute-done.14.o = bf16[256,128]{1,0:T(8,128)(2,1)S(1)} collective-permute-done((bf16[256,128]{1,0:T(8,128)(2,1)S(1)}, bf16[256,128]{1,0:T(8,128)(2,1)S(1)}, u32[]{:S(2)}, u32[]{:S(2)}) %collective-permute-start.14) | collective-permute-done | bytes 65568 | tf_op jit(solution)/shard_map/ppermute | solution.py:63
  53.0 2.2 collective-permute-done.10.o
  58.9 4.1 %shard_map.315.bias_ref = f32[4,4,176,176]{3,2,1,0:T(8,128)S(1)} custom-call(bf16[4,16,256]{2,1,0:T(8,128)(2,1)S(1)} %shard_map.310.notes_ref, f32[12,256]{1,0:T(8,128)S(1)} %get-tuple-element.462.ext_ref), custom_call_target="tpu_custom_call" | custom-call | tf_op jit(solution)/shard_map/pallas_call | solution.py:241
  62.9 7.5 %collective-permute-done.16.o = bf16[128,1024]{1,0:T(8,128)(2,1)S(1)} collective-permute-done((bf16[128,1024]{1,0:T(8,128)(2,1)S(1)}, bf16[128,1024]{1,0:T(8,128)(2,1)S(1)}, u32[]{:S(2)}, u32[]{:S(2)}) %collective-permute-start.16) | collective-permute-done | bytes 262176 | tf_op jit(solution)/shard_map/ppermute | solution.py:63
  71.3 6.4 %collective-permute-done.19.rest_2_ = bf16[512,256]{1,0:T(8,128)(2,1)S(1)} collective-permute-done((bf16[512,256]{1,0:T(8,128)(2,1)S(1)}, bf16[512,256]{1,0:T(8,128)(2,1)S(1)}, u32[]{:S(2)}, u32[]{:S(2)}) %collective-permute-start.19) | collective-permute-done | bytes 262176 | tf_op jit(solution)/shard_map/ppermute | solution.py:63
  77.8 5.4 %collective-permute-done.17.o = bf16[256,1024]{1,0:T(8,128)(2,1)S(1)} collective-permute-done((bf16[256,1024]{1,0:T(8,128)(2,1)S(1)}, bf16[256,1024]{1,0:T(8,128)(2,1)S(1)}, u32[]{:S(2)}, u32[]{:S(2)}) %collective-permute-start.17) | collective-permute-done | bytes 524320 | tf_op jit(solution)/shard_map/ppermute | solution.py:63
  83.4 3.1 %shard_map.320 = (bf16[704,1024]{1,0:T(8,128)(2,1)S(1)}, bf16[704,768]{1,0:T(8,128)(2,1)S(1)}, f32[4,4,176,176]{3,2,1,0:T(8,128)S(1)}, bf16[2,176,256]{2,1,0:T(8,128)(2,1)S(1)}) custom-call(s32[2]{0:T(128)S(1)} %pad_add_fusion.at.at_ref, bf16[176,1024]{1,0:T(8,128)(2,1)S(1)} %collective-permute-done.12.refs_2_.d0, ...), custom_call_target="tpu_custom_call" | custom-call | tf_op jit(solution)/shard_map/pallas_call | solution.py:31
  89.1 3.6 %collective-permute-done.21.o = bf16[256,1024]{1,0:T(8,128)(2,1)S(1)} collective-permute-done((bf16[256,1024]{1,0:T(8,128)(2,1)S(1)}, bf16[256,1024]{1,0:T(8,128)(2,1)S(1)}, u32[]{:S(2)}, u32[]{:S(2)}) %collective-permute-start.21) | collective-permute-done | bytes 524320 | tf_op jit(solution)/shard_map/ppermute | solution.py:63
  95.0 3.1 %shard_map.322 = (bf16[704,1024]{1,0:T(8,128)(2,1)S(1)}, bf16[704,768]{1,0:T(8,128)(2,1)S(1)}, f32[4,4,176,176]{3,2,1,0:T(8,128)S(1)}, bf16[2,176,256]{2,1,0:T(8,128)(2,1)S(1)}) custom-call(s32[2]{0:T(128)S(1)} %pad_add_fusion.at.at_ref, ...), custom_call_target="tpu_custom_call", output_to_operand_aliasing={{0}: (7, {}), {1}: (8, {}), {2}: (9, {})} | custom-call | tf_op jit(solution)/shard_map/pallas_call | solution.py:31
  103.5 9.3 %collective-permute-done.32.x0 = bf16[176,1024]{1,0:T(8,128)(2,1)S(1)} collective-permute-done((bf16[176,1024]{1,0:T(8,128)(2,1)S(1)}, bf16[176,1024]{1,0:T(8,128)(2,1)S(1)}, u32[]{:S(2)}, u32[]{:S(2)}) %collective-permute-start.32) | collective-permute-done | bytes 360480 | tf_op jit(solution)/shard_map/ppermute | solution.py:63
  114.2 2.8 %shard_map.326 = (bf16[704,1024]{1,0:T(8,128)(2,1)S(1)}, f32[704,1024]{1,0:T(8,128)S(1)}, bf16[704,1024]{1,0:T(8,128)(2,1)S(1)}, f32[176,1024]{1,0:T(8,128)S(1)}, bf16[176,1024]{1,0:T(8,128)(2,1)S(1)}) custom-call(s32[2]{0:T(128)S(1)} %pad_add_fusion.at.at_ref, bf16[176,1024]{1,0:T(8,128)(2,1)S(1)} %get-tuple-element.521.x0, ...), custom_call_target="tpu_custom_call" | custom-call | tf_op jit(solution)/shard_map/pallas_call | solution.py:31
  117.1 2.9 %shard_map.327 = (bf16[704,1024]{1,0:T(8,128)(2,1)S(1)}, f32[704,1024]{1,0:T(8,128)S(1)}, bf16[704,1024]{1,0:T(8,128)(2,1)S(1)}, f32[176,1024]{1,0:T(8,128)S(1)}, bf16[176,1024]{1,0:T(8,128)(2,1)S(1)}) custom-call(s32[2]{0:T(128)S(1)} %pad_add_fusion.at.at_ref, ...), custom_call_target="tpu_custom_call", output_to_operand_aliasing={{0}: (8, {}), {1}: (9, {}), {2}: (10, {})} | custom-call | tf_op jit(solution)/shard_map/pallas_call | solution.py:31
  123.6 8.7 %collective-permute-done.35.got_y = bf16[176,1024]{1,0:T(8,128)(2,1)S(1)} collective-permute-done((bf16[176,1024]{1,0:T(8,128)(2,1)S(1)}, bf16[176,1024]{1,0:T(8,128)(2,1)S(1)}, u32[]{:S(2)}, u32[]{:S(2)}) %collective-permute-start.35) | collective-permute-done | bytes 360480 | tf_op jit(solution)/shard_map/ppermute | solution.py:63
  135.5 7.9 %collective-permute-done.38.g0 = bf16[176,1024]{1,0:T(8,128)(2,1)S(1)} collective-permute-done((bf16[176,1024]{1,0:T(8,128)(2,1)S(1)}, bf16[176,1024]{1,0:T(8,128)(2,1)S(1)}, u32[]{:S(2)}, u32[]{:S(2)}) %collective-permute-start.38) | collective-permute-done | bytes 360480 | tf_op jit(solution)/shard_map/ppermute | solution.py:63
  143.5 2.6 shard_map.330
  146.1 2.4 shard_map.331
  158.4 9.2 %collective-permute-done.41.got_y = bf16[176,1024]{1,0:T(8,128)(2,1)S(1)} collective-permute-done((bf16[176,1024]{1,0:T(8,128)(2,1)S(1)}, bf16[176,1024]{1,0:T(8,128)(2,1)S(1)}, u32[]{:S(2)}, u32[]{:S(2)}) %collective-permute-start.41) | collective-permute-done | bytes 360480 | tf_op jit(solution)/shard_map/ppermute | solution.py:63
  173.9 4.9 %shard_map.335 = (bf16[704,768]{1,0:T(8,128)(2,1)S(1)}, f32[4,768]{1,0:T(4,128)S(1)}, f32[12,128,128]{2,1,0:T(8,128)S(1)}) custom-call(bf16[704,768]{1,0:T(8,128)(2,1)S(1)} %get-tuple-element.643.qkv_ref, f32[4,4,176,176]{3,2,1,0:T(8,128)S(1)} %get-tuple-element.644.probs_ref, bf16[176,256]{1,0:T(8,128)(2,1)S(1)} %get-tuple-element.632.g0, ...), custom_call_target="tpu_custom_call" | custom-call | tf_op jit(solution)/shard_map/pallas_call | solution.py:31
  180.4 5.3 %shard_map.339 = (bf16[704,768]{1,0:T(8,128)(2,1)S(1)}, f32[4,768]{1,0:T(4,128)S(1)}, f32[12,128,128]{2,1,0:T(8,128)S(1)}, f32[12,256]{1,0:T(8,128)S(1)}) custom-call(bf16[704,768]{1,0:T(8,128)(2,1)S(1)} %get-tuple-element.643.qkv_ref, ...), custom_call_target="tpu_custom_call", output_to_operand_aliasing={{0}: (5, {}), {1}: (6, {}), {2}: (7, {})} | custom-call | tf_op jit(solution)/shard_map/pallas_call | solution.py:31
  189.8 2.7 shard_map.340
  196.1 5.7 %collective-permute-done.52.refs_2_ = bf16[2,128,1024]{2,1,0:T(8,128)(2,1)S(1)} collective-permute-done((bf16[2,128,1024]{2,1,0:T(8,128)(2,1)S(1)}, bf16[2,128,1024]{2,1,0:T(8,128)(2,1)S(1)}, u32[]{:S(2)}, u32[]{:S(2)}) %collective-permute-start.52) | collective-permute-done | bytes 524320 | tf_op jit(solution)/shard_map/ppermute | solution.py:63
  205.6 14.1 %collective-permute-done.57.refs_3_ = bf16[128,1024]{1,0:T(8,128)(2,1)S(1)} collective-permute-done((bf16[128,1024]{1,0:T(8,128)(2,1)S(1)}, bf16[128,1024]{1,0:T(8,128)(2,1)S(1)}, u32[]{:S(2)}, u32[]{:S(2)}) %collective-permute-start.57) | collective-permute-done | bytes 262176 | tf_op jit(solution)/shard_map/ppermute | solution.py:63
  219.6 6.5 %collective-permute-done.56.refs_2_ = bf16[2,128,512]{2,1,0:T(8,128)(2,1)S(1)} collective-permute-done((bf16[2,128,512]{2,1,0:T(8,128)(2,1)S(1)}, bf16[2,128,512]{2,1,0:T(8,128)(2,1)S(1)}, u32[]{:S(2)}, u32[]{:S(2)}) %collective-permute-start.56) | collective-permute-done | bytes 262176 | tf_op jit(solution)/shard_map/ppermute | solution.py:63
  228.2 6.8 %collective-permute-done.58.refs_6_ = bf16[2,128,640]{2,1,0:T(8,128)(2,1)S(1)} collective-permute-done((bf16[2,128,640]{2,1,0:T(8,128)(2,1)S(1)}, bf16[2,128,640]{2,1,0:T(8,128)(2,1)S(1)}, u32[]{:S(2)}, u32[]{:S(2)}) %collective-permute-start.58) | collective-permute-done | bytes 327712 | tf_op jit(solution)/shard_map/ppermute | solution.py:63
  239.5 20.3 %collective-permute-done.61.refs_3_ = bf16[128,512]{1,0:T(8,128)(2,1)S(1)} collective-permute-done((bf16[128,512]{1,0:T(8,128)(2,1)S(1)}, bf16[128,512]{1,0:T(8,128)(2,1)S(1)}, u32[]{:S(2)}, u32[]{:S(2)}) %collective-permute-start.61) | collective-permute-done | bytes 131104 | tf_op jit(solution)/shard_map/ppermute | solution.py:63
  266.1 8.9 %collective-permute-done.64.other = bf16[2,32,3200]{2,1,0:T(8,128)(2,1)S(1)} collective-permute-done((bf16[2,32,3200]{2,1,0:T(8,128)(2,1)S(1)}, bf16[2,32,3200]{2,1,0:T(8,128)(2,1)S(1)}, u32[]{:S(2)}, u32[]{:S(2)}) %collective-permute-start.64) | collective-permute-done | bytes 409632 | tf_op jit(solution)/shard_map/ppermute | solution.py:63
  (218 shorter events, 86.3 us)
Async XLA Ops:
  18.5 15.7 %collective-permute-start.5 = (bf16[128,1024]{1,0:T(8,128)(2,1)S(1)}, bf16[128,1024]{1,0:T(8,128)(2,1)S(1)}, u32[]{:S(2)}, u32[]{:S(2)}) collective-permute-start(bf16[128,1024]{1,0:T(8,128)(2,1)S(1)} %bitcast.79), channel_id=1, source_target_pairs={{0,16},{4,20},{8,24},{12,28},{16,0},{20,4},{24,8},{28,12},{1,17},{... | collective-permute-start | bytes 786440 | tf_op jit(solution)/shard_map/ppermute | solution.py:63
  34.2 20.9 %collective-permute-start.10 = (bf16[256,1024]{1,0:T(8,128)(2,1)S(1)}, bf16[256,1024]{1,0:T(8,128)(2,1)S(1)}, u32[]{:S(2)}, u32[]{:S(2)}) collective-permute-start(bf16[256,1024]{1,0:T(8,128)(2,1)S(1)} %shard_map.309.m), channel_id=1, source_target_pairs={{0,8},{4,12},{8,0},{12,4},{16,24},{20,28},{24,16},{28,20},{1,9},{5... | collective-permute-start | bytes 1572872 | tf_op jit(solution)/shard_map/ppermute | solution.py:63
  35.2 17.8 %collective-permute-start.11 = (bf16[128,1024]{1,0:T(8,128)(2,1)S(1)}, bf16[128,1024]{1,0:T(8,128)(2,1)S(1)}, u32[]{:S(2)}, u32[]{:S(2)}) collective-permute-start(bf16[128,1024]{1,0:T(8,128)(2,1)S(1)} %bitcast.85), channel_id=1, source_target_pairs={{0,16},{4,20},{8,24},{12,28},{16,0},{20,4},{24,8},{28,12},{1,17},{... | collective-permute-start | bytes 786440 | tf_op jit(solution)/shard_map/ppermute | solution.py:63
  38.5 14.5 %collective-permute-start.14 = (bf16[256,128]{1,0:T(8,128)(2,1)S(1)}, bf16[256,128]{1,0:T(8,128)(2,1)S(1)}, u32[]{:S(2)}, u32[]{:S(2)}) collective-permute-start(bf16[256,128]{1,0:T(8,128)(2,1)S(1)} %shard_map.308.m), channel_id=1, source_target_pairs={{0,16},{4,20},{8,24},{12,28},{16,0},{20,4},{24,8},{28,12},{1,17},{... | collective-permute-start | bytes 196616 | tf_op jit(solution)/shard_map/ppermute | solution.py:63
  55.2 28.0 %collective-permute-start.15 = (bf16[512,1024]{1,0:T(8,128)(2,1)S(1)}, bf16[512,1024]{1,0:T(8,128)(2,1)S(1)}, u32[]{:S(2)}, u32[]{:S(2)}) collective-permute-start(bf16[512,1024]{1,0:T(8,128)(2,1)S(1)} %shard_map.312.refs_0_.near_ref), channel_id=1, source_target_pairs={{0,4},{4,0},{8,12},{12,8},{16,20},{20,16},{24,28},{28,24},{1,5},{5... | collective-permute-start | bytes 3145736 | tf_op jit(solution)/shard_map/ppermute | solution.py:63
  56.8 13.6 %collective-permute-start.16 = (bf16[128,1024]{1,0:T(8,128)(2,1)S(1)}, bf16[128,1024]{1,0:T(8,128)(2,1)S(1)}, u32[]{:S(2)}, u32[]{:S(2)}) collective-permute-start(bf16[128,1024]{1,0:T(8,128)(2,1)S(1)} %bitcast.83), channel_id=1, source_target_pairs={{0,16},{4,20},{8,24},{12,28},{16,0},{20,4},{24,8},{28,12},{1,17},{... | collective-permute-start | bytes 786440 | tf_op jit(solution)/shard_map/ppermute | solution.py:63
  70.4 12.7 %collective-permute-start.17 = (bf16[256,1024]{1,0:T(8,128)(2,1)S(1)}, bf16[256,1024]{1,0:T(8,128)(2,1)S(1)}, u32[]{:S(2)}, u32[]{:S(2)}) collective-permute-start(bf16[256,1024]{1,0:T(8,128)(2,1)S(1)} %shard_map.316.m), channel_id=1, source_target_pairs={{0,8},{4,12},{8,0},{12,4},{16,24},{20,28},{24,16},{28,20},{1,9},{5... | collective-permute-start | bytes 1572872 | tf_op jit(solution)/shard_map/ppermute | solution.py:63
  71.0 21.7 %collective-permute-start.21 = (bf16[256,1024]{1,0:T(8,128)(2,1)S(1)}, bf16[256,1024]{1,0:T(8,128)(2,1)S(1)}, u32[]{:S(2)}, u32[]{:S(2)}) collective-permute-start(bf16[256,1024]{1,0:T(8,128)(2,1)S(1)} %shard_map.311.m), channel_id=1, source_target_pairs={{0,4},{4,0},{8,12},{12,8},{16,20},{20,16},{24,28},{28,24},{1,5},{5... | collective-permute-start | bytes 1572872 | tf_op jit(solution)/shard_map/ppermute | solution.py:63
  71.3 11.9 %collective-permute-start.18 = (bf16[512,256]{1,0:T(8,128)(2,1)S(1)}, bf16[512,256]{1,0:T(8,128)(2,1)S(1)}, u32[]{:S(2)}, u32[]{:S(2)}) collective-permute-start(bf16[512,256]{1,0:T(8,128)(2,1)S(1)} %shard_map.317.rest_0_), channel_id=1, source_target_pairs={{0,1},{1,0},{2,3},{3,2},{4,5},{5,4},{6,7},{7,6},{8,9},{9,8},{10,11... | collective-permute-start | bytes 786440 | tf_op jit(solution)/shard_map/ppermute | solution.py:63
  83.3 11.2 %collective-permute-start.26 = (bf16[512,256]{1,0:T(8,128)(2,1)S(1)}, bf16[512,256]{1,0:T(8,128)(2,1)S(1)}, u32[]{:S(2)}, u32[]{:S(2)}) collective-permute-start(bf16[512,256]{1,0:T(8,128)(2,1)S(1)} %shard_map.319.rest_4_), channel_id=1, source_target_pairs={{0,2},{1,3},{2,0},{3,1},{4,6},{5,7},{6,4},{7,5},{8,10},{9,11},{10,... | collective-permute-start | bytes 786440 | tf_op jit(solution)/shard_map/ppermute | solution.py:63
  86.4 11.6 %collective-permute-start.23 = (bf16[2,176,256]{2,1,0:T(8,128)(2,1)S(1)}, bf16[2,176,256]{2,1,0:T(8,128)(2,1)S(1)}, u32[]{:S(2)}, u32[]{:S(2)}) collective-permute-start(bf16[2,176,256]{2,1,0:T(8,128)(2,1)S(1)} %get-tuple-element.480), channel_id=1, source_target_pairs={{0,2},{1,3},{2,0},{3,1},{4,6},{5,7},{6,4},{7,5},{8,10},{9,11},{10,... | collective-permute-start | bytes 540680 | tf_op jit(solution)/shard_map/ppermute | solution.py:63
  88.5 24.7 %collective-permute-start.29 = (bf16[512,1024]{1,0:T(8,128)(2,1)S(1)}, bf16[512,1024]{1,0:T(8,128)(2,1)S(1)}, u32[]{:S(2)}, u32[]{:S(2)}) collective-permute-start(bf16[512,1024]{1,0:T(8,128)(2,1)S(1)} %shard_map.318.up_near), channel_id=1, source_target_pairs={{0,4},{4,0},{8,12},{12,8},{16,20},{20,16},{24,28},{28,24},{1,5},{5... | collective-permute-start | bytes 3145736 | tf_op jit(solution)/shard_map/ppermute | solution.py:63
  92.7 21.5 %collective-permute-start.30 = (bf16[512,1024]{1,0:T(8,128)(2,1)S(1)}, bf16[512,1024]{1,0:T(8,128)(2,1)S(1)}, u32[]{:S(2)}, u32[]{:S(2)}) collective-permute-start(bf16[512,1024]{1,0:T(8,128)(2,1)S(1)} %shard_map.321.down_near), channel_id=1, source_target_pairs={{0,8},{4,12},{8,0},{12,4},{16,24},{20,28},{24,16},{28,20},{1,9},{5... | collective-permute-start | bytes 3145736 | tf_op jit(solution)/shard_map/ppermute | solution.py:63
  102.2 10.5 %collective-permute-start.32 = (bf16[176,1024]{1,0:T(8,128)(2,1)S(1)}, bf16[176,1024]{1,0:T(8,128)(2,1)S(1)}, u32[]{:S(2)}, u32[]{:S(2)}) collective-permute-start(bf16[176,1024]{1,0:T(8,128)(2,1)S(1)} %get-tuple-element.521.x0), channel_id=1, source_target_pairs={{0,2},{1,3},{2,0},{3,1},{4,6},{5,7},{6,4},{7,5},{8,10},{9,11},{10,... | collective-permute-start | bytes 1081352 | tf_op jit(solution)/shard_map/ppermute | solution.py:63
  121.8 10.6 %collective-permute-start.35 = (bf16[176,1024]{1,0:T(8,128)(2,1)S(1)}, bf16[176,1024]{1,0:T(8,128)(2,1)S(1)}, u32[]{:S(2)}, u32[]{:S(2)}) collective-permute-start(bf16[176,1024]{1,0:T(8,128)(2,1)S(1)} %shard_map.328), channel_id=1, source_target_pairs={{0,2},{1,3},{2,0},{3,1},{4,6},{5,7},{6,4},{7,5},{8,10},{9,11},{10,... | collective-permute-start | bytes 1081352 | tf_op jit(solution)/shard_map/ppermute | solution.py:63
  150.1 30.2 %collective-permute-start.47 = (bf16[2,2,128,1024]{3,2,1,0:T(8,128)(2,1)S(1)}, bf16[2,2,128,1024]{3,2,1,0:T(8,128)(2,1)S(1)}, u32[]{:S(2)}, u32[]{:S(2)}) collective-permute-start(bf16[2,2,128,1024]{3,2,1,0:T(8,128)(2,1)S(1)} %bitcast.97), channel_id=1, source_target_pairs={{0,8},{4,12},{8,0},{12,4},{16,24},{20,28},{24,16},{28,20},{1,9},{5... | collective-permute-start | bytes 3145736 | tf_op jit(solution)/shard_map/ppermute | solution.py:63
  155.1 25.2 %collective-permute-start.45 = (bf16[2,2,128,1024]{3,2,1,0:T(8,128)(2,1)S(1)}, bf16[2,2,128,1024]{3,2,1,0:T(8,128)(2,1)S(1)}, u32[]{:S(2)}, u32[]{:S(2)}) collective-permute-start(bf16[2,2,128,1024]{3,2,1,0:T(8,128)(2,1)S(1)} %bitcast.98), channel_id=1, source_target_pairs={{0,4},{4,0},{8,12},{12,8},{16,20},{20,16},{24,28},{28,24},{1,5},{5... | collective-permute-start | bytes 3145736 | tf_op jit(solution)/shard_map/ppermute | solution.py:63
  156.7 10.8 %collective-permute-start.41 = (bf16[176,1024]{1,0:T(8,128)(2,1)S(1)}, bf16[176,1024]{1,0:T(8,128)(2,1)S(1)}, u32[]{:S(2)}, u32[]{:S(2)}) collective-permute-start(bf16[176,1024]{1,0:T(8,128)(2,1)S(1)} %shard_map.332), channel_id=1, source_target_pairs={{0,2},{1,3},{2,0},{3,1},{4,6},{5,7},{6,4},{7,5},{8,10},{9,11},{10,... | collective-permute-start | bytes 1081352 | tf_op jit(solution)/shard_map/ppermute | solution.py:63
  179.1 13.4 %collective-permute-start.48 = (bf16[1024,256]{1,0:T(8,128)(2,1)S(1)}, bf16[1024,256]{1,0:T(8,128)(2,1)S(1)}, u32[]{:S(2)}, u32[]{:S(2)}) collective-permute-start(bf16[1024,256]{1,0:T(8,128)(2,1)S(1)} %get-tuple-element.627), channel_id=1, source_target_pairs={{0,1},{1,0},{2,3},{3,2},{4,5},{5,4},{6,7},{7,6},{8,9},{9,8},{10,11... | collective-permute-start | bytes 1572872 | tf_op jit(solution)/shard_map/ppermute | solution.py:63
  179.6 14.1 %collective-permute-start.49 = (bf16[1024,256]{1,0:T(8,128)(2,1)S(1)}, bf16[1024,256]{1,0:T(8,128)(2,1)S(1)}, u32[]{:S(2)}, u32[]{:S(2)}) collective-permute-start(bf16[1024,256]{1,0:T(8,128)(2,1)S(1)} %shard_map.337), channel_id=1, source_target_pairs={{0,2},{1,3},{2,0},{3,1},{4,6},{5,7},{6,4},{7,5},{8,10},{9,11},{10,... | collective-permute-start | bytes 1572872 | tf_op jit(solution)/shard_map/ppermute | solution.py:63
  187.0 14.9 %collective-permute-start.52 = (bf16[2,128,1024]{2,1,0:T(8,128)(2,1)S(1)}, bf16[2,128,1024]{2,1,0:T(8,128)(2,1)S(1)}, u32[]{:S(2)}, u32[]{:S(2)}) collective-permute-start(bf16[2,128,1024]{2,1,0:T(8,128)(2,1)S(1)} %shard_map.338), channel_id=1, source_target_pairs={{0,8},{4,12},{8,0},{12,4},{16,24},{20,28},{24,16},{28,20},{1,9},{5... | collective-permute-start | bytes 1572872 | tf_op jit(solution)/shard_map/ppermute | solution.py:63
  188.2 14.9 %collective-permute-start.55 = (bf16[2,2,128,512]{3,2,1,0:T(8,128)(2,1)S(1)}, bf16[2,2,128,512]{3,2,1,0:T(8,128)(2,1)S(1)}, u32[]{:S(2)}, u32[]{:S(2)}) collective-permute-start(bf16[2,2,128,512]{3,2,1,0:T(8,128)(2,1)S(1)} %bitcast.99), channel_id=1, source_target_pairs={{0,4},{4,0},{8,12},{12,8},{16,20},{20,16},{24,28},{28,24},{1,5},{5... | collective-permute-start | bytes 1572872 | tf_op jit(solution)/shard_map/ppermute | solution.py:63
  193.7 32.4 %collective-permute-start.54 = (bf16[2,2,128,640]{3,2,1,0:T(8,128)(2,1)S(1)}, bf16[2,2,128,640]{3,2,1,0:T(8,128)(2,1)S(1)}, u32[]{:S(2)}, u32[]{:S(2)}) collective-permute-start(bf16[2,2,128,640]{3,2,1,0:T(8,128)(2,1)S(1)} %shard_map.341), channel_id=1, source_target_pairs={{0,8},{4,12},{8,0},{12,4},{16,24},{20,28},{24,16},{28,20},{1,9},{5... | collective-permute-start | bytes 1966088 | tf_op jit(solution)/shard_map/ppermute | solution.py:63
  201.9 17.7 %collective-permute-start.57 = (bf16[128,1024]{1,0:T(8,128)(2,1)S(1)}, bf16[128,1024]{1,0:T(8,128)(2,1)S(1)}, u32[]{:S(2)}, u32[]{:S(2)}) collective-permute-start(bf16[128,1024]{1,0:T(8,128)(2,1)S(1)} %shard_map.343), channel_id=1, source_target_pairs={{0,16},{4,20},{8,24},{12,28},{16,0},{20,4},{24,8},{28,12},{1,17},{... | collective-permute-start | bytes 786440 | tf_op jit(solution)/shard_map/ppermute | solution.py:63
  203.2 22.9 %collective-permute-start.56 = (bf16[2,128,512]{2,1,0:T(8,128)(2,1)S(1)}, bf16[2,128,512]{2,1,0:T(8,128)(2,1)S(1)}, u32[]{:S(2)}, u32[]{:S(2)}) collective-permute-start(bf16[2,128,512]{2,1,0:T(8,128)(2,1)S(1)} %shard_map.345), channel_id=1, source_target_pairs={{0,8},{4,12},{8,0},{12,4},{16,24},{20,28},{24,16},{28,20},{1,9},{5... | collective-permute-start | bytes 786440 | tf_op jit(solution)/shard_map/ppermute | solution.py:63
  204.0 24.2 %collective-permute-start.59 = (bf16[2,128,1024]{2,1,0:T(8,128)(2,1)S(1)}, bf16[2,128,1024]{2,1,0:T(8,128)(2,1)S(1)}, u32[]{:S(2)}, u32[]{:S(2)}) collective-permute-start(bf16[2,128,1024]{2,1,0:T(8,128)(2,1)S(1)} %shard_map.346), channel_id=1, source_target_pairs={{0,4},{4,0},{8,12},{12,8},{16,20},{20,16},{24,28},{28,24},{1,5},{5... | collective-permute-start | bytes 1572872 | tf_op jit(solution)/shard_map/ppermute | solution.py:63
  226.9 12.4 %collective-permute-start.50 = (bf16[176,1024]{1,0:T(8,128)(2,1)S(1)}, bf16[176,1024]{1,0:T(8,128)(2,1)S(1)}, u32[]{:S(2)}, u32[]{:S(2)}) collective-permute-start(bf16[176,1024]{1,0:T(8,128)(2,1)S(1)} %get-tuple-element.676), channel_id=1, source_target_pairs={{0,1},{1,0},{2,3},{3,2},{4,5},{5,4},{6,7},{7,6},{8,9},{9,8},{10,11... | collective-permute-start | bytes 1081352 | tf_op jit(solution)/shard_map/ppermute | solution.py:63
  226.9 12.4 %collective-permute-start.53 = (bf16[176,1024]{1,0:T(8,128)(2,1)S(1)}, bf16[176,1024]{1,0:T(8,128)(2,1)S(1)}, u32[]{:S(2)}, u32[]{:S(2)}) collective-permute-start(bf16[176,1024]{1,0:T(8,128)(2,1)S(1)} %shard_map.344), channel_id=1, source_target_pairs={{0,2},{1,3},{2,0},{3,1},{4,6},{5,7},{6,4},{7,5},{8,10},{9,11},{10,... | collective-permute-start | bytes 1081352 | tf_op jit(solution)/shard_map/ppermute | solution.py:63
  235.1 24.7 %collective-permute-start.60 = (bf16[128,1024]{1,0:T(8,128)(2,1)S(1)}, bf16[128,1024]{1,0:T(8,128)(2,1)S(1)}, u32[]{:S(2)}, u32[]{:S(2)}) collective-permute-start(bf16[128,1024]{1,0:T(8,128)(2,1)S(1)} %shard_map.349), channel_id=1, source_target_pairs={{0,16},{4,20},{8,24},{12,28},{16,0},{20,4},{24,8},{28,12},{1,17},{... | collective-permute-start | bytes 786440 | tf_op jit(solution)/shard_map/ppermute | solution.py:63
  236.3 23.5 %collective-permute-start.62 = (bf16[128,640]{1,0:T(8,128)(2,1)S(1)}, bf16[128,640]{1,0:T(8,128)(2,1)S(1)}, u32[]{:S(2)}, u32[]{:S(2)}) collective-permute-start(bf16[128,640]{1,0:T(8,128)(2,1)S(1)} %shard_map.350), channel_id=1, source_target_pairs={{0,16},{4,20},{8,24},{12,28},{16,0},{20,4},{24,8},{28,12},{1,17},{... | collective-permute-start | bytes 491528 | tf_op jit(solution)/shard_map/ppermute | solution.py:63
  238.2 21.6 %collective-permute-start.61 = (bf16[128,512]{1,0:T(8,128)(2,1)S(1)}, bf16[128,512]{1,0:T(8,128)(2,1)S(1)}, u32[]{:S(2)}, u32[]{:S(2)}) collective-permute-start(bf16[128,512]{1,0:T(8,128)(2,1)S(1)} %shard_map.348), channel_id=1, source_target_pairs={{0,16},{4,20},{8,24},{12,28},{16,0},{20,4},{24,8},{28,12},{1,17},{... | collective-permute-start | bytes 393224 | tf_op jit(solution)/shard_map/ppermute | solution.py:63
  263.3 11.6 %collective-permute-start.64 = (bf16[2,32,3200]{2,1,0:T(8,128)(2,1)S(1)}, bf16[2,32,3200]{2,1,0:T(8,128)(2,1)S(1)}, u32[]{:S(2)}, u32[]{:S(2)}) collective-permute-start(bf16[2,32,3200]{2,1,0:T(8,128)(2,1)S(1)} %get-tuple-element.742), channel_id=1, source_target_pairs={{0,2},{1,3},{2,0},{3,1},{4,6},{5,7},{6,4},{7,5},{8,10},{9,11},{10,... | collective-permute-start | bytes 1228808 | tf_op jit(solution)/shard_map/ppermute | solution.py:63
  (50 other events, 365.0 us)
where the time goes:
time: 281 us; the launch traced here: 277 us
  waiting for transfers between devices  158 us (56%)
  starting transfers between devices  52.7 us (19%)
  Pallas kernels  51.8 us (18%)
  matrix products  6.02 us (2%)
  local copies, waits for them, and re-layouts  5.66 us (2%)
    ppermute x65, waiting for transfers between devices, swap(): lax.ppermute(x, axis, [(i, i ^ b) for i in range(lax.axis_size(axis))])  158 us
    ppermute x65, starting transfers between devices, swap(): lax.ppermute(x, axis, [(i, i ^ b) for i in range(lax.axis_size(axis))])  52.7 us
    pallas_call x60, Pallas kernels, call(): pl.pallas_call(kernel, in_specs=[pl.BlockSpec(memory_space=m) for m in sp...  47.8 us
    dot_general x7, matrix products, dot_tn(): lax.dot_general(a, b, (((0,), (0,)), ((), ())), preferred_element_type=f32)  6.02 us
  transfers between devices with their start and end apart: 65, of which 30 were waited for; matrix products, arithmetic and copies ran while one was open for 3% of the time, Pallas kernels for 15%

commit v1 on v0

--- a/solution.py
+++ b/solution.py
@@ -26,7 +26,7 @@
     return jax.ShapeDtypeStruct(tuple(shape), kind)
 
 
-def call(kernel, ins, outs, scratch=(), scalars=0, alias=None, vmem=16):
+def call(kernel, ins, outs, scratch=(), scalars=0, alias=None, vmem=16, cost=0):
     spaces = [pltpu.SMEM] * scalars + [pltpu.VMEM] * (len(ins) - scalars)
     return pl.pallas_call(
         kernel,
@@ -35,7 +35,9 @@
         out_shape=list(outs),
         scratch_shapes=list(scratch),
         input_output_aliases=alias or {},
-        cost_estimate=pl.CostEstimate(flops=0, bytes_accessed=0, transcendentals=0),
+        cost_estimate=pl.CostEstimate(
+            flops=int(cost * 1e9), bytes_accessed=0, transcendentals=0
+        ),
         compiler_params=pltpu.CompilerParams(vmem_limit_bytes=vmem * 2**20),
     )(*ins)
 
@@ -485,6 +487,15 @@
             for half in range(2):
                 block = part[doc_at(n), half * BLOCK : (half + 1) * BLOCK]
                 out[:, far_block(place, q + half, order)] = block.astype(out.dtype)
+
+
+def half_grad_kernel(near, start, left_ref, right_ref, out_ref):
+    left = left_ref[...]
+    if near is not None:
+        left = left_ref[:, : D // 2] if near else left_ref[:, D // 2 :]
+    for n in range(out_ref.shape[1] // TILE):
+        at = slice(start + n * TILE, start + (n + 1) * TILE)
+        out_ref[:, n * TILE : (n + 1) * TILE] = dot_tn(left, right_ref[:, at]).astype(bf16)
 
 
 def normal_parts(u):
@@ -923,19 +934,20 @@
     )
     meet.far_pair(keep, give)
 
-    def half_grad(left, right, near):
-        left = left[:, : D // 2] if near else left[:, D // 2 :]
-        return dot_tn(left, right).astype(bf16)
-
-    give = run(partial(half_grad, near=False), d_ffn_group, act_low)
-    s_down = Scatter(run, (give,), "dp", X_Z, given=give)
-    s_down.send()
+    def half_grad(left, right, near, start=0, columns=None):
+        out = shape_of((D if near is None else D // 2, columns or right.shape[1]), bf16)
+        (made,) = run(
+            lambda *ins: call(partial(half_grad_kernel, near, start), ins, [out]), left, right
+        )
+        return made
+
     meet.send()
-    keep = run(partial(half_grad, near=True), d_ffn_group, act_low)
-    s_down.own(keep)
-    keep = run(partial(half_grad, near=True), normed_group, d_pre)
-    give = run(partial(half_grad, near=False), normed_group, d_pre)
-    s_up = Scatter(run, (keep,), "dp", Z_X, given=give).send()
+    give = half_grad(d_ffn_group, act_low, False)
+    s_down = Scatter(run, (give,), "dp", X_Z, given=give).send()
+    give = half_grad(normed_group, d_pre, False)
+    s_up = Scatter(run, (give,), "dp", Z_X, given=give).send()
+    s_down.own(half_grad(d_ffn_group, act_low, True))
+    s_up.own(half_grad(normed_group, d_pre, True))
 
     d_branch, d_resid_one, sums_one, a0, a1, a2 = run(
         lambda *ins: call(
@@ -948,7 +960,9 @@
     far = swap(a2, by_y)
     got_c = swap(a1, by_c)
     parts = run(
-        lambda *ins: call(partial(proj_grad_kernel, width), ins, [col_out] * 4, scalars=1),
+        lambda *ins: call(
+            partial(proj_grad_kernel, width), ins, [col_out] * 4, scalars=1, cost=1.3
+        ),
         at, attended, d_branch,
     )
     meet_proj = Meet().near_pair(parts[0], parts[1]).far_pair(parts[2], parts[3])
@@ -956,14 +970,12 @@
     d_qkv, d_sums, d_grid = run(
         lambda *ins: call(
             partial(attend_back_kernel, heads, (0, 1), False), ins,
-            [qkv_out, shape_of((tp, 3 * width), f32), grids],
+            [qkv_out, shape_of((tp, 3 * width), f32), grids], cost=10,
         ),
         qkv, probs, a0, got_c, notes,
     )
     got_far = swap(second(far), by_c)
     meet_proj.send()
-    run.wait(s_up.other, s_down.other)
-    s_up.take().send()
     d_qkv, d_sums, d_grid, d_ext = run(
         lambda *ins: call(
             partial(attend_back_kernel, heads, (2, 3), True), ins,
@@ -973,18 +985,17 @@
         qkv, probs, far, got_far, notes, d_qkv, d_sums, d_grid,
     )
 
-    def columns_grad(group, d_qkv, near):
-        left = group[:, : D // 2] if near else group[:, D // 2 :]
-        return dot_tn(left, d_qkv[:, : D // 2]).astype(bf16)
-
     def with_proj(q, k, c, y, small):
         p = (k.astype(f32) + c.astype(f32) + y.astype(f32)).astype(bf16)
         return jnp.concatenate([q, p, small], axis=-1).astype(f32)
 
-    keep = run(partial(columns_grad, near=True), group, d_qkv)
-    grad_b = run(lambda g, d: dot_tn(g, d[:, D // 2 :]).astype(bf16), group, d_qkv)
-    give = run(partial(columns_grad, near=False), group, d_qkv)
-    s_first = Scatter(run, (keep,), "dp", Z_X, given=give).send()
+    give = half_grad(group, d_qkv, False, 0, D // 2)
+    s_first = Scatter(run, (give,), "dp", Z_X, given=give).send()
+    across = s_first.other
+    run.wait(s_up.other, s_down.other)
+    s_up.take().send()
+    s_first.own(half_grad(group, d_qkv, True, 0, D // 2))
+    grad_b = half_grad(group, d_qkv, None, D // 2, 3 * width - D // 2)
     plains = [pltpu.VMEM((24, D), f32)] * 2
     (small_grads,) = run(
         lambda *ins: call(
@@ -993,26 +1004,24 @@
         ),
         at, d_ext, d_sums, d_up_bias, sums_one, sums_two,
     )
+    parts = run(
+        lambda *ins: call(
+            partial(tokens_back_kernel, width), ins, [wide_f, wide_b, wide_f, wide_b], scalars=1
+        ),
+        at, d_qkv, g_first.x, g_first.other,
+    )
+    meet_tok = Meet().near_pair(parts[0], parts[1]).far_pair(parts[2], parts[3])
     s_second = Scatter(
         run, (grad_b, *meet_proj.terms(), small_grads), "dp", Z_X, walk=(1, 2, 0), base=with_proj
     ).send()
-    parts = run(
-        lambda *ins: call(
-            partial(tokens_back_kernel, width), ins, [wide_f, wide_b, wide_f, wide_b], scalars=1
-        ),
-        at, d_qkv, g_first.x, g_first.other,
-    )
-    meet_tok = Meet().near_pair(parts[0], parts[1]).far_pair(parts[2], parts[3])
     s_up.take().send()
+    s_first.take().send()
+    s_down.take().send(across)
     meet_tok.send()
-    s_first.take().send()
+    run.wait(s_down.other, s_second.other, s_first.other, s_up.other)
     s_down.take().send()
-    run.wait(s_second.other, s_first.other, s_up.other)
     s_second.take().send()
     s_first.take().send()
-    run.wait(s_down.other, s_second.other)
-    s_down.take().send()
-    s_second.take().send()
 
     def columns_back(scatters):
         sums = [x.sum().reshape(tp, rows, -1) for x in scatters]
@@ -1040,14 +1049,24 @@
                             place = pl.multiple_of((i * tp + f) * w, w)
                             out[:, pl.ds(place, w)] = ref[n, :, start : start + w].astype(f32)
                             start += w
-                    part = ref[n, :, start:].astype(f32)
-                    total = part if total is None else total + part
-            small_outs(total, ends)
+                    if ends:
+                        part = ref[n, :, start:].astype(f32)
+                        total = part if total is None else total + part
+            if ends:
+                small_outs(total, ends)
 
         return run(
             lambda *ins: call(fn, ins, outs + ends, scalars=1), at, exchanged.mine, exchanged.other
         )
 
+    s_up.take()
+    x_up = columns_back([s_up]).turn()
+    s_second.take().send()
+    run.wait(x_up.other, s_down.other, s_first.other, s_second.other)
+    s_down.take()
+    s_first.take()
+    s_second.take()
+    x_rest = columns_back([s_down, s_first, s_second])
     out_f = shape_of((1, SLOTS, D), f32)
     grad_tokens = run(
         lambda *ins: glue(
@@ -1058,15 +1077,10 @@
         ),
         d_resid_one, *meet_tok.terms(),
     )
-    run.wait(s_down.other, s_first.other, s_second.other)
-    s_down.take()
-    s_up.take()
-    s_first.take()
-    s_second.take()
-    back = columns_back([s_up, s_down, s_first, s_second]).turn()
-
-    grad_up, grad_down, grad_qkv, grad_proj, *out = whole_rows(
-        back, (1, 1, 3, 1), (hidden, hidden, width, width), (1,) * 6 + (2, 6, 4)
+    x_rest.turn()
+    (grad_up,) = whole_rows(x_up, (1,), (hidden,), ())
+    grad_down, grad_qkv, grad_proj, *out = whole_rows(
+        x_rest, (1, 3, 1), (hidden, width, width), (1,) * 6 + (2, 6, 4)
     )
     out = [x.reshape(-1) for x in out]
     return (

time: 281 us -> 269 us (0.957)
  waiting for transfers between devices: 158 us -> 140 us
  Pallas kernels: 51.8 us -> 60.3 us
  matrix products: 6.02 us -> 0 us
  starting transfers between devices: 52.7 us -> 57.3 us
    ppermute x65 -> x67, waiting for transfers between devices: 158 us -> 140 us  [swap(): lax.ppermute(x, axis, [(i, i ^ b) for i in range(lax.axis_size(axis))])]
    pallas_call x60 -> x70, Pallas kernels: 47.8 us -> 56.2 us  [call(): pl.pallas_call(kernel, in_specs=[pl.BlockSpec(memory_space=m) for m in sp...]
    dot_general x7 -> x0, matrix products: 6.02 us -> none  [dot_tn(): lax.dot_general(a, b, (((0,), (0,)), ((), ())), preferred_element_type=f32)]
    ppermute x65 -> x67, starting transfers between devices: 52.7 us -> 57.3 us  [swap(): lax.ppermute(x, axis, [(i, i ^ b) for i in range(lax.axis_size(axis))])]
  transfers between devices with their start and end apart: 65 -> 67, of which waited for: 30 -> 31; matrix products, arithmetic and copies ran while one was open for 3% -> 1% of each run, Pallas kernels for 15% -> 19%
where the time goes in v1:
time: 269 us; the launch traced here: 266 us
  waiting for transfers between devices  140 us (52%)
  Pallas kernels  60.3 us (22%)
  starting transfers between devices  57.3 us (21%)
  local copies, waits for them, and re-layouts  5.66 us (2%)
    ppermute x67, waiting for transfers between devices, swap(): lax.ppermute(x, axis, [(i, i ^ b) for i in range(lax.axis_size(axis))])  140 us
    ppermute x67, starting transfers between devices, swap(): lax.ppermute(x, axis, [(i, i ^ b) for i in range(lax.axis_size(axis))])  57.3 us
    pallas_call x70, Pallas kernels, call(): pl.pallas_call(kernel, in_specs=[pl.BlockSpec(memory_space=m) for m in sp...  56.2 us
  transfers between devices with their start and end apart: 67, of which 31 were waited for; matrix products, arithmetic and copies ran while one was open for 1% of the time, Pallas kernels for 19%

profile of v1, /device:TPU:0, one launch (start us, length us, event | category | flops | bytes accessed | tf_op | source)
XLA Modules:
  0.0 266.2 jit_solution(15844185894447344889)
XLA Ops:
  7.6 3.0 %collective-permute-start.3 = (bf16[2,32,1024]{2,1,0:T(8,128)(2,1)S(1)}, bf16[2,32,1024]{2,1,0:T(8,128)(2,1)S(1)}, u32[]{:S(2)}, u32[]{:S(2)}) collective-permute-start(bf16[2,32,1024]{2,1,0:T(8,128)(2,1)S(1)} %get-tuple-element.411), channel_id=1, source_target_pairs={{0,2},{1,3},{2,0},{3,1},{4,6},{5,7},{6,4},{7,5},{8,10},{9,11},{10,... | collective-permute-start | bytes 393224 | tf_op jit(solution)/shard_map/ppermute | solution.py:65
  11.9 2.4 collective-permute-done.3.other
  18.5 2.7 collective-permute-start.5
  21.7 3.1 %collective-permute-done.6.o = bf16[32,128]{1,0:T(8,128)(2,1)S(1)} collective-permute-done((bf16[32,128]{1,0:T(8,128)(2,1)S(1)}, bf16[32,128]{1,0:T(8,128)(2,1)S(1)}, u32[]{:S(2)}, u32[]{:S(2)}) %collective-permute-start.6) | collective-permute-done | bytes 8224 | tf_op jit(solution)/shard_map/ppermute | solution.py:65
  30.6 3.5 %collective-permute-done.9.o = bf16[128,128]{1,0:T(8,128)(2,1)S(1)} collective-permute-done((bf16[128,128]{1,0:T(8,128)(2,1)S(1)}, bf16[128,128]{1,0:T(8,128)(2,1)S(1)}, u32[]{:S(2)}, u32[]{:S(2)}) %collective-permute-start.9) | collective-permute-done | bytes 32800 | tf_op jit(solution)/shard_map/ppermute | solution.py:65
  35.2 3.3 %collective-permute-start.11 = (bf16[128,1024]{1,0:T(8,128)(2,1)S(1)}, bf16[128,1024]{1,0:T(8,128)(2,1)S(1)}, u32[]{:S(2)}, u32[]{:S(2)}) collective-permute-start(bf16[128,1024]{1,0:T(8,128)(2,1)S(1)} %bitcast.83), channel_id=1, source_target_pairs={{0,16},{4,20},{8,24},{12,28},{16,0},{20,4},{24,8},{28,12},{1,17},{... | collective-permute-start | bytes 786440 | tf_op jit(solution)/shard_map/ppermute | solution.py:65
  38.5 14.4 %collective-permute-done.14.o = bf16[256,128]{1,0:T(8,128)(2,1)S(1)} collective-permute-done((bf16[256,128]{1,0:T(8,128)(2,1)S(1)}, bf16[256,128]{1,0:T(8,128)(2,1)S(1)}, u32[]{:S(2)}, u32[]{:S(2)}) %collective-permute-start.14) | collective-permute-done | bytes 65568 | tf_op jit(solution)/shard_map/ppermute | solution.py:65
  58.9 4.1 %shard_map.315.bias_ref = f32[4,4,176,176]{3,2,1,0:T(8,128)S(1)} custom-call(bf16[4,16,256]{2,1,0:T(8,128)(2,1)S(1)} %shard_map.310.notes_ref, f32[12,256]{1,0:T(8,128)S(1)} %get-tuple-element.473.ext_ref), custom_call_target="tpu_custom_call" | custom-call | tf_op jit(solution)/shard_map/pallas_call | solution.py:243
  62.9 7.5 %collective-permute-done.16.o = bf16[128,1024]{1,0:T(8,128)(2,1)S(1)} collective-permute-done((bf16[128,1024]{1,0:T(8,128)(2,1)S(1)}, bf16[128,1024]{1,0:T(8,128)(2,1)S(1)}, u32[]{:S(2)}, u32[]{:S(2)}) %collective-permute-start.16) | collective-permute-done | bytes 262176 | tf_op jit(solution)/shard_map/ppermute | solution.py:65
  71.3 6.4 %collective-permute-done.19.rest_2_ = bf16[512,256]{1,0:T(8,128)(2,1)S(1)} collective-permute-done((bf16[512,256]{1,0:T(8,128)(2,1)S(1)}, bf16[512,256]{1,0:T(8,128)(2,1)S(1)}, u32[]{:S(2)}, u32[]{:S(2)}) %collective-permute-start.19) | collective-permute-done | bytes 262176 | tf_op jit(solution)/shard_map/ppermute | solution.py:65
  77.8 5.4 %collective-permute-done.17.o = bf16[256,1024]{1,0:T(8,128)(2,1)S(1)} collective-permute-done((bf16[256,1024]{1,0:T(8,128)(2,1)S(1)}, bf16[256,1024]{1,0:T(8,128)(2,1)S(1)}, u32[]{:S(2)}, u32[]{:S(2)}) %collective-permute-start.17) | collective-permute-done | bytes 524320 | tf_op jit(solution)/shard_map/ppermute | solution.py:65
  83.4 3.1 %shard_map.320 = (bf16[704,1024]{1,0:T(8,128)(2,1)S(1)}, bf16[704,768]{1,0:T(8,128)(2,1)S(1)}, f32[4,4,176,176]{3,2,1,0:T(8,128)S(1)}, bf16[2,176,256]{2,1,0:T(8,128)(2,1)S(1)}) custom-call(s32[2]{0:T(128)S(1)} %pad_add_fusion.at.at_ref, bf16[176,1024]{1,0:T(8,128)(2,1)S(1)} %collective-permute-done.12.refs_2_.d0, ...), custom_call_target="tpu_custom_call" | custom-call | tf_op jit(solution)/shard_map/pallas_call | solution.py:31
  89.1 3.6 %collective-permute-done.21.o = bf16[256,1024]{1,0:T(8,128)(2,1)S(1)} collective-permute-done((bf16[256,1024]{1,0:T(8,128)(2,1)S(1)}, bf16[256,1024]{1,0:T(8,128)(2,1)S(1)}, u32[]{:S(2)}, u32[]{:S(2)}) %collective-permute-start.21) | collective-permute-done | bytes 524320 | tf_op jit(solution)/shard_map/ppermute | solution.py:65
  95.0 3.1 %shard_map.322 = (bf16[704,1024]{1,0:T(8,128)(2,1)S(1)}, bf16[704,768]{1,0:T(8,128)(2,1)S(1)}, f32[4,4,176,176]{3,2,1,0:T(8,128)S(1)}, bf16[2,176,256]{2,1,0:T(8,128)(2,1)S(1)}) custom-call(s32[2]{0:T(128)S(1)} %pad_add_fusion.at.at_ref, ...), custom_call_target="tpu_custom_call", output_to_operand_aliasing={{0}: (7, {}), {1}: (8, {}), {2}: (9, {})} | custom-call | tf_op jit(solution)/shard_map/pallas_call | solution.py:31
  103.4 9.3 %collective-permute-done.32.x0 = bf16[176,1024]{1,0:T(8,128)(2,1)S(1)} collective-permute-done((bf16[176,1024]{1,0:T(8,128)(2,1)S(1)}, bf16[176,1024]{1,0:T(8,128)(2,1)S(1)}, u32[]{:S(2)}, u32[]{:S(2)}) %collective-permute-start.32) | collective-permute-done | bytes 360480 | tf_op jit(solution)/shard_map/ppermute | solution.py:65
  114.2 2.8 %shard_map.326 = (bf16[704,1024]{1,0:T(8,128)(2,1)S(1)}, f32[704,1024]{1,0:T(8,128)S(1)}, bf16[704,1024]{1,0:T(8,128)(2,1)S(1)}, f32[176,1024]{1,0:T(8,128)S(1)}, bf16[176,1024]{1,0:T(8,128)(2,1)S(1)}) custom-call(s32[2]{0:T(128)S(1)} %pad_add_fusion.at.at_ref, bf16[176,1024]{1,0:T(8,128)(2,1)S(1)} %get-tuple-element.532.x0, ...), custom_call_target="tpu_custom_call" | custom-call | tf_op jit(solution)/shard_map/pallas_call | solution.py:31
  117.1 2.9 %shard_map.327 = (bf16[704,1024]{1,0:T(8,128)(2,1)S(1)}, f32[704,1024]{1,0:T(8,128)S(1)}, bf16[704,1024]{1,0:T(8,128)(2,1)S(1)}, f32[176,1024]{1,0:T(8,128)S(1)}, bf16[176,1024]{1,0:T(8,128)(2,1)S(1)}) custom-call(s32[2]{0:T(128)S(1)} %pad_add_fusion.at.at_ref, ...), custom_call_target="tpu_custom_call", output_to_operand_aliasing={{0}: (8, {}), {1}: (9, {}), {2}: (10, {})} | custom-call | tf_op jit(solution)/shard_map/pallas_call | solution.py:31
  123.6 8.7 %collective-permute-done.35.got_y = bf16[176,1024]{1,0:T(8,128)(2,1)S(1)} collective-permute-done((bf16[176,1024]{1,0:T(8,128)(2,1)S(1)}, bf16[176,1024]{1,0:T(8,128)(2,1)S(1)}, u32[]{:S(2)}, u32[]{:S(2)}) %collective-permute-start.35) | collective-permute-done | bytes 360480 | tf_op jit(solution)/shard_map/ppermute | solution.py:65
  135.5 7.9 %collective-permute-done.38.g0 = bf16[176,1024]{1,0:T(8,128)(2,1)S(1)} collective-permute-done((bf16[176,1024]{1,0:T(8,128)(2,1)S(1)}, bf16[176,1024]{1,0:T(8,128)(2,1)S(1)}, u32[]{:S(2)}, u32[]{:S(2)}) %collective-permute-start.38) | collective-permute-done | bytes 360480 | tf_op jit(solution)/shard_map/ppermute | solution.py:65
  143.4 2.6 shard_map.330
  146.0 2.4 shard_map.331
  166.9 4.9 %shard_map.339 = (bf16[704,768]{1,0:T(8,128)(2,1)S(1)}, f32[4,768]{1,0:T(4,128)S(1)}, f32[12,128,128]{2,1,0:T(8,128)S(1)}) custom-call(bf16[704,768]{1,0:T(8,128)(2,1)S(1)} %get-tuple-element.652.qkv_ref, f32[4,4,176,176]{3,2,1,0:T(8,128)S(1)} %get-tuple-element.653.probs_ref, bf16[176,256]{1,0:T(8,128)(2,1)S(1)} %get-tuple-element.643.g0, ...), custom_call_target="tpu_custom_call" | custom-call | flops 10000000000 | tf_op jit(solution)/shard_map/pallas_call | solution.py:31
  173.7 5.3 %shard_map.342 = (bf16[704,768]{1,0:T(8,128)(2,1)S(1)}, f32[4,768]{1,0:T(4,128)S(1)}, f32[12,128,128]{2,1,0:T(8,128)S(1)}, f32[12,256]{1,0:T(8,128)S(1)}) custom-call(bf16[704,768]{1,0:T(8,128)(2,1)S(1)} %get-tuple-element.652.qkv_ref, ...), custom_call_target="tpu_custom_call", output_to_operand_aliasing={{0}: (5, {}), {1}: (6, {}), {2}: (7, {})} | custom-call | tf_op jit(solution)/shard_map/pallas_call | solution.py:31
  185.5 2.7 %shard_map.347 = bf16[1024,128]{1,0:T(8,128)(2,1)S(1)} custom-call(s32[2]{0:T(128)S(1)} %pad_add_fusion.at.at_ref, f32[12,256]{1,0:T(8,128)S(1)} %get-tuple-element.672.ext_ref, f32[4,768]{1,0:T(4,128)S(1)} %get-tuple-element.673.sums_ref, f32[2,1024]{1,0:T(2,128)S(1)} %get-tuple-element.674.up_ref, f32[3,1024]{1,0:T(4,128)S(1)} %get-tuple-element.675.one_ref, ...), custom_call_target="tpu_custom_call" | custom-call | tf_op jit(solution)/shard_map/pallas_call | solution.py:31
  190.7 6.1 %collective-permute-done.51.refs_2_ = bf16[2,128,1024]{2,1,0:T(8,128)(2,1)S(1)} collective-permute-done((bf16[2,128,1024]{2,1,0:T(8,128)(2,1)S(1)}, bf16[2,128,1024]{2,1,0:T(8,128)(2,1)S(1)}, u32[]{:S(2)}, u32[]{:S(2)}) %collective-permute-start.51) | collective-permute-done | bytes 524320 | tf_op jit(solution)/shard_map/ppermute | solution.py:65
  200.6 19.4 %collective-permute-done.57.refs_2_ = bf16[2,128,512]{2,1,0:T(8,128)(2,1)S(1)} collective-permute-done((bf16[2,128,512]{2,1,0:T(8,128)(2,1)S(1)}, bf16[2,128,512]{2,1,0:T(8,128)(2,1)S(1)}, u32[]{:S(2)}, u32[]{:S(2)}) %collective-permute-start.57) | collective-permute-done | bytes 262176 | tf_op jit(solution)/shard_map/ppermute | solution.py:65
  221.9 2.7 %collective-permute-start.59 = (bf16[128,1024]{1,0:T(8,128)(2,1)S(1)}, bf16[128,1024]{1,0:T(8,128)(2,1)S(1)}, u32[]{:S(2)}, u32[]{:S(2)}) collective-permute-start(bf16[128,1024]{1,0:T(8,128)(2,1)S(1)} %shard_map.354), channel_id=1, source_target_pairs={{0,16},{4,20},{8,24},{12,28},{16,0},{20,4},{24,8},{28,12},{1,17},{... | collective-permute-start | bytes 786440 | tf_op jit(solution)/shard_map/ppermute | solution.py:65
  225.5 2.4 collective-permute-done.60.refs_6_
  228.0 2.7 %collective-permute-start.64 = (bf16[128,640]{1,0:T(8,128)(2,1)S(1)}, bf16[128,640]{1,0:T(8,128)(2,1)S(1)}, u32[]{:S(2)}, u32[]{:S(2)}) collective-permute-start(bf16[128,640]{1,0:T(8,128)(2,1)S(1)} %shard_map.360), channel_id=1, source_target_pairs={{0,16},{4,20},{8,24},{12,28},{16,0},{20,4},{24,8},{28,12},{1,17},{... | collective-permute-start | bytes 491528 | tf_op jit(solution)/shard_map/ppermute | solution.py:65
  232.6 14.1 %collective-permute-done.63.refs_3_ = bf16[128,512]{1,0:T(8,128)(2,1)S(1)} collective-permute-done((bf16[128,512]{1,0:T(8,128)(2,1)S(1)}, bf16[128,512]{1,0:T(8,128)(2,1)S(1)}, u32[]{:S(2)}, u32[]{:S(2)}) %collective-permute-start.63) | collective-permute-done | bytes 131104 | tf_op jit(solution)/shard_map/ppermute | solution.py:65
  250.8 5.5 %collective-permute-done.54.refs_3_ = bf16[176,1024]{1,0:T(8,128)(2,1)S(1)} collective-permute-done((bf16[176,1024]{1,0:T(8,128)(2,1)S(1)}, bf16[176,1024]{1,0:T(8,128)(2,1)S(1)}, u32[]{:S(2)}, u32[]{:S(2)}) %collective-permute-start.54) | collective-permute-done | bytes 360480 | tf_op jit(solution)/shard_map/ppermute | solution.py:65
  261.6 2.3 collective-permute-done.66.other
  (225 shorter events, 93.4 us)
Async XLA Ops:
  18.5 15.7 %collective-permute-start.5 = (bf16[128,1024]{1,0:T(8,128)(2,1)S(1)}, bf16[128,1024]{1,0:T(8,128)(2,1)S(1)}, u32[]{:S(2)}, u32[]{:S(2)}) collective-permute-start(bf16[128,1024]{1,0:T(8,128)(2,1)S(1)} %bitcast.74), channel_id=1, source_target_pairs={{0,16},{4,20},{8,24},{12,28},{16,0},{20,4},{24,8},{28,12},{1,17},{... | collective-permute-start | bytes 786440 | tf_op jit(solution)/shard_map/ppermute | solution.py:65
  34.2 20.9 %collective-permute-start.10 = (bf16[256,1024]{1,0:T(8,128)(2,1)S(1)}, bf16[256,1024]{1,0:T(8,128)(2,1)S(1)}, u32[]{:S(2)}, u32[]{:S(2)}) collective-permute-start(bf16[256,1024]{1,0:T(8,128)(2,1)S(1)} %shard_map.309.m), channel_id=1, source_target_pairs={{0,8},{4,12},{8,0},{12,4},{16,24},{20,28},{24,16},{28,20},{1,9},{5... | collective-permute-start | bytes 1572872 | tf_op jit(solution)/shard_map/ppermute | solution.py:65
  35.2 17.8 %collective-permute-start.11 = (bf16[128,1024]{1,0:T(8,128)(2,1)S(1)}, bf16[128,1024]{1,0:T(8,128)(2,1)S(1)}, u32[]{:S(2)}, u32[]{:S(2)}) collective-permute-start(bf16[128,1024]{1,0:T(8,128)(2,1)S(1)} %bitcast.83), channel_id=1, source_target_pairs={{0,16},{4,20},{8,24},{12,28},{16,0},{20,4},{24,8},{28,12},{1,17},{... | collective-permute-start | bytes 786440 | tf_op jit(solution)/shard_map/ppermute | solution.py:65
  38.5 14.5 %collective-permute-start.14 = (bf16[256,128]{1,0:T(8,128)(2,1)S(1)}, bf16[256,128]{1,0:T(8,128)(2,1)S(1)}, u32[]{:S(2)}, u32[]{:S(2)}) collective-permute-start(bf16[256,128]{1,0:T(8,128)(2,1)S(1)} %shard_map.308.m), channel_id=1, source_target_pairs={{0,16},{4,20},{8,24},{12,28},{16,0},{20,4},{24,8},{28,12},{1,17},{... | collective-permute-start | bytes 196616 | tf_op jit(solution)/shard_map/ppermute | solution.py:65
  55.2 28.0 %collective-permute-start.15 = (bf16[512,1024]{1,0:T(8,128)(2,1)S(1)}, bf16[512,1024]{1,0:T(8,128)(2,1)S(1)}, u32[]{:S(2)}, u32[]{:S(2)}) collective-permute-start(bf16[512,1024]{1,0:T(8,128)(2,1)S(1)} %shard_map.312.refs_0_.near_ref), channel_id=1, source_target_pairs={{0,4},{4,0},{8,12},{12,8},{16,20},{20,16},{24,28},{28,24},{1,5},{5... | collective-permute-start | bytes 3145736 | tf_op jit(solution)/shard_map/ppermute | solution.py:65
  56.8 13.6 %collective-permute-start.16 = (bf16[128,1024]{1,0:T(8,128)(2,1)S(1)}, bf16[128,1024]{1,0:T(8,128)(2,1)S(1)}, u32[]{:S(2)}, u32[]{:S(2)}) collective-permute-start(bf16[128,1024]{1,0:T(8,128)(2,1)S(1)} %bitcast.81), channel_id=1, source_target_pairs={{0,16},{4,20},{8,24},{12,28},{16,0},{20,4},{24,8},{28,12},{1,17},{... | collective-permute-start | bytes 786440 | tf_op jit(solution)/shard_map/ppermute | solution.py:65
  70.4 12.7 %collective-permute-start.17 = (bf16[256,1024]{1,0:T(8,128)(2,1)S(1)}, bf16[256,1024]{1,0:T(8,128)(2,1)S(1)}, u32[]{:S(2)}, u32[]{:S(2)}) collective-permute-start(bf16[256,1024]{1,0:T(8,128)(2,1)S(1)} %shard_map.316.m), channel_id=1, source_target_pairs={{0,8},{4,12},{8,0},{12,4},{16,24},{20,28},{24,16},{28,20},{1,9},{5... | collective-permute-start | bytes 1572872 | tf_op jit(solution)/shard_map/ppermute | solution.py:65
  71.0 21.7 %collective-permute-start.21 = (bf16[256,1024]{1,0:T(8,128)(2,1)S(1)}, bf16[256,1024]{1,0:T(8,128)(2,1)S(1)}, u32[]{:S(2)}, u32[]{:S(2)}) collective-permute-start(bf16[256,1024]{1,0:T(8,128)(2,1)S(1)} %shard_map.311.m), channel_id=1, source_target_pairs={{0,4},{4,0},{8,12},{12,8},{16,20},{20,16},{24,28},{28,24},{1,5},{5... | collective-permute-start | bytes 1572872 | tf_op jit(solution)/shard_map/ppermute | solution.py:65
  71.3 11.9 %collective-permute-start.18 = (bf16[512,256]{1,0:T(8,128)(2,1)S(1)}, bf16[512,256]{1,0:T(8,128)(2,1)S(1)}, u32[]{:S(2)}, u32[]{:S(2)}) collective-permute-start(bf16[512,256]{1,0:T(8,128)(2,1)S(1)} %shard_map.317.rest_0_), channel_id=1, source_target_pairs={{0,1},{1,0},{2,3},{3,2},{4,5},{5,4},{6,7},{7,6},{8,9},{9,8},{10,11... | collective-permute-start | bytes 786440 | tf_op jit(solution)/shard_map/ppermute | solution.py:65
  83.3 11.2 %collective-permute-start.26 = (bf16[512,256]{1,0:T(8,128)(2,1)S(1)}, bf16[512,256]{1,0:T(8,128)(2,1)S(1)}, u32[]{:S(2)}, u32[]{:S(2)}) collective-permute-start(bf16[512,256]{1,0:T(8,128)(2,1)S(1)} %shard_map.319.rest_4_), channel_id=1, source_target_pairs={{0,2},{1,3},{2,0},{3,1},{4,6},{5,7},{6,4},{7,5},{8,10},{9,11},{10,... | collective-permute-start | bytes 786440 | tf_op jit(solution)/shard_map/ppermute | solution.py:65
  86.4 11.6 %collective-permute-start.23 = (bf16[2,176,256]{2,1,0:T(8,128)(2,1)S(1)}, bf16[2,176,256]{2,1,0:T(8,128)(2,1)S(1)}, u32[]{:S(2)}, u32[]{:S(2)}) collective-permute-start(bf16[2,176,256]{2,1,0:T(8,128)(2,1)S(1)} %get-tuple-element.491), channel_id=1, source_target_pairs={{0,2},{1,3},{2,0},{3,1},{4,6},{5,7},{6,4},{7,5},{8,10},{9,11},{10,... | collective-permute-start | bytes 540680 | tf_op jit(solution)/shard_map/ppermute | solution.py:65
  88.5 24.7 %collective-permute-start.29 = (bf16[512,1024]{1,0:T(8,128)(2,1)S(1)}, bf16[512,1024]{1,0:T(8,128)(2,1)S(1)}, u32[]{:S(2)}, u32[]{:S(2)}) collective-permute-start(bf16[512,1024]{1,0:T(8,128)(2,1)S(1)} %shard_map.318.up_near), channel_id=1, source_target_pairs={{0,4},{4,0},{8,12},{12,8},{16,20},{20,16},{24,28},{28,24},{1,5},{5... | collective-permute-start | bytes 3145736 | tf_op jit(solution)/shard_map/ppermute | solution.py:65
  92.7 21.5 %collective-permute-start.30 = (bf16[512,1024]{1,0:T(8,128)(2,1)S(1)}, bf16[512,1024]{1,0:T(8,128)(2,1)S(1)}, u32[]{:S(2)}, u32[]{:S(2)}) collective-permute-start(bf16[512,1024]{1,0:T(8,128)(2,1)S(1)} %shard_map.321.down_near), channel_id=1, source_target_pairs={{0,8},{4,12},{8,0},{12,4},{16,24},{20,28},{24,16},{28,20},{1,9},{5... | collective-permute-start | bytes 3145736 | tf_op jit(solution)/shard_map/ppermute | solution.py:65
  102.2 10.5 %collective-permute-start.32 = (bf16[176,1024]{1,0:T(8,128)(2,1)S(1)}, bf16[176,1024]{1,0:T(8,128)(2,1)S(1)}, u32[]{:S(2)}, u32[]{:S(2)}) collective-permute-start(bf16[176,1024]{1,0:T(8,128)(2,1)S(1)} %get-tuple-element.532.x0), channel_id=1, source_target_pairs={{0,2},{1,3},{2,0},{3,1},{4,6},{5,7},{6,4},{7,5},{8,10},{9,11},{10,... | collective-permute-start | bytes 1081352 | tf_op jit(solution)/shard_map/ppermute | solution.py:65
  121.7 10.5 %collective-permute-start.35 = (bf16[176,1024]{1,0:T(8,128)(2,1)S(1)}, bf16[176,1024]{1,0:T(8,128)(2,1)S(1)}, u32[]{:S(2)}, u32[]{:S(2)}) collective-permute-start(bf16[176,1024]{1,0:T(8,128)(2,1)S(1)} %shard_map.328), channel_id=1, source_target_pairs={{0,2},{1,3},{2,0},{3,1},{4,6},{5,7},{6,4},{7,5},{8,10},{9,11},{10,... | collective-permute-start | bytes 1081352 | tf_op jit(solution)/shard_map/ppermute | solution.py:65
  149.0 10.6 %collective-permute-start.37 = (bf16[176,1024]{1,0:T(8,128)(2,1)S(1)}, bf16[176,1024]{1,0:T(8,128)(2,1)S(1)}, u32[]{:S(2)}, u32[]{:S(2)}) collective-permute-start(bf16[176,1024]{1,0:T(8,128)(2,1)S(1)} %get-tuple-element.582), channel_id=1, source_target_pairs={{0,1},{1,0},{2,3},{3,2},{4,5},{5,4},{6,7},{7,6},{8,9},{9,8},{10,11... | collective-permute-start | bytes 1081352 | tf_op jit(solution)/shard_map/ppermute | solution.py:65
  150.4 10.8 %collective-permute-start.41 = (bf16[176,1024]{1,0:T(8,128)(2,1)S(1)}, bf16[176,1024]{1,0:T(8,128)(2,1)S(1)}, u32[]{:S(2)}, u32[]{:S(2)}) collective-permute-start(bf16[176,1024]{1,0:T(8,128)(2,1)S(1)} %shard_map.332), channel_id=1, source_target_pairs={{0,2},{1,3},{2,0},{3,1},{4,6},{5,7},{6,4},{7,5},{8,10},{9,11},{10,... | collective-permute-start | bytes 1081352 | tf_op jit(solution)/shard_map/ppermute | solution.py:65
  155.3 25.2 %collective-permute-start.46 = (bf16[2,2,128,1024]{3,2,1,0:T(8,128)(2,1)S(1)}, bf16[2,2,128,1024]{3,2,1,0:T(8,128)(2,1)S(1)}, u32[]{:S(2)}, u32[]{:S(2)}) collective-permute-start(bf16[2,2,128,1024]{3,2,1,0:T(8,128)(2,1)S(1)} %bitcast.77), channel_id=1, source_target_pairs={{0,4},{4,0},{8,12},{12,8},{16,20},{20,16},{24,28},{28,24},{1,5},{5... | collective-permute-start | bytes 3145736 | tf_op jit(solution)/shard_map/ppermute | solution.py:65
  156.9 24.9 %collective-permute-start.47 = (bf16[2,2,128,1024]{3,2,1,0:T(8,128)(2,1)S(1)}, bf16[2,2,128,1024]{3,2,1,0:T(8,128)(2,1)S(1)}, u32[]{:S(2)}, u32[]{:S(2)}) collective-permute-start(bf16[2,2,128,1024]{3,2,1,0:T(8,128)(2,1)S(1)} %bitcast.76), channel_id=1, source_target_pairs={{0,8},{4,12},{8,0},{12,4},{16,24},{20,28},{24,16},{28,20},{1,9},{5... | collective-permute-start | bytes 3145736 | tf_op jit(solution)/shard_map/ppermute | solution.py:65
  166.4 23.9 %collective-permute-start.52 = (bf16[1024,256]{1,0:T(8,128)(2,1)S(1)}, bf16[1024,256]{1,0:T(8,128)(2,1)S(1)}, u32[]{:S(2)}, u32[]{:S(2)}) collective-permute-start(bf16[1024,256]{1,0:T(8,128)(2,1)S(1)} %get-tuple-element.638), channel_id=1, source_target_pairs={{0,1},{1,0},{2,3},{3,2},{4,5},{5,4},{6,7},{7,6},{8,9},{9,8},{10,11... | collective-permute-start | bytes 1572872 | tf_op jit(solution)/shard_map/ppermute | solution.py:65
  172.1 18.2 %collective-permute-start.53 = (bf16[1024,256]{1,0:T(8,128)(2,1)S(1)}, bf16[1024,256]{1,0:T(8,128)(2,1)S(1)}, u32[]{:S(2)}, u32[]{:S(2)}) collective-permute-start(bf16[1024,256]{1,0:T(8,128)(2,1)S(1)} %shard_map.341), channel_id=1, source_target_pairs={{0,2},{1,3},{2,0},{3,1},{4,6},{5,7},{6,4},{7,5},{8,10},{9,11},{10,... | collective-permute-start | bytes 1572872 | tf_op jit(solution)/shard_map/ppermute | solution.py:65
  181.9 14.9 %collective-permute-start.51 = (bf16[2,128,1024]{2,1,0:T(8,128)(2,1)S(1)}, bf16[2,128,1024]{2,1,0:T(8,128)(2,1)S(1)}, u32[]{:S(2)}, u32[]{:S(2)}) collective-permute-start(bf16[2,128,1024]{2,1,0:T(8,128)(2,1)S(1)} %shard_map.344), channel_id=1, source_target_pairs={{0,8},{4,12},{8,0},{12,4},{16,24},{20,28},{24,16},{28,20},{1,9},{5... | collective-permute-start | bytes 1572872 | tf_op jit(solution)/shard_map/ppermute | solution.py:65
  183.7 13.2 %collective-permute-start.50 = (bf16[2,2,128,512]{3,2,1,0:T(8,128)(2,1)S(1)}, bf16[2,2,128,512]{3,2,1,0:T(8,128)(2,1)S(1)}, u32[]{:S(2)}, u32[]{:S(2)}) collective-permute-start(bf16[2,2,128,512]{3,2,1,0:T(8,128)(2,1)S(1)} %bitcast.80), channel_id=1, source_target_pairs={{0,4},{4,0},{8,12},{12,8},{16,20},{20,16},{24,28},{28,24},{1,5},{5... | collective-permute-start | bytes 1572872 | tf_op jit(solution)/shard_map/ppermute | solution.py:65
  190.4 29.6 %collective-permute-start.56 = (bf16[2,2,128,640]{3,2,1,0:T(8,128)(2,1)S(1)}, bf16[2,2,128,640]{3,2,1,0:T(8,128)(2,1)S(1)}, u32[]{:S(2)}, u32[]{:S(2)}) collective-permute-start(bf16[2,2,128,640]{3,2,1,0:T(8,128)(2,1)S(1)} %shard_map.349), channel_id=1, source_target_pairs={{0,8},{4,12},{8,0},{12,4},{16,24},{20,28},{24,16},{28,20},{1,9},{5... | collective-permute-start | bytes 1966088 | tf_op jit(solution)/shard_map/ppermute | solution.py:65
  197.1 22.9 %collective-permute-start.55 = (bf16[2,128,1024]{2,1,0:T(8,128)(2,1)S(1)}, bf16[2,128,1024]{2,1,0:T(8,128)(2,1)S(1)}, u32[]{:S(2)}, u32[]{:S(2)}) collective-permute-start(bf16[2,128,1024]{2,1,0:T(8,128)(2,1)S(1)} %shard_map.352), channel_id=1, source_target_pairs={{0,4},{4,0},{8,12},{12,8},{16,20},{20,16},{24,28},{28,24},{1,5},{5... | collective-permute-start | bytes 1572872 | tf_op jit(solution)/shard_map/ppermute | solution.py:65
  197.7 22.2 %collective-permute-start.57 = (bf16[2,128,512]{2,1,0:T(8,128)(2,1)S(1)}, bf16[2,128,512]{2,1,0:T(8,128)(2,1)S(1)}, u32[]{:S(2)}, u32[]{:S(2)}) collective-permute-start(bf16[2,128,512]{2,1,0:T(8,128)(2,1)S(1)} %shard_map.351), channel_id=1, source_target_pairs={{0,8},{4,12},{8,0},{12,4},{16,24},{20,28},{24,16},{28,20},{1,9},{5... | collective-permute-start | bytes 786440 | tf_op jit(solution)/shard_map/ppermute | solution.py:65
  199.5 20.5 %collective-permute-start.58 = (bf16[128,1024]{1,0:T(8,128)(2,1)S(1)}, bf16[128,1024]{1,0:T(8,128)(2,1)S(1)}, u32[]{:S(2)}, u32[]{:S(2)}) collective-permute-start(bf16[128,1024]{1,0:T(8,128)(2,1)S(1)} %shard_map.350), channel_id=1, source_target_pairs={{0,16},{4,20},{8,24},{12,28},{16,0},{20,4},{24,8},{28,12},{1,17},{... | collective-permute-start | bytes 786440 | tf_op jit(solution)/shard_map/ppermute | solution.py:65
  221.9 26.4 %collective-permute-start.59 = (bf16[128,1024]{1,0:T(8,128)(2,1)S(1)}, bf16[128,1024]{1,0:T(8,128)(2,1)S(1)}, u32[]{:S(2)}, u32[]{:S(2)}) collective-permute-start(bf16[128,1024]{1,0:T(8,128)(2,1)S(1)} %shard_map.354), channel_id=1, source_target_pairs={{0,16},{4,20},{8,24},{12,28},{16,0},{20,4},{24,8},{28,12},{1,17},{... | collective-permute-start | bytes 786440 | tf_op jit(solution)/shard_map/ppermute | solution.py:65
  224.6 22.1 %collective-permute-start.63 = (bf16[128,512]{1,0:T(8,128)(2,1)S(1)}, bf16[128,512]{1,0:T(8,128)(2,1)S(1)}, u32[]{:S(2)}, u32[]{:S(2)}) collective-permute-start(bf16[128,512]{1,0:T(8,128)(2,1)S(1)} %shard_map.356), channel_id=1, source_target_pairs={{0,16},{4,20},{8,24},{12,28},{16,0},{20,4},{24,8},{28,12},{1,17},{... | collective-permute-start | bytes 393224 | tf_op jit(solution)/shard_map/ppermute | solution.py:65
  228.0 21.8 %collective-permute-start.64 = (bf16[128,640]{1,0:T(8,128)(2,1)S(1)}, bf16[128,640]{1,0:T(8,128)(2,1)S(1)}, u32[]{:S(2)}, u32[]{:S(2)}) collective-permute-start(bf16[128,640]{1,0:T(8,128)(2,1)S(1)} %shard_map.360), channel_id=1, source_target_pairs={{0,16},{4,20},{8,24},{12,28},{16,0},{20,4},{24,8},{28,12},{1,17},{... | collective-permute-start | bytes 491528 | tf_op jit(solution)/shard_map/ppermute | solution.py:65
  230.7 17.6 %collective-permute-start.62 = (bf16[2,32,1024]{2,1,0:T(8,128)(2,1)S(1)}, bf16[2,32,1024]{2,1,0:T(8,128)(2,1)S(1)}, u32[]{:S(2)}, u32[]{:S(2)}) collective-permute-start(bf16[2,32,1024]{2,1,0:T(8,128)(2,1)S(1)} %get-tuple-element.723), channel_id=1, source_target_pairs={{0,2},{1,3},{2,0},{3,1},{4,6},{5,7},{6,4},{7,5},{8,10},{9,11},{10,... | collective-permute-start | bytes 393224 | tf_op jit(solution)/shard_map/ppermute | solution.py:65
  232.6 18.2 %collective-permute-start.48 = (bf16[176,1024]{1,0:T(8,128)(2,1)S(1)}, bf16[176,1024]{1,0:T(8,128)(2,1)S(1)}, u32[]{:S(2)}, u32[]{:S(2)}) collective-permute-start(bf16[176,1024]{1,0:T(8,128)(2,1)S(1)} %get-tuple-element.682), channel_id=1, source_target_pairs={{0,1},{1,0},{2,3},{3,2},{4,5},{5,4},{6,7},{7,6},{8,9},{9,8},{10,11... | collective-permute-start | bytes 1081352 | tf_op jit(solution)/shard_map/ppermute | solution.py:65
  (52 other events, 379.0 us)

commit v2 on v1

--- a/solution.py
+++ b/solution.py
@@ -489,13 +489,11 @@
                 out[:, far_block(place, q + half, order)] = block.astype(out.dtype)
 
 
-def half_grad_kernel(near, start, left_ref, right_ref, out_ref):
-    left = left_ref[...]
-    if near is not None:
-        left = left_ref[:, : D // 2] if near else left_ref[:, D // 2 :]
-    for n in range(out_ref.shape[1] // TILE):
-        at = slice(start + n * TILE, start + (n + 1) * TILE)
-        out_ref[:, n * TILE : (n + 1) * TILE] = dot_tn(left, right_ref[:, at]).astype(bf16)
+def half_grad_kernel(near, left_ref, right_ref, out_ref):
+    left = left_ref[:, : D // 2] if near else left_ref[:, D // 2 :]
+    for n in range(right_ref.shape[1] // TILE):
+        at = slice(n * TILE, (n + 1) * TILE)
+        out_ref[:, at] = dot_tn(left, right_ref[:, at]).astype(bf16)
 
 
 def normal_parts(u):
@@ -934,11 +932,9 @@
     )
     meet.far_pair(keep, give)
 
-    def half_grad(left, right, near, start=0, columns=None):
-        out = shape_of((D if near is None else D // 2, columns or right.shape[1]), bf16)
-        (made,) = run(
-            lambda *ins: call(partial(half_grad_kernel, near, start), ins, [out]), left, right
-        )
+    def half_grad(left, right, near):
+        out = shape_of((D // 2, right.shape[1]), bf16)
+        (made,) = run(lambda *ins: call(partial(half_grad_kernel, near), ins, [out]), left, right)
         return made
 
     meet.send()
@@ -985,17 +981,16 @@
         qkv, probs, far, got_far, notes, d_qkv, d_sums, d_grid,
     )
 
-    def with_proj(q, k, c, y, small):
+    def with_proj(k, c, y, small):
         p = (k.astype(f32) + c.astype(f32) + y.astype(f32)).astype(bf16)
-        return jnp.concatenate([q, p, small], axis=-1).astype(f32)
-
-    give = half_grad(group, d_qkv, False, 0, D // 2)
+        return jnp.concatenate([p, small], axis=-1).astype(f32)
+
+    give = half_grad(group, d_qkv, False)
     s_first = Scatter(run, (give,), "dp", Z_X, given=give).send()
-    across = s_first.other
     run.wait(s_up.other, s_down.other)
     s_up.take().send()
-    s_first.own(half_grad(group, d_qkv, True, 0, D // 2))
-    grad_b = half_grad(group, d_qkv, None, D // 2, 3 * width - D // 2)
+    s_down.take().send()
+    s_first.own(half_grad(group, d_qkv, True))
     plains = [pltpu.VMEM((24, D), f32)] * 2
     (small_grads,) = run(
         lambda *ins: call(
@@ -1012,16 +1007,16 @@
     )
     meet_tok = Meet().near_pair(parts[0], parts[1]).far_pair(parts[2], parts[3])
     s_second = Scatter(
-        run, (grad_b, *meet_proj.terms(), small_grads), "dp", Z_X, walk=(1, 2, 0), base=with_proj
+        run, (*meet_proj.terms(), small_grads), "dp", Z_X, base=with_proj
     ).send()
     s_up.take().send()
     s_first.take().send()
-    s_down.take().send(across)
+    run.wait(s_first.other)
+    s_first.take().send()
     meet_tok.send()
-    run.wait(s_down.other, s_second.other, s_first.other, s_up.other)
+    run.wait(s_up.other, s_down.other, s_second.other, s_first.other)
+    s_second.take().send()
     s_down.take().send()
-    s_second.take().send()
-    s_first.take().send()
 
     def columns_back(scatters):
         sums = [x.sum().reshape(tp, rows, -1) for x in scatters]
@@ -1061,12 +1056,6 @@
 
     s_up.take()
     x_up = columns_back([s_up]).turn()
-    s_second.take().send()
-    run.wait(x_up.other, s_down.other, s_first.other, s_second.other)
-    s_down.take()
-    s_first.take()
-    s_second.take()
-    x_rest = columns_back([s_down, s_first, s_second])
     out_f = shape_of((1, SLOTS, D), f32)
     grad_tokens = run(
         lambda *ins: glue(
@@ -1077,6 +1066,13 @@
         ),
         d_resid_one, *meet_tok.terms(),
     )
+    run.wait(s_second.other, x_up.other)
+    s_second.take().send()
+    run.wait(s_down.other, s_second.other)
+    s_down.take()
+    s_first.take()
+    s_second.take()
+    x_rest = columns_back([s_down, s_first, s_second])
     x_rest.turn()
     (grad_up,) = whole_rows(x_up, (1,), (hidden,), ())
     grad_down, grad_qkv, grad_proj, *out = whole_rows(

time: 269 us -> 264 us (0.981)
  starting transfers between devices: 57.3 us -> 53.6 us
    ppermute x67, starting transfers between devices: 57.3 us -> 53.6 us  [swap(): lax.ppermute(x, axis, [(i, i ^ b) for i in range(lax.axis_size(axis))])]
    pallas_call x70 -> x69, Pallas kernels: 56.2 us -> 56 us  [call(): pl.pallas_call(kernel, in_specs=[pl.BlockSpec(memory_space=m) for m in sp...]
  transfers between devices with their start and end apart: 67 -> 67, of which waited for: 31 -> 35; matrix products, arithmetic and copies ran while one was open for 1% -> 1% of each run, Pallas kernels for 19% -> 19%
where the time goes in v2:
time: 264 us; the launch traced here: 261 us
  waiting for transfers between devices  138 us (52%)
  Pallas kernels  60.1 us (23%)
  starting transfers between devices  53.6 us (20%)
  local copies, waits for them, and re-layouts  5.66 us (2%)
    ppermute x67, waiting for transfers between devices, swap(): lax.ppermute(x, axis, [(i, i ^ b) for i in range(lax.axis_size(axis))])  138 us
    pallas_call x69, Pallas kernels, call(): pl.pallas_call(kernel, in_specs=[pl.BlockSpec(memory_space=m) for m in sp...  56 us
    ppermute x67, starting transfers between devices, swap(): lax.ppermute(x, axis, [(i, i ^ b) for i in range(lax.axis_size(axis))])  53.6 us
    unnamed x35, local copies, waits for them, and re-layouts  5.29 us
  transfers between devices with their start and end apart: 67, of which 35 were waited for; matrix products, arithmetic and copies ran while one was open for 1% of the time, Pallas kernels for 19%

profile of v2, /device:TPU:0, one launch (start us, length us, event | category | flops | bytes accessed | tf_op | source)
XLA Modules:
  0.0 261.0 jit_solution(6936623640844467638)
XLA Ops:
  7.6 3.0 %collective-permute-start.3 = (bf16[2,32,1024]{2,1,0:T(8,128)(2,1)S(1)}, bf16[2,32,1024]{2,1,0:T(8,128)(2,1)S(1)}, u32[]{:S(2)}, u32[]{:S(2)}) collective-permute-start(bf16[2,32,1024]{2,1,0:T(8,128)(2,1)S(1)} %get-tuple-element.404), channel_id=1, source_target_pairs={{0,2},{1,3},{2,0},{3,1},{4,6},{5,7},{6,4},{7,5},{8,10},{9,11},{10,... | collective-permute-start | bytes 393224 | tf_op jit(solution)/shard_map/ppermute | solution.py:65
  11.9 2.4 collective-permute-done.3.other
  18.5 2.7 %collective-permute-start.5 = (bf16[128,1024]{1,0:T(8,128)(2,1)S(1)}, bf16[128,1024]{1,0:T(8,128)(2,1)S(1)}, u32[]{:S(2)}, u32[]{:S(2)}) collective-permute-start(bf16[128,1024]{1,0:T(8,128)(2,1)S(1)} %bitcast.69), channel_id=1, source_target_pairs={{0,16},{4,20},{8,24},{12,28},{16,0},{20,4},{24,8},{28,12},{1,17},{... | collective-permute-start | bytes 786440 | tf_op jit(solution)/shard_map/ppermute | solution.py:65
  21.7 3.1 %collective-permute-done.6.o = bf16[32,128]{1,0:T(8,128)(2,1)S(1)} collective-permute-done((bf16[32,128]{1,0:T(8,128)(2,1)S(1)}, bf16[32,128]{1,0:T(8,128)(2,1)S(1)}, u32[]{:S(2)}, u32[]{:S(2)}) %collective-permute-start.6) | collective-permute-done | bytes 8224 | tf_op jit(solution)/shard_map/ppermute | solution.py:65
  30.6 3.5 %collective-permute-done.9.o = bf16[128,128]{1,0:T(8,128)(2,1)S(1)} collective-permute-done((bf16[128,128]{1,0:T(8,128)(2,1)S(1)}, bf16[128,128]{1,0:T(8,128)(2,1)S(1)}, u32[]{:S(2)}, u32[]{:S(2)}) %collective-permute-start.9) | collective-permute-done | bytes 32800 | tf_op jit(solution)/shard_map/ppermute | solution.py:65
  35.2 3.3 %collective-permute-start.11 = (bf16[128,1024]{1,0:T(8,128)(2,1)S(1)}, bf16[128,1024]{1,0:T(8,128)(2,1)S(1)}, u32[]{:S(2)}, u32[]{:S(2)}) collective-permute-start(bf16[128,1024]{1,0:T(8,128)(2,1)S(1)} %bitcast.78), channel_id=1, source_target_pairs={{0,16},{4,20},{8,24},{12,28},{16,0},{20,4},{24,8},{28,12},{1,17},{... | collective-permute-start | bytes 786440 | tf_op jit(solution)/shard_map/ppermute | solution.py:65
  38.5 14.4 %collective-permute-done.14.o = bf16[256,128]{1,0:T(8,128)(2,1)S(1)} collective-permute-done((bf16[256,128]{1,0:T(8,128)(2,1)S(1)}, bf16[256,128]{1,0:T(8,128)(2,1)S(1)}, u32[]{:S(2)}, u32[]{:S(2)}) %collective-permute-start.14) | collective-permute-done | bytes 65568 | tf_op jit(solution)/shard_map/ppermute | solution.py:65
  58.9 4.1 %shard_map.315.bias_ref = f32[4,4,176,176]{3,2,1,0:T(8,128)S(1)} custom-call(bf16[4,16,256]{2,1,0:T(8,128)(2,1)S(1)} %shard_map.310.notes_ref, f32[12,256]{1,0:T(8,128)S(1)} %get-tuple-element.466.ext_ref), custom_call_target="tpu_custom_call" | custom-call | tf_op jit(solution)/shard_map/pallas_call | solution.py:243
  62.9 7.5 %collective-permute-done.16.o = bf16[128,1024]{1,0:T(8,128)(2,1)S(1)} collective-permute-done((bf16[128,1024]{1,0:T(8,128)(2,1)S(1)}, bf16[128,1024]{1,0:T(8,128)(2,1)S(1)}, u32[]{:S(2)}, u32[]{:S(2)}) %collective-permute-start.16) | collective-permute-done | bytes 262176 | tf_op jit(solution)/shard_map/ppermute | solution.py:65
  71.3 6.4 %collective-permute-done.19.rest_2_ = bf16[512,256]{1,0:T(8,128)(2,1)S(1)} collective-permute-done((bf16[512,256]{1,0:T(8,128)(2,1)S(1)}, bf16[512,256]{1,0:T(8,128)(2,1)S(1)}, u32[]{:S(2)}, u32[]{:S(2)}) %collective-permute-start.19) | collective-permute-done | bytes 262176 | tf_op jit(solution)/shard_map/ppermute | solution.py:65
  77.8 5.4 %collective-permute-done.17.o = bf16[256,1024]{1,0:T(8,128)(2,1)S(1)} collective-permute-done((bf16[256,1024]{1,0:T(8,128)(2,1)S(1)}, bf16[256,1024]{1,0:T(8,128)(2,1)S(1)}, u32[]{:S(2)}, u32[]{:S(2)}) %collective-permute-start.17) | collective-permute-done | bytes 524320 | tf_op jit(solution)/shard_map/ppermute | solution.py:65
  83.4 3.1 %shard_map.320 = (bf16[704,1024]{1,0:T(8,128)(2,1)S(1)}, bf16[704,768]{1,0:T(8,128)(2,1)S(1)}, f32[4,4,176,176]{3,2,1,0:T(8,128)S(1)}, bf16[2,176,256]{2,1,0:T(8,128)(2,1)S(1)}) custom-call(s32[2]{0:T(128)S(1)} %pad_add_fusion.at.at_ref, bf16[176,1024]{1,0:T(8,128)(2,1)S(1)} %collective-permute-done.12.refs_2_.d0, ...), custom_call_target="tpu_custom_call" | custom-call | tf_op jit(solution)/shard_map/pallas_call | solution.py:31
  89.1 3.6 %collective-permute-done.21.o = bf16[256,1024]{1,0:T(8,128)(2,1)S(1)} collective-permute-done((bf16[256,1024]{1,0:T(8,128)(2,1)S(1)}, bf16[256,1024]{1,0:T(8,128)(2,1)S(1)}, u32[]{:S(2)}, u32[]{:S(2)}) %collective-permute-start.21) | collective-permute-done | bytes 524320 | tf_op jit(solution)/shard_map/ppermute | solution.py:65
  95.0 3.1 %shard_map.322 = (bf16[704,1024]{1,0:T(8,128)(2,1)S(1)}, bf16[704,768]{1,0:T(8,128)(2,1)S(1)}, f32[4,4,176,176]{3,2,1,0:T(8,128)S(1)}, bf16[2,176,256]{2,1,0:T(8,128)(2,1)S(1)}) custom-call(s32[2]{0:T(128)S(1)} %pad_add_fusion.at.at_ref, ...), custom_call_target="tpu_custom_call", output_to_operand_aliasing={{0}: (7, {}), {1}: (8, {}), {2}: (9, {})} | custom-call | tf_op jit(solution)/shard_map/pallas_call | solution.py:31
  103.4 9.3 %collective-permute-done.32.x0 = bf16[176,1024]{1,0:T(8,128)(2,1)S(1)} collective-permute-done((bf16[176,1024]{1,0:T(8,128)(2,1)S(1)}, bf16[176,1024]{1,0:T(8,128)(2,1)S(1)}, u32[]{:S(2)}, u32[]{:S(2)}) %collective-permute-start.32) | collective-permute-done | bytes 360480 | tf_op jit(solution)/shard_map/ppermute | solution.py:65
  114.2 2.8 %shard_map.326 = (bf16[704,1024]{1,0:T(8,128)(2,1)S(1)}, f32[704,1024]{1,0:T(8,128)S(1)}, bf16[704,1024]{1,0:T(8,128)(2,1)S(1)}, f32[176,1024]{1,0:T(8,128)S(1)}, bf16[176,1024]{1,0:T(8,128)(2,1)S(1)}) custom-call(s32[2]{0:T(128)S(1)} %pad_add_fusion.at.at_ref, bf16[176,1024]{1,0:T(8,128)(2,1)S(1)} %get-tuple-element.525.x0, ...), custom_call_target="tpu_custom_call" | custom-call | tf_op jit(solution)/shard_map/pallas_call | solution.py:31
  117.1 2.9 %shard_map.327 = (bf16[704,1024]{1,0:T(8,128)(2,1)S(1)}, f32[704,1024]{1,0:T(8,128)S(1)}, bf16[704,1024]{1,0:T(8,128)(2,1)S(1)}, f32[176,1024]{1,0:T(8,128)S(1)}, bf16[176,1024]{1,0:T(8,128)(2,1)S(1)}) custom-call(s32[2]{0:T(128)S(1)} %pad_add_fusion.at.at_ref, ...), custom_call_target="tpu_custom_call", output_to_operand_aliasing={{0}: (8, {}), {1}: (9, {}), {2}: (10, {})} | custom-call | tf_op jit(solution)/shard_map/pallas_call | solution.py:31
  123.6 8.7 %collective-permute-done.35.got_y = bf16[176,1024]{1,0:T(8,128)(2,1)S(1)} collective-permute-done((bf16[176,1024]{1,0:T(8,128)(2,1)S(1)}, bf16[176,1024]{1,0:T(8,128)(2,1)S(1)}, u32[]{:S(2)}, u32[]{:S(2)}) %collective-permute-start.35) | collective-permute-done | bytes 360480 | tf_op jit(solution)/shard_map/ppermute | solution.py:65
  135.5 7.9 %collective-permute-done.38.g0 = bf16[176,1024]{1,0:T(8,128)(2,1)S(1)} collective-permute-done((bf16[176,1024]{1,0:T(8,128)(2,1)S(1)}, bf16[176,1024]{1,0:T(8,128)(2,1)S(1)}, u32[]{:S(2)}, u32[]{:S(2)}) %collective-permute-start.38) | collective-permute-done | bytes 360480 | tf_op jit(solution)/shard_map/ppermute | solution.py:65
  143.4 2.6 %shard_map.330 = (bf16[704,1024]{1,0:T(8,128)(2,1)S(1)}, bf16[704,1024]{1,0:T(8,128)(2,1)S(1)}, f32[2,1024]{1,0:T(2,128)S(1)}, f32[176,1024]{1,0:T(8,128)S(1)}, bf16[176,1024]{1,0:T(8,128)(2,1)S(1)}) custom-call(s32[2]{0:T(128)S(1)} %pad_add_fusion.at.at_ref, bf16[176,1024]{1,0:T(8,128)(2,1)S(1)} %get-tuple-element.567.g0, ...), custom_call_target="tpu_custom_call" | custom-call | tf_op jit(solution)/shard_map/pallas_call | solution.py:31
  146.0 2.4 shard_map.331
  166.6 4.9 %shard_map.339 = (bf16[704,768]{1,0:T(8,128)(2,1)S(1)}, f32[4,768]{1,0:T(4,128)S(1)}, f32[12,128,128]{2,1,0:T(8,128)S(1)}) custom-call(bf16[704,768]{1,0:T(8,128)(2,1)S(1)} %get-tuple-element.645.qkv_ref, f32[4,4,176,176]{3,2,1,0:T(8,128)S(1)} %get-tuple-element.646.probs_ref, bf16[176,256]{1,0:T(8,128)(2,1)S(1)} %get-tuple-element.636.g0, ...), custom_call_target="tpu_custom_call" | custom-call | flops 10000000000 | tf_op jit(solution)/shard_map/pallas_call | solution.py:31
  172.9 5.3 %shard_map.342 = (bf16[704,768]{1,0:T(8,128)(2,1)S(1)}, f32[4,768]{1,0:T(4,128)S(1)}, f32[12,128,128]{2,1,0:T(8,128)S(1)}, f32[12,256]{1,0:T(8,128)S(1)}) custom-call(bf16[704,768]{1,0:T(8,128)(2,1)S(1)} %get-tuple-element.645.qkv_ref, ...), custom_call_target="tpu_custom_call", output_to_operand_aliasing={{0}: (5, {}), {1}: (6, {}), {2}: (7, {})} | custom-call | tf_op jit(solution)/shard_map/pallas_call | solution.py:31
  185.3 2.7 %shard_map.347 = bf16[1024,128]{1,0:T(8,128)(2,1)S(1)} custom-call(s32[2]{0:T(128)S(1)} %pad_add_fusion.at.at_ref, f32[12,256]{1,0:T(8,128)S(1)} %get-tuple-element.665.ext_ref, f32[4,768]{1,0:T(4,128)S(1)} %get-tuple-element.666.sums_ref, f32[2,1024]{1,0:T(2,128)S(1)} %get-tuple-element.667.up_ref, f32[3,1024]{1,0:T(4,128)S(1)} %get-tuple-element.668.one_ref, ...), custom_call_target="tpu_custom_call" | custom-call | tf_op jit(solution)/shard_map/pallas_call | solution.py:31
  190.0 5.0 %collective-permute-done.53 = bf16[1024,256]{1,0:T(8,128)(2,1)S(1)} collective-permute-done((bf16[1024,256]{1,0:T(8,128)(2,1)S(1)}, bf16[1024,256]{1,0:T(8,128)(2,1)S(1)}, u32[]{:S(2)}, u32[]{:S(2)}) %collective-permute-start.53) | collective-permute-done | bytes 524320 | tf_op jit(solution)/shard_map/ppermute | solution.py:65
  195.4 4.1 %collective-permute-done.50.refs_1_ = bf16[2,2,128,768]{3,2,1,0:T(8,128)(2,1)S(1)} collective-permute-done((bf16[2,2,128,768]{3,2,1,0:T(8,128)(2,1)S(1)}, bf16[2,2,128,768]{3,2,1,0:T(8,128)(2,1)S(1)}, u32[]{:S(2)}, u32[]{:S(2)}) %collective-permute-start.50) | collective-permute-done | bytes 786464 | tf_op jit(solution)/shard_map/ppermute | solution.py:65
  204.0 9.3 %collective-permute-done.54.refs_2_ = bf16[2,128,768]{2,1,0:T(8,128)(2,1)S(1)} collective-permute-done((bf16[2,128,768]{2,1,0:T(8,128)(2,1)S(1)}, bf16[2,128,768]{2,1,0:T(8,128)(2,1)S(1)}, u32[]{:S(2)}, u32[]{:S(2)}) %collective-permute-start.54) | collective-permute-done | bytes 393248 | tf_op jit(solution)/shard_map/ppermute | solution.py:65
  218.6 4.2 %collective-permute-done.56.refs_3_ = bf16[128,1024]{1,0:T(8,128)(2,1)S(1)} collective-permute-done((bf16[128,1024]{1,0:T(8,128)(2,1)S(1)}, bf16[128,1024]{1,0:T(8,128)(2,1)S(1)}, u32[]{:S(2)}, u32[]{:S(2)}) %collective-permute-start.56) | collective-permute-done | bytes 262176 | tf_op jit(solution)/shard_map/ppermute | solution.py:65
  222.8 3.5 %collective-permute-done.59.refs_3_ = bf16[128,768]{1,0:T(8,128)(2,1)S(1)} collective-permute-done((bf16[128,768]{1,0:T(8,128)(2,1)S(1)}, bf16[128,768]{1,0:T(8,128)(2,1)S(1)}, u32[]{:S(2)}, u32[]{:S(2)}) %collective-permute-start.59) | collective-permute-done | bytes 196640 | tf_op jit(solution)/shard_map/ppermute | solution.py:65
  230.1 7.1 %collective-permute-done.62.refs_5_ = bf16[2,128,384]{2,1,0:T(8,128)(2,1)S(1)} collective-permute-done((bf16[2,128,384]{2,1,0:T(8,128)(2,1)S(1)}, bf16[2,128,384]{2,1,0:T(8,128)(2,1)S(1)}, u32[]{:S(2)}, u32[]{:S(2)}) %collective-permute-start.62) | collective-permute-done | bytes 196640 | tf_op jit(solution)/shard_map/ppermute | solution.py:65
  237.8 7.5 %collective-permute-done.61.refs_3_ = bf16[128,1024]{1,0:T(8,128)(2,1)S(1)} collective-permute-done((bf16[128,1024]{1,0:T(8,128)(2,1)S(1)}, bf16[128,1024]{1,0:T(8,128)(2,1)S(1)}, u32[]{:S(2)}, u32[]{:S(2)}) %collective-permute-start.61) | collective-permute-done | bytes 262176 | tf_op jit(solution)/shard_map/ppermute | solution.py:65
  253.4 5.4 %collective-permute-done.66.other = bf16[2,32,2176]{2,1,0:T(8,128)(2,1)S(1)} collective-permute-done((bf16[2,32,2176]{2,1,0:T(8,128)(2,1)S(1)}, bf16[2,32,2176]{2,1,0:T(8,128)(2,1)S(1)}, u32[]{:S(2)}, u32[]{:S(2)}) %collective-permute-start.66) | collective-permute-done | bytes 278560 | tf_op jit(solution)/shard_map/ppermute | solution.py:65
  (224 shorter events, 97.3 us)
Async XLA Ops:
  14.3 10.5 %collective-permute-start.8 = (bf16[2,32,2048]{2,1,0:T(8,128)(2,1)S(1)}, bf16[2,32,2048]{2,1,0:T(8,128)(2,1)S(1)}, u32[]{:S(2)}, u32[]{:S(2)}) collective-permute-start(bf16[2,32,2048]{2,1,0:T(8,128)(2,1)S(1)} %get-tuple-element.433), channel_id=1, source_target_pairs={{0,2},{1,3},{2,0},{3,1},{4,6},{5,7},{6,4},{7,5},{8,10},{9,11},{10,... | collective-permute-start | bytes 786440 | tf_op jit(solution)/shard_map/ppermute | solution.py:65
  18.5 15.7 %collective-permute-start.5 = (bf16[128,1024]{1,0:T(8,128)(2,1)S(1)}, bf16[128,1024]{1,0:T(8,128)(2,1)S(1)}, u32[]{:S(2)}, u32[]{:S(2)}) collective-permute-start(bf16[128,1024]{1,0:T(8,128)(2,1)S(1)} %bitcast.69), channel_id=1, source_target_pairs={{0,16},{4,20},{8,24},{12,28},{16,0},{20,4},{24,8},{28,12},{1,17},{... | collective-permute-start | bytes 786440 | tf_op jit(solution)/shard_map/ppermute | solution.py:65
  34.2 20.9 %collective-permute-start.10 = (bf16[256,1024]{1,0:T(8,128)(2,1)S(1)}, bf16[256,1024]{1,0:T(8,128)(2,1)S(1)}, u32[]{:S(2)}, u32[]{:S(2)}) collective-permute-start(bf16[256,1024]{1,0:T(8,128)(2,1)S(1)} %shard_map.309.m), channel_id=1, source_target_pairs={{0,8},{4,12},{8,0},{12,4},{16,24},{20,28},{24,16},{28,20},{1,9},{5... | collective-permute-start | bytes 1572872 | tf_op jit(solution)/shard_map/ppermute | solution.py:65
  35.2 17.8 %collective-permute-start.11 = (bf16[128,1024]{1,0:T(8,128)(2,1)S(1)}, bf16[128,1024]{1,0:T(8,128)(2,1)S(1)}, u32[]{:S(2)}, u32[]{:S(2)}) collective-permute-start(bf16[128,1024]{1,0:T(8,128)(2,1)S(1)} %bitcast.78), channel_id=1, source_target_pairs={{0,16},{4,20},{8,24},{12,28},{16,0},{20,4},{24,8},{28,12},{1,17},{... | collective-permute-start | bytes 786440 | tf_op jit(solution)/shard_map/ppermute | solution.py:65
  38.5 14.5 %collective-permute-start.14 = (bf16[256,128]{1,0:T(8,128)(2,1)S(1)}, bf16[256,128]{1,0:T(8,128)(2,1)S(1)}, u32[]{:S(2)}, u32[]{:S(2)}) collective-permute-start(bf16[256,128]{1,0:T(8,128)(2,1)S(1)} %shard_map.308.m), channel_id=1, source_target_pairs={{0,16},{4,20},{8,24},{12,28},{16,0},{20,4},{24,8},{28,12},{1,17},{... | collective-permute-start | bytes 196616 | tf_op jit(solution)/shard_map/ppermute | solution.py:65
  55.2 28.0 %collective-permute-start.15 = (bf16[512,1024]{1,0:T(8,128)(2,1)S(1)}, bf16[512,1024]{1,0:T(8,128)(2,1)S(1)}, u32[]{:S(2)}, u32[]{:S(2)}) collective-permute-start(bf16[512,1024]{1,0:T(8,128)(2,1)S(1)} %shard_map.312.refs_0_.near_ref), channel_id=1, source_target_pairs={{0,4},{4,0},{8,12},{12,8},{16,20},{20,16},{24,28},{28,24},{1,5},{5... | collective-permute-start | bytes 3145736 | tf_op jit(solution)/shard_map/ppermute | solution.py:65
  56.8 13.6 %collective-permute-start.16 = (bf16[128,1024]{1,0:T(8,128)(2,1)S(1)}, bf16[128,1024]{1,0:T(8,128)(2,1)S(1)}, u32[]{:S(2)}, u32[]{:S(2)}) collective-permute-start(bf16[128,1024]{1,0:T(8,128)(2,1)S(1)} %bitcast.76), channel_id=1, source_target_pairs={{0,16},{4,20},{8,24},{12,28},{16,0},{20,4},{24,8},{28,12},{1,17},{... | collective-permute-start | bytes 786440 | tf_op jit(solution)/shard_map/ppermute | solution.py:65
  70.4 12.7 %collective-permute-start.17 = (bf16[256,1024]{1,0:T(8,128)(2,1)S(1)}, bf16[256,1024]{1,0:T(8,128)(2,1)S(1)}, u32[]{:S(2)}, u32[]{:S(2)}) collective-permute-start(bf16[256,1024]{1,0:T(8,128)(2,1)S(1)} %shard_map.316.m), channel_id=1, source_target_pairs={{0,8},{4,12},{8,0},{12,4},{16,24},{20,28},{24,16},{28,20},{1,9},{5... | collective-permute-start | bytes 1572872 | tf_op jit(solution)/shard_map/ppermute | solution.py:65
  71.0 21.7 %collective-permute-start.21 = (bf16[256,1024]{1,0:T(8,128)(2,1)S(1)}, bf16[256,1024]{1,0:T(8,128)(2,1)S(1)}, u32[]{:S(2)}, u32[]{:S(2)}) collective-permute-start(bf16[256,1024]{1,0:T(8,128)(2,1)S(1)} %shard_map.311.m), channel_id=1, source_target_pairs={{0,4},{4,0},{8,12},{12,8},{16,20},{20,16},{24,28},{28,24},{1,5},{5... | collective-permute-start | bytes 1572872 | tf_op jit(solution)/shard_map/ppermute | solution.py:65
  71.3 11.9 %collective-permute-start.18 = (bf16[512,256]{1,0:T(8,128)(2,1)S(1)}, bf16[512,256]{1,0:T(8,128)(2,1)S(1)}, u32[]{:S(2)}, u32[]{:S(2)}) collective-permute-start(bf16[512,256]{1,0:T(8,128)(2,1)S(1)} %shard_map.317.rest_0_), channel_id=1, source_target_pairs={{0,1},{1,0},{2,3},{3,2},{4,5},{5,4},{6,7},{7,6},{8,9},{9,8},{10,11... | collective-permute-start | bytes 786440 | tf_op jit(solution)/shard_map/ppermute | solution.py:65
  83.3 11.2 %collective-permute-start.26 = (bf16[512,256]{1,0:T(8,128)(2,1)S(1)}, bf16[512,256]{1,0:T(8,128)(2,1)S(1)}, u32[]{:S(2)}, u32[]{:S(2)}) collective-permute-start(bf16[512,256]{1,0:T(8,128)(2,1)S(1)} %shard_map.319.rest_4_), channel_id=1, source_target_pairs={{0,2},{1,3},{2,0},{3,1},{4,6},{5,7},{6,4},{7,5},{8,10},{9,11},{10,... | collective-permute-start | bytes 786440 | tf_op jit(solution)/shard_map/ppermute | solution.py:65
  86.4 11.6 %collective-permute-start.23 = (bf16[2,176,256]{2,1,0:T(8,128)(2,1)S(1)}, bf16[2,176,256]{2,1,0:T(8,128)(2,1)S(1)}, u32[]{:S(2)}, u32[]{:S(2)}) collective-permute-start(bf16[2,176,256]{2,1,0:T(8,128)(2,1)S(1)} %get-tuple-element.484), channel_id=1, source_target_pairs={{0,2},{1,3},{2,0},{3,1},{4,6},{5,7},{6,4},{7,5},{8,10},{9,11},{10,... | collective-permute-start | bytes 540680 | tf_op jit(solution)/shard_map/ppermute | solution.py:65
  88.5 24.7 %collective-permute-start.29 = (bf16[512,1024]{1,0:T(8,128)(2,1)S(1)}, bf16[512,1024]{1,0:T(8,128)(2,1)S(1)}, u32[]{:S(2)}, u32[]{:S(2)}) collective-permute-start(bf16[512,1024]{1,0:T(8,128)(2,1)S(1)} %shard_map.318.up_near), channel_id=1, source_target_pairs={{0,4},{4,0},{8,12},{12,8},{16,20},{20,16},{24,28},{28,24},{1,5},{5... | collective-permute-start | bytes 3145736 | tf_op jit(solution)/shard_map/ppermute | solution.py:65
  92.7 21.5 %collective-permute-start.30 = (bf16[512,1024]{1,0:T(8,128)(2,1)S(1)}, bf16[512,1024]{1,0:T(8,128)(2,1)S(1)}, u32[]{:S(2)}, u32[]{:S(2)}) collective-permute-start(bf16[512,1024]{1,0:T(8,128)(2,1)S(1)} %shard_map.321.down_near), channel_id=1, source_target_pairs={{0,8},{4,12},{8,0},{12,4},{16,24},{20,28},{24,16},{28,20},{1,9},{5... | collective-permute-start | bytes 3145736 | tf_op jit(solution)/shard_map/ppermute | solution.py:65
  102.2 10.5 %collective-permute-start.32 = (bf16[176,1024]{1,0:T(8,128)(2,1)S(1)}, bf16[176,1024]{1,0:T(8,128)(2,1)S(1)}, u32[]{:S(2)}, u32[]{:S(2)}) collective-permute-start(bf16[176,1024]{1,0:T(8,128)(2,1)S(1)} %get-tuple-element.525.x0), channel_id=1, source_target_pairs={{0,2},{1,3},{2,0},{3,1},{4,6},{5,7},{6,4},{7,5},{8,10},{9,11},{10,... | collective-permute-start | bytes 1081352 | tf_op jit(solution)/shard_map/ppermute | solution.py:65
  121.7 10.5 %collective-permute-start.35 = (bf16[176,1024]{1,0:T(8,128)(2,1)S(1)}, bf16[176,1024]{1,0:T(8,128)(2,1)S(1)}, u32[]{:S(2)}, u32[]{:S(2)}) collective-permute-start(bf16[176,1024]{1,0:T(8,128)(2,1)S(1)} %shard_map.328), channel_id=1, source_target_pairs={{0,2},{1,3},{2,0},{3,1},{4,6},{5,7},{6,4},{7,5},{8,10},{9,11},{10,... | collective-permute-start | bytes 1081352 | tf_op jit(solution)/shard_map/ppermute | solution.py:65
  149.0 10.6 %collective-permute-start.37 = (bf16[176,1024]{1,0:T(8,128)(2,1)S(1)}, bf16[176,1024]{1,0:T(8,128)(2,1)S(1)}, u32[]{:S(2)}, u32[]{:S(2)}) collective-permute-start(bf16[176,1024]{1,0:T(8,128)(2,1)S(1)} %get-tuple-element.575), channel_id=1, source_target_pairs={{0,1},{1,0},{2,3},{3,2},{4,5},{5,4},{6,7},{7,6},{8,9},{9,8},{10,11... | collective-permute-start | bytes 1081352 | tf_op jit(solution)/shard_map/ppermute | solution.py:65
  150.4 10.8 %collective-permute-start.41 = (bf16[176,1024]{1,0:T(8,128)(2,1)S(1)}, bf16[176,1024]{1,0:T(8,128)(2,1)S(1)}, u32[]{:S(2)}, u32[]{:S(2)}) collective-permute-start(bf16[176,1024]{1,0:T(8,128)(2,1)S(1)} %shard_map.332), channel_id=1, source_target_pairs={{0,2},{1,3},{2,0},{3,1},{4,6},{5,7},{6,4},{7,5},{8,10},{9,11},{10,... | collective-permute-start | bytes 1081352 | tf_op jit(solution)/shard_map/ppermute | solution.py:65
  155.3 25.7 %collective-permute-start.47 = (bf16[2,2,128,1024]{3,2,1,0:T(8,128)(2,1)S(1)}, bf16[2,2,128,1024]{3,2,1,0:T(8,128)(2,1)S(1)}, u32[]{:S(2)}, u32[]{:S(2)}) collective-permute-start(bf16[2,2,128,1024]{3,2,1,0:T(8,128)(2,1)S(1)} %bitcast.72), channel_id=1, source_target_pairs={{0,4},{4,0},{8,12},{12,8},{16,20},{20,16},{24,28},{28,24},{1,5},{5... | collective-permute-start | bytes 3145736 | tf_op jit(solution)/shard_map/ppermute | solution.py:65
  156.9 24.9 %collective-permute-start.46 = (bf16[2,2,128,1024]{3,2,1,0:T(8,128)(2,1)S(1)}, bf16[2,2,128,1024]{3,2,1,0:T(8,128)(2,1)S(1)}, u32[]{:S(2)}, u32[]{:S(2)}) collective-permute-start(bf16[2,2,128,1024]{3,2,1,0:T(8,128)(2,1)S(1)} %bitcast.71), channel_id=1, source_target_pairs={{0,8},{4,12},{8,0},{12,4},{16,24},{20,28},{24,16},{28,20},{1,9},{5... | collective-permute-start | bytes 3145736 | tf_op jit(solution)/shard_map/ppermute | solution.py:65
  179.1 20.4 %collective-permute-start.50 = (bf16[2,2,128,768]{3,2,1,0:T(8,128)(2,1)S(1)}, bf16[2,2,128,768]{3,2,1,0:T(8,128)(2,1)S(1)}, u32[]{:S(2)}, u32[]{:S(2)}) collective-permute-start(bf16[2,2,128,768]{3,2,1,0:T(8,128)(2,1)S(1)} %bitcast.74), channel_id=1, source_target_pairs={{0,4},{4,0},{8,12},{12,8},{16,20},{20,16},{24,28},{28,24},{1,5},{5... | collective-permute-start | bytes 2359304 | tf_op jit(solution)/shard_map/ppermute | solution.py:65
  180.7 14.3 %collective-permute-start.53 = (bf16[1024,256]{1,0:T(8,128)(2,1)S(1)}, bf16[1024,256]{1,0:T(8,128)(2,1)S(1)}, u32[]{:S(2)}, u32[]{:S(2)}) collective-permute-start(bf16[1024,256]{1,0:T(8,128)(2,1)S(1)} %shard_map.341), channel_id=1, source_target_pairs={{0,2},{1,3},{2,0},{3,1},{4,6},{5,7},{6,4},{7,5},{8,10},{9,11},{10,... | collective-permute-start | bytes 1572872 | tf_op jit(solution)/shard_map/ppermute | solution.py:65
  181.9 13.4 %collective-permute-start.51 = (bf16[2,128,1024]{2,1,0:T(8,128)(2,1)S(1)}, bf16[2,128,1024]{2,1,0:T(8,128)(2,1)S(1)}, u32[]{:S(2)}, u32[]{:S(2)}) collective-permute-start(bf16[2,128,1024]{2,1,0:T(8,128)(2,1)S(1)} %shard_map.344), channel_id=1, source_target_pairs={{0,8},{4,12},{8,0},{12,4},{16,24},{20,28},{24,16},{28,20},{1,9},{5... | collective-permute-start | bytes 1572872 | tf_op jit(solution)/shard_map/ppermute | solution.py:65
  183.8 32.0 %collective-permute-start.57 = (bf16[2,128,1024]{2,1,0:T(8,128)(2,1)S(1)}, bf16[2,128,1024]{2,1,0:T(8,128)(2,1)S(1)}, u32[]{:S(2)}, u32[]{:S(2)}) collective-permute-start(bf16[2,128,1024]{2,1,0:T(8,128)(2,1)S(1)} %shard_map.345), channel_id=1, source_target_pairs={{0,4},{4,0},{8,12},{12,8},{16,20},{20,16},{24,28},{28,24},{1,5},{5... | collective-permute-start | bytes 1572872 | tf_op jit(solution)/shard_map/ppermute | solution.py:65
  199.6 13.7 %collective-permute-start.54 = (bf16[2,128,768]{2,1,0:T(8,128)(2,1)S(1)}, bf16[2,128,768]{2,1,0:T(8,128)(2,1)S(1)}, u32[]{:S(2)}, u32[]{:S(2)}) collective-permute-start(bf16[2,128,768]{2,1,0:T(8,128)(2,1)S(1)} %shard_map.351), channel_id=1, source_target_pairs={{0,8},{4,12},{8,0},{12,4},{16,24},{20,28},{24,16},{28,20},{1,9},{5... | collective-permute-start | bytes 1179656 | tf_op jit(solution)/shard_map/ppermute | solution.py:65
  201.4 14.3 %collective-permute-start.49 = (bf16[176,1024]{1,0:T(8,128)(2,1)S(1)}, bf16[176,1024]{1,0:T(8,128)(2,1)S(1)}, u32[]{:S(2)}, u32[]{:S(2)}) collective-permute-start(bf16[176,1024]{1,0:T(8,128)(2,1)S(1)} %get-tuple-element.677), channel_id=1, source_target_pairs={{0,1},{1,0},{2,3},{3,2},{4,5},{5,4},{6,7},{7,6},{8,9},{9,8},{10,11... | collective-permute-start | bytes 1081352 | tf_op jit(solution)/shard_map/ppermute | solution.py:65
  201.4 17.2 %collective-permute-start.58 = (bf16[2,2,128,384]{3,2,1,0:T(8,128)(2,1)S(1)}, bf16[2,2,128,384]{3,2,1,0:T(8,128)(2,1)S(1)}, u32[]{:S(2)}, u32[]{:S(2)}) collective-permute-start(bf16[2,2,128,384]{3,2,1,0:T(8,128)(2,1)S(1)} %shard_map.349), channel_id=1, source_target_pairs={{0,4},{4,0},{8,12},{12,8},{16,20},{20,16},{24,28},{28,24},{1,5},{5... | collective-permute-start | bytes 1179656 | tf_op jit(solution)/shard_map/ppermute | solution.py:65
  202.9 19.9 %collective-permute-start.56 = (bf16[128,1024]{1,0:T(8,128)(2,1)S(1)}, bf16[128,1024]{1,0:T(8,128)(2,1)S(1)}, u32[]{:S(2)}, u32[]{:S(2)}) collective-permute-start(bf16[128,1024]{1,0:T(8,128)(2,1)S(1)} %shard_map.350), channel_id=1, source_target_pairs={{0,16},{4,20},{8,24},{12,28},{16,0},{20,4},{24,8},{28,12},{1,17},{... | collective-permute-start | bytes 786440 | tf_op jit(solution)/shard_map/ppermute | solution.py:65
  213.3 13.0 %collective-permute-start.59 = (bf16[128,768]{1,0:T(8,128)(2,1)S(1)}, bf16[128,768]{1,0:T(8,128)(2,1)S(1)}, u32[]{:S(2)}, u32[]{:S(2)}) collective-permute-start(bf16[128,768]{1,0:T(8,128)(2,1)S(1)} %shard_map.352), channel_id=1, source_target_pairs={{0,16},{4,20},{8,24},{12,28},{16,0},{20,4},{24,8},{28,12},{1,17},{... | collective-permute-start | bytes 589832 | tf_op jit(solution)/shard_map/ppermute | solution.py:65
  215.7 14.2 %collective-permute-start.48 = (bf16[176,1024]{1,0:T(8,128)(2,1)S(1)}, bf16[176,1024]{1,0:T(8,128)(2,1)S(1)}, u32[]{:S(2)}, u32[]{:S(2)}) collective-permute-start(bf16[176,1024]{1,0:T(8,128)(2,1)S(1)} %get-tuple-element.675), channel_id=1, source_target_pairs={{0,1},{1,0},{2,3},{3,2},{4,5},{5,4},{6,7},{7,6},{8,9},{9,8},{10,11... | collective-permute-start | bytes 1081352 | tf_op jit(solution)/shard_map/ppermute | solution.py:65
  215.8 14.1 %collective-permute-start.55 = (bf16[176,1024]{1,0:T(8,128)(2,1)S(1)}, bf16[176,1024]{1,0:T(8,128)(2,1)S(1)}, u32[]{:S(2)}, u32[]{:S(2)}) collective-permute-start(bf16[176,1024]{1,0:T(8,128)(2,1)S(1)} %shard_map.353), channel_id=1, source_target_pairs={{0,2},{1,3},{2,0},{3,1},{4,6},{5,7},{6,4},{7,5},{8,10},{9,11},{10,... | collective-permute-start | bytes 1081352 | tf_op jit(solution)/shard_map/ppermute | solution.py:65
  227.4 17.9 %collective-permute-start.61 = (bf16[128,1024]{1,0:T(8,128)(2,1)S(1)}, bf16[128,1024]{1,0:T(8,128)(2,1)S(1)}, u32[]{:S(2)}, u32[]{:S(2)}) collective-permute-start(bf16[128,1024]{1,0:T(8,128)(2,1)S(1)} %shard_map.355), channel_id=1, source_target_pairs={{0,16},{4,20},{8,24},{12,28},{16,0},{20,4},{24,8},{28,12},{1,17},{... | collective-permute-start | bytes 786440 | tf_op jit(solution)/shard_map/ppermute | solution.py:65
  (52 other events, 381.4 us)

commit v3 on v2

--- a/solution.py
+++ b/solution.py
@@ -414,7 +414,7 @@
 def softmax_rows(q, k, bias):
     s = dot_nt(q, k) * 0.125 + bias
     e = jnp.exp(s - jnp.max(s, axis=-1, keepdims=True))
-    return e / jnp.sum(e, axis=-1, keepdims=True)
+    return e * (1.0 / jnp.sum(e, axis=-1, keepdims=True))
 
 
 def attend_kernel(heads, pair, at_ref, d0, d1, near_ref, far_ref, add_ref, bias_ref, *rest):
@@ -496,9 +496,16 @@
         out_ref[:, at] = dot_tn(left, right_ref[:, at]).astype(bf16)
 
 
-def normal_parts(u):
-    density = jnp.exp(-0.5 * u * u)
-    return 0.5 + 0.5 * lax.erf(u * (0.5**0.5)), u * density * ((2 * jnp.pi) ** -0.5)
+def normal_below(u):
+    return 0.5 + 0.5 * lax.erf(u * (0.5**0.5))
+
+
+def slope_kernel(pre_ref, slope_ref):
+    for n in range(pre_ref.shape[1] // TILE):
+        at = slice(n * TILE, (n + 1) * TILE)
+        u = pre_ref[:, at]
+        density = jnp.exp(-0.5 * u * u) * ((2 * jnp.pi) ** -0.5)
+        slope_ref[:, at] = normal_below(u) + u * density
 
 
 TILE = 256
@@ -513,9 +520,8 @@
         at = slice(n * TILE, (n + 1) * TILE)
         pre = dot_nn(group_ref[both, : D // 2], up_near[:, at])
         pre = pre + dot_nn(group_ref[both, D // 2 :], up_far[:, at]) + add_ref[:, at]
-        below, tilt = normal_parts(pre)
-        slope_ref[both, at] = below + tilt
-        act_ref[both, at] = (pre * below).astype(bf16)
+        slope_ref[both, at] = pre
+        act_ref[both, at] = (pre * normal_below(pre)).astype(bf16)
     parts_back(act_ref[both, :], down_near, down_far, (keep_ref, give_ref), at_ref[1], X_Z)
 
 
@@ -589,7 +595,8 @@
 
 
 def attend_back_kernel(heads, pair, last, qkv_ref, probs_ref, g0, g1, notes_ref, *rest):
-    dqkv_ref, sums_ref, grid_ref = rest[-4:-1] if last else rest[-3:]
+    ds_ref, wide_ref = rest[-2:]
+    dqkv_ref, sums_ref, grid_ref = rest[-6:-3] if last else rest[-5:-2]
     width = heads * HD
     for j, grad_ref in zip(pair, (g0.at[0] if last else g0, g1)):
         notes = notes_ref[j].astype(f32)
@@ -603,24 +610,28 @@
             p = probs_ref[j, h]
             dp = dot_nt(g, v)
             ds = (p * (dp - jnp.sum(p * dp, axis=-1, keepdims=True))).astype(bf16)
+            ds_ref[doc_at(h), :] = ds
             dq = (dot_nn(ds, k) * 0.125).astype(bf16)
             dk = (dot_tn(ds, q) * 0.125).astype(bf16)
             dv = dot_tn(p.astype(bf16), g).astype(bf16)
             for c, d in enumerate((dq, dk, dv)):
                 at = slice(c * width + h * HD, c * width + (h + 1) * HD)
                 dqkv_ref[doc_at(j), at] = d
-            part = dot_nt(ds, hots).astype(bf16)
-            for n in range(3):
-                term = dot_nn(flipped[n], part[:, n * NB : (n + 1) * NB])
-                if j == 0:
-                    grid_ref[n * heads + h] = term
-                else:
-                    grid_ref[n * heads + h] += term
+        part = dot_nt(ds_ref[...], hots).astype(bf16)
+        for n in range(3):
+            for h in range(heads):
+                wide_ref[:, h * NB : (h + 1) * NB] = part[doc_at(h), n * NB : (n + 1) * NB]
+            term = dot_nn(flipped[n], wide_ref[...])
+            if j == 0:
+                grid_ref[n] = term
+            else:
+                grid_ref[n] += term
         sums_ref[j : j + 1, :] = jnp.sum(dqkv_ref[doc_at(j), :].astype(f32), axis=0, keepdims=True)
     if last:
-        ext_ref = rest[-1]
+        ext_ref = rest[-3]
         for n in range(3 * heads):
-            wide = jnp.concatenate([grid_ref[n], jnp.zeros((NB, NB), f32)], axis=1)
+            block = grid_ref[n // heads, :, (n % heads) * NB : (n % heads + 1) * NB]
+            wide = jnp.concatenate([block, jnp.zeros((NB, NB), f32)], axis=1)
             skew = pltpu.roll(wide, 1, 1, stride=1, stride_axis=0)
             ext_ref[n : n + 1, :] = jnp.sum(skew, axis=0, keepdims=True)
 
@@ -903,6 +914,7 @@
         at, *normed_pieces[2:], *ffn_weights, my_upb, normed_group, slope, act_low,
     )
     meet.far_pair(keep, give).send()
+    (slope,) = run(lambda *ins: call(slope_kernel, ins, [hid_f]), slope)
     encoded, d_ffn, d_resid_two, sums_two = run(
         lambda *ins: call(
             second_norm_kernel, ins,
@@ -962,11 +974,12 @@
         at, attended, d_branch,
     )
     meet_proj = Meet().near_pair(parts[0], parts[1]).far_pair(parts[2], parts[3])
-    grids = shape_of((3 * heads, NB, NB), f32)
+    grids = shape_of((3, NB, heads * NB), f32)
+    room = [pltpu.VMEM((heads * ROWS, ROWS), bf16), pltpu.VMEM((ROWS, heads * NB), bf16)]
     d_qkv, d_sums, d_grid = run(
         lambda *ins: call(
             partial(attend_back_kernel, heads, (0, 1), False), ins,
-            [qkv_out, shape_of((tp, 3 * width), f32), grids], cost=10,
+            [qkv_out, shape_of((tp, 3 * width), f32), grids], room, cost=10,
         ),
         qkv, probs, a0, got_c, notes,
     )
@@ -976,6 +989,7 @@
         lambda *ins: call(
             partial(attend_back_kernel, heads, (2, 3), True), ins,
             [qkv_out, shape_of((tp, 3 * width), f32), grids, shape_of((3 * heads, 2 * NB), f32)],
+            room,
             alias={5: 0, 6: 1, 7: 2},
         ),
         qkv, probs, far, got_far, notes, d_qkv, d_sums, d_grid,

time: 264 us -> 261 us (0.989)
  waiting for transfers between devices: 138 us -> 135 us
    ppermute x67, waiting for transfers between devices: 138 us -> 135 us  [swap(): lax.ppermute(x, axis, [(i, i ^ b) for i in range(lax.axis_size(axis))])]
    pallas_call x69 -> x70, Pallas kernels: 56 us -> 54.3 us  [call(): pl.pallas_call(kernel, in_specs=[pl.BlockSpec(memory_space=m) for m in sp...]
  transfers between devices with their start and end apart: 67 -> 67, of which waited for: 35 -> 36; matrix products, arithmetic and copies ran while one was open for 1% -> 1% of each run, Pallas kernels for 19% -> 19%
where the time goes in v3:
time: 261 us; the launch traced here: 258 us
  waiting for transfers between devices  135 us (52%)
  Pallas kernels  58.3 us (22%)
  starting transfers between devices  55.6 us (21%)
  local copies, waits for them, and re-layouts  5.66 us (2%)
  between operations  2.62 us (1%)
    ppermute x67, waiting for transfers between devices, swap(): lax.ppermute(x, axis, [(i, i ^ b) for i in range(lax.axis_size(axis))])  135 us
    ppermute x67, starting transfers between devices, swap(): lax.ppermute(x, axis, [(i, i ^ b) for i in range(lax.axis_size(axis))])  55.6 us
    pallas_call x70, Pallas kernels, call(): pl.pallas_call(kernel, in_specs=[pl.BlockSpec(memory_space=m) for m in sp...  54.3 us
    unnamed x35, local copies, waits for them, and re-layouts  5.29 us
  transfers between devices with their start and end apart: 67, of which 36 were waited for; matrix products, arithmetic and copies ran while one was open for 1% of the time, Pallas kernels for 19%

profile of v3, /device:TPU:0, one launch (start us, length us, event | category | flops | bytes accessed | tf_op | source)
XLA Modules:
  0.0 258.4 jit_solution(8483804524279303227)
XLA Ops:
  7.6 3.0 %collective-permute-start.3 = (bf16[2,32,1024]{2,1,0:T(8,128)(2,1)S(1)}, bf16[2,32,1024]{2,1,0:T(8,128)(2,1)S(1)}, u32[]{:S(2)}, u32[]{:S(2)}) collective-permute-start(bf16[2,32,1024]{2,1,0:T(8,128)(2,1)S(1)} %get-tuple-element.405), channel_id=1, source_target_pairs={{0,2},{1,3},{2,0},{3,1},{4,6},{5,7},{6,4},{7,5},{8,10},{9,11},{10,... | collective-permute-start | bytes 393224 | tf_op jit(solution)/shard_map/ppermute | solution.py:65
  11.9 2.4 collective-permute-done.3.other
  18.5 2.7 %collective-permute-start.5 = (bf16[128,1024]{1,0:T(8,128)(2,1)S(1)}, bf16[128,1024]{1,0:T(8,128)(2,1)S(1)}, u32[]{:S(2)}, u32[]{:S(2)}) collective-permute-start(bf16[128,1024]{1,0:T(8,128)(2,1)S(1)} %bitcast.69), channel_id=1, source_target_pairs={{0,16},{4,20},{8,24},{12,28},{16,0},{20,4},{24,8},{28,12},{1,17},{... | collective-permute-start | bytes 786440 | tf_op jit(solution)/shard_map/ppermute | solution.py:65
  21.7 3.1 %collective-permute-done.6.o = bf16[32,128]{1,0:T(8,128)(2,1)S(1)} collective-permute-done((bf16[32,128]{1,0:T(8,128)(2,1)S(1)}, bf16[32,128]{1,0:T(8,128)(2,1)S(1)}, u32[]{:S(2)}, u32[]{:S(2)}) %collective-permute-start.6) | collective-permute-done | bytes 8224 | tf_op jit(solution)/shard_map/ppermute | solution.py:65
  30.6 3.5 %collective-permute-done.9.o = bf16[128,128]{1,0:T(8,128)(2,1)S(1)} collective-permute-done((bf16[128,128]{1,0:T(8,128)(2,1)S(1)}, bf16[128,128]{1,0:T(8,128)(2,1)S(1)}, u32[]{:S(2)}, u32[]{:S(2)}) %collective-permute-start.9) | collective-permute-done | bytes 32800 | tf_op jit(solution)/shard_map/ppermute | solution.py:65
  35.2 3.3 %collective-permute-start.11 = (bf16[128,1024]{1,0:T(8,128)(2,1)S(1)}, bf16[128,1024]{1,0:T(8,128)(2,1)S(1)}, u32[]{:S(2)}, u32[]{:S(2)}) collective-permute-start(bf16[128,1024]{1,0:T(8,128)(2,1)S(1)} %bitcast.78), channel_id=1, source_target_pairs={{0,16},{4,20},{8,24},{12,28},{16,0},{20,4},{24,8},{28,12},{1,17},{... | collective-permute-start | bytes 786440 | tf_op jit(solution)/shard_map/ppermute | solution.py:65
  38.5 14.4 %collective-permute-done.14.o = bf16[256,128]{1,0:T(8,128)(2,1)S(1)} collective-permute-done((bf16[256,128]{1,0:T(8,128)(2,1)S(1)}, bf16[256,128]{1,0:T(8,128)(2,1)S(1)}, u32[]{:S(2)}, u32[]{:S(2)}) %collective-permute-start.14) | collective-permute-done | bytes 65568 | tf_op jit(solution)/shard_map/ppermute | solution.py:65
  58.9 4.1 %shard_map.315.bias_ref = f32[4,4,176,176]{3,2,1,0:T(8,128)S(1)} custom-call(bf16[4,16,256]{2,1,0:T(8,128)(2,1)S(1)} %shard_map.310.notes_ref, f32[12,256]{1,0:T(8,128)S(1)} %get-tuple-element.467.ext_ref), custom_call_target="tpu_custom_call" | custom-call | tf_op jit(solution)/shard_map/pallas_call | solution.py:243
  62.9 7.5 %collective-permute-done.16.o = bf16[128,1024]{1,0:T(8,128)(2,1)S(1)} collective-permute-done((bf16[128,1024]{1,0:T(8,128)(2,1)S(1)}, bf16[128,1024]{1,0:T(8,128)(2,1)S(1)}, u32[]{:S(2)}, u32[]{:S(2)}) %collective-permute-start.16) | collective-permute-done | bytes 262176 | tf_op jit(solution)/shard_map/ppermute | solution.py:65
  71.3 6.4 %collective-permute-done.19.rest_2_ = bf16[512,256]{1,0:T(8,128)(2,1)S(1)} collective-permute-done((bf16[512,256]{1,0:T(8,128)(2,1)S(1)}, bf16[512,256]{1,0:T(8,128)(2,1)S(1)}, u32[]{:S(2)}, u32[]{:S(2)}) %collective-permute-start.19) | collective-permute-done | bytes 262176 | tf_op jit(solution)/shard_map/ppermute | solution.py:65
  77.8 5.4 %collective-permute-done.17.o = bf16[256,1024]{1,0:T(8,128)(2,1)S(1)} collective-permute-done((bf16[256,1024]{1,0:T(8,128)(2,1)S(1)}, bf16[256,1024]{1,0:T(8,128)(2,1)S(1)}, u32[]{:S(2)}, u32[]{:S(2)}) %collective-permute-start.17) | collective-permute-done | bytes 524320 | tf_op jit(solution)/shard_map/ppermute | solution.py:65
  83.4 3.1 %shard_map.320 = (bf16[704,1024]{1,0:T(8,128)(2,1)S(1)}, bf16[704,768]{1,0:T(8,128)(2,1)S(1)}, f32[4,4,176,176]{3,2,1,0:T(8,128)S(1)}, bf16[2,176,256]{2,1,0:T(8,128)(2,1)S(1)}) custom-call(s32[2]{0:T(128)S(1)} %pad_add_fusion.at.at_ref, bf16[176,1024]{1,0:T(8,128)(2,1)S(1)} %collective-permute-done.12.refs_2_.d0, ...), custom_call_target="tpu_custom_call" | custom-call | tf_op jit(solution)/shard_map/pallas_call | solution.py:31
  89.1 3.6 %collective-permute-done.21.o = bf16[256,1024]{1,0:T(8,128)(2,1)S(1)} collective-permute-done((bf16[256,1024]{1,0:T(8,128)(2,1)S(1)}, bf16[256,1024]{1,0:T(8,128)(2,1)S(1)}, u32[]{:S(2)}, u32[]{:S(2)}) %collective-permute-start.21) | collective-permute-done | bytes 524320 | tf_op jit(solution)/shard_map/ppermute | solution.py:65
  95.0 3.1 %shard_map.322 = (bf16[704,1024]{1,0:T(8,128)(2,1)S(1)}, bf16[704,768]{1,0:T(8,128)(2,1)S(1)}, f32[4,4,176,176]{3,2,1,0:T(8,128)S(1)}, bf16[2,176,256]{2,1,0:T(8,128)(2,1)S(1)}) custom-call(s32[2]{0:T(128)S(1)} %pad_add_fusion.at.at_ref, ...), custom_call_target="tpu_custom_call", output_to_operand_aliasing={{0}: (7, {}), {1}: (8, {}), {2}: (9, {})} | custom-call | tf_op jit(solution)/shard_map/pallas_call | solution.py:31
  103.4 9.3 %collective-permute-done.32.x0 = bf16[176,1024]{1,0:T(8,128)(2,1)S(1)} collective-permute-done((bf16[176,1024]{1,0:T(8,128)(2,1)S(1)}, bf16[176,1024]{1,0:T(8,128)(2,1)S(1)}, u32[]{:S(2)}, u32[]{:S(2)}) %collective-permute-start.32) | collective-permute-done | bytes 360480 | tf_op jit(solution)/shard_map/ppermute | solution.py:65
  114.2 2.5 shard_map.326
  116.7 2.5 shard_map.327
  123.9 7.7 %collective-permute-done.35.got_y = bf16[176,1024]{1,0:T(8,128)(2,1)S(1)} collective-permute-done((bf16[176,1024]{1,0:T(8,128)(2,1)S(1)}, bf16[176,1024]{1,0:T(8,128)(2,1)S(1)}, u32[]{:S(2)}, u32[]{:S(2)}) %collective-permute-start.35) | collective-permute-done | bytes 360480 | tf_op jit(solution)/shard_map/ppermute | solution.py:65
  134.8 7.9 %collective-permute-done.38.g0 = bf16[176,1024]{1,0:T(8,128)(2,1)S(1)} collective-permute-done((bf16[176,1024]{1,0:T(8,128)(2,1)S(1)}, bf16[176,1024]{1,0:T(8,128)(2,1)S(1)}, u32[]{:S(2)}, u32[]{:S(2)}) %collective-permute-start.38) | collective-permute-done | bytes 360480 | tf_op jit(solution)/shard_map/ppermute | solution.py:65
  142.7 2.6 shard_map.331
  145.3 2.4 shard_map.332
  165.8 4.0 %shard_map.340 = (bf16[704,768]{1,0:T(8,128)(2,1)S(1)}, f32[4,768]{1,0:T(4,128)S(1)}, f32[3,128,512]{2,1,0:T(8,128)S(1)}) custom-call(bf16[704,768]{1,0:T(8,128)(2,1)S(1)} %get-tuple-element.647.qkv_ref, f32[4,4,176,176]{3,2,1,0:T(8,128)S(1)} %get-tuple-element.648.probs_ref, bf16[176,256]{1,0:T(8,128)(2,1)S(1)} %get-tuple-element.638.g0, ...), custom_call_target="tpu_custom_call" | custom-call | flops 10000000000 | tf_op jit(solution)/shard_map/pallas_call | solution.py:31
  171.1 4.4 %shard_map.343 = (bf16[704,768]{1,0:T(8,128)(2,1)S(1)}, f32[4,768]{1,0:T(4,128)S(1)}, f32[3,128,512]{2,1,0:T(8,128)S(1)}, f32[12,256]{1,0:T(8,128)S(1)}) custom-call(bf16[704,768]{1,0:T(8,128)(2,1)S(1)} %get-tuple-element.647.qkv_ref, ...), custom_call_target="tpu_custom_call", output_to_operand_aliasing={{0}: (5, {}), {1}: (6, {}), {2}: (7, {})} | custom-call | tf_op jit(solution)/shard_map/pallas_call | solution.py:31
  184.4 2.7 %shard_map.348 = bf16[1024,128]{1,0:T(8,128)(2,1)S(1)} custom-call(s32[2]{0:T(128)S(1)} %pad_add_fusion.at.at_ref, f32[12,256]{1,0:T(8,128)S(1)} %get-tuple-element.667.ext_ref, f32[4,768]{1,0:T(4,128)S(1)} %get-tuple-element.668.sums_ref, f32[2,1024]{1,0:T(2,128)S(1)} %get-tuple-element.669.up_ref, f32[3,1024]{1,0:T(4,128)S(1)} %get-tuple-element.670.one_ref, ...), custom_call_target="tpu_custom_call" | custom-call | tf_op jit(solution)/shard_map/pallas_call | solution.py:31
  189.1 3.1 %collective-permute-done.53 = bf16[1024,256]{1,0:T(8,128)(2,1)S(1)} collective-permute-done((bf16[1024,256]{1,0:T(8,128)(2,1)S(1)}, bf16[1024,256]{1,0:T(8,128)(2,1)S(1)}, u32[]{:S(2)}, u32[]{:S(2)}) %collective-permute-start.53) | collective-permute-done | bytes 524320 | tf_op jit(solution)/shard_map/ppermute | solution.py:65
  193.9 2.9 %collective-permute-done.50.refs_1_ = bf16[2,2,128,768]{3,2,1,0:T(8,128)(2,1)S(1)} collective-permute-done((bf16[2,2,128,768]{3,2,1,0:T(8,128)(2,1)S(1)}, bf16[2,2,128,768]{3,2,1,0:T(8,128)(2,1)S(1)}, u32[]{:S(2)}, u32[]{:S(2)}) %collective-permute-start.50) | collective-permute-done | bytes 786464 | tf_op jit(solution)/shard_map/ppermute | solution.py:65
  201.3 10.3 %collective-permute-done.54.refs_2_ = bf16[2,128,768]{2,1,0:T(8,128)(2,1)S(1)} collective-permute-done((bf16[2,128,768]{2,1,0:T(8,128)(2,1)S(1)}, bf16[2,128,768]{2,1,0:T(8,128)(2,1)S(1)}, u32[]{:S(2)}, u32[]{:S(2)}) %collective-permute-start.54) | collective-permute-done | bytes 393248 | tf_op jit(solution)/shard_map/ppermute | solution.py:65
  216.2 4.0 %collective-permute-done.56.refs_3_ = bf16[128,1024]{1,0:T(8,128)(2,1)S(1)} collective-permute-done((bf16[128,1024]{1,0:T(8,128)(2,1)S(1)}, bf16[128,1024]{1,0:T(8,128)(2,1)S(1)}, u32[]{:S(2)}, u32[]{:S(2)}) %collective-permute-start.56) | collective-permute-done | bytes 262176 | tf_op jit(solution)/shard_map/ppermute | solution.py:65
  220.2 3.5 %collective-permute-done.59.refs_3_ = bf16[128,768]{1,0:T(8,128)(2,1)S(1)} collective-permute-done((bf16[128,768]{1,0:T(8,128)(2,1)S(1)}, bf16[128,768]{1,0:T(8,128)(2,1)S(1)}, u32[]{:S(2)}, u32[]{:S(2)}) %collective-permute-start.59) | collective-permute-done | bytes 196640 | tf_op jit(solution)/shard_map/ppermute | solution.py:65
  228.3 6.8 %collective-permute-done.62.refs_5_ = bf16[2,128,384]{2,1,0:T(8,128)(2,1)S(1)} collective-permute-done((bf16[2,128,384]{2,1,0:T(8,128)(2,1)S(1)}, bf16[2,128,384]{2,1,0:T(8,128)(2,1)S(1)}, u32[]{:S(2)}, u32[]{:S(2)}) %collective-permute-start.62) | collective-permute-done | bytes 196640 | tf_op jit(solution)/shard_map/ppermute | solution.py:65
  235.6 7.0 %collective-permute-done.61.refs_3_ = bf16[128,1024]{1,0:T(8,128)(2,1)S(1)} collective-permute-done((bf16[128,1024]{1,0:T(8,128)(2,1)S(1)}, bf16[128,1024]{1,0:T(8,128)(2,1)S(1)}, u32[]{:S(2)}, u32[]{:S(2)}) %collective-permute-start.61) | collective-permute-done | bytes 262176 | tf_op jit(solution)/shard_map/ppermute | solution.py:65
  251.6 4.5 %collective-permute-done.66.other = bf16[2,32,2176]{2,1,0:T(8,128)(2,1)S(1)} collective-permute-done((bf16[2,32,2176]{2,1,0:T(8,128)(2,1)S(1)}, bf16[2,32,2176]{2,1,0:T(8,128)(2,1)S(1)}, u32[]{:S(2)}, u32[]{:S(2)}) %collective-permute-start.66) | collective-permute-done | bytes 278560 | tf_op jit(solution)/shard_map/ppermute | solution.py:65
  (225 shorter events, 102.4 us)
Async XLA Ops:
  18.5 15.7 %collective-permute-start.5 = (bf16[128,1024]{1,0:T(8,128)(2,1)S(1)}, bf16[128,1024]{1,0:T(8,128)(2,1)S(1)}, u32[]{:S(2)}, u32[]{:S(2)}) collective-permute-start(bf16[128,1024]{1,0:T(8,128)(2,1)S(1)} %bitcast.69), channel_id=1, source_target_pairs={{0,16},{4,20},{8,24},{12,28},{16,0},{20,4},{24,8},{28,12},{1,17},{... | collective-permute-start | bytes 786440 | tf_op jit(solution)/shard_map/ppermute | solution.py:65
  34.2 20.9 %collective-permute-start.10 = (bf16[256,1024]{1,0:T(8,128)(2,1)S(1)}, bf16[256,1024]{1,0:T(8,128)(2,1)S(1)}, u32[]{:S(2)}, u32[]{:S(2)}) collective-permute-start(bf16[256,1024]{1,0:T(8,128)(2,1)S(1)} %shard_map.309.m), channel_id=1, source_target_pairs={{0,8},{4,12},{8,0},{12,4},{16,24},{20,28},{24,16},{28,20},{1,9},{5... | collective-permute-start | bytes 1572872 | tf_op jit(solution)/shard_map/ppermute | solution.py:65
  35.2 17.8 %collective-permute-start.11 = (bf16[128,1024]{1,0:T(8,128)(2,1)S(1)}, bf16[128,1024]{1,0:T(8,128)(2,1)S(1)}, u32[]{:S(2)}, u32[]{:S(2)}) collective-permute-start(bf16[128,1024]{1,0:T(8,128)(2,1)S(1)} %bitcast.78), channel_id=1, source_target_pairs={{0,16},{4,20},{8,24},{12,28},{16,0},{20,4},{24,8},{28,12},{1,17},{... | collective-permute-start | bytes 786440 | tf_op jit(solution)/shard_map/ppermute | solution.py:65
  38.5 14.5 %collective-permute-start.14 = (bf16[256,128]{1,0:T(8,128)(2,1)S(1)}, bf16[256,128]{1,0:T(8,128)(2,1)S(1)}, u32[]{:S(2)}, u32[]{:S(2)}) collective-permute-start(bf16[256,128]{1,0:T(8,128)(2,1)S(1)} %shard_map.308.m), channel_id=1, source_target_pairs={{0,16},{4,20},{8,24},{12,28},{16,0},{20,4},{24,8},{28,12},{1,17},{... | collective-permute-start | bytes 196616 | tf_op jit(solution)/shard_map/ppermute | solution.py:65
  55.2 28.0 %collective-permute-start.15 = (bf16[512,1024]{1,0:T(8,128)(2,1)S(1)}, bf16[512,1024]{1,0:T(8,128)(2,1)S(1)}, u32[]{:S(2)}, u32[]{:S(2)}) collective-permute-start(bf16[512,1024]{1,0:T(8,128)(2,1)S(1)} %shard_map.312.refs_0_.near_ref), channel_id=1, source_target_pairs={{0,4},{4,0},{8,12},{12,8},{16,20},{20,16},{24,28},{28,24},{1,5},{5... | collective-permute-start | bytes 3145736 | tf_op jit(solution)/shard_map/ppermute | solution.py:65
  56.8 13.6 %collective-permute-start.16 = (bf16[128,1024]{1,0:T(8,128)(2,1)S(1)}, bf16[128,1024]{1,0:T(8,128)(2,1)S(1)}, u32[]{:S(2)}, u32[]{:S(2)}) collective-permute-start(bf16[128,1024]{1,0:T(8,128)(2,1)S(1)} %bitcast.76), channel_id=1, source_target_pairs={{0,16},{4,20},{8,24},{12,28},{16,0},{20,4},{24,8},{28,12},{1,17},{... | collective-permute-start | bytes 786440 | tf_op jit(solution)/shard_map/ppermute | solution.py:65
  70.4 12.7 %collective-permute-start.17 = (bf16[256,1024]{1,0:T(8,128)(2,1)S(1)}, bf16[256,1024]{1,0:T(8,128)(2,1)S(1)}, u32[]{:S(2)}, u32[]{:S(2)}) collective-permute-start(bf16[256,1024]{1,0:T(8,128)(2,1)S(1)} %shard_map.316.m), channel_id=1, source_target_pairs={{0,8},{4,12},{8,0},{12,4},{16,24},{20,28},{24,16},{28,20},{1,9},{5... | collective-permute-start | bytes 1572872 | tf_op jit(solution)/shard_map/ppermute | solution.py:65
  71.0 21.7 %collective-permute-start.21 = (bf16[256,1024]{1,0:T(8,128)(2,1)S(1)}, bf16[256,1024]{1,0:T(8,128)(2,1)S(1)}, u32[]{:S(2)}, u32[]{:S(2)}) collective-permute-start(bf16[256,1024]{1,0:T(8,128)(2,1)S(1)} %shard_map.311.m), channel_id=1, source_target_pairs={{0,4},{4,0},{8,12},{12,8},{16,20},{20,16},{24,28},{28,24},{1,5},{5... | collective-permute-start | bytes 1572872 | tf_op jit(solution)/shard_map/ppermute | solution.py:65
  71.3 11.9 %collective-permute-start.18 = (bf16[512,256]{1,0:T(8,128)(2,1)S(1)}, bf16[512,256]{1,0:T(8,128)(2,1)S(1)}, u32[]{:S(2)}, u32[]{:S(2)}) collective-permute-start(bf16[512,256]{1,0:T(8,128)(2,1)S(1)} %shard_map.317.rest_0_), channel_id=1, source_target_pairs={{0,1},{1,0},{2,3},{3,2},{4,5},{5,4},{6,7},{7,6},{8,9},{9,8},{10,11... | collective-permute-start | bytes 786440 | tf_op jit(solution)/shard_map/ppermute | solution.py:65
  83.3 11.2 %collective-permute-start.26 = (bf16[512,256]{1,0:T(8,128)(2,1)S(1)}, bf16[512,256]{1,0:T(8,128)(2,1)S(1)}, u32[]{:S(2)}, u32[]{:S(2)}) collective-permute-start(bf16[512,256]{1,0:T(8,128)(2,1)S(1)} %shard_map.319.rest_4_), channel_id=1, source_target_pairs={{0,2},{1,3},{2,0},{3,1},{4,6},{5,7},{6,4},{7,5},{8,10},{9,11},{10,... | collective-permute-start | bytes 786440 | tf_op jit(solution)/shard_map/ppermute | solution.py:65
  86.5 11.6 %collective-permute-start.23 = (bf16[2,176,256]{2,1,0:T(8,128)(2,1)S(1)}, bf16[2,176,256]{2,1,0:T(8,128)(2,1)S(1)}, u32[]{:S(2)}, u32[]{:S(2)}) collective-permute-start(bf16[2,176,256]{2,1,0:T(8,128)(2,1)S(1)} %get-tuple-element.485), channel_id=1, source_target_pairs={{0,2},{1,3},{2,0},{3,1},{4,6},{5,7},{6,4},{7,5},{8,10},{9,11},{10,... | collective-permute-start | bytes 540680 | tf_op jit(solution)/shard_map/ppermute | solution.py:65
  88.5 24.7 %collective-permute-start.29 = (bf16[512,1024]{1,0:T(8,128)(2,1)S(1)}, bf16[512,1024]{1,0:T(8,128)(2,1)S(1)}, u32[]{:S(2)}, u32[]{:S(2)}) collective-permute-start(bf16[512,1024]{1,0:T(8,128)(2,1)S(1)} %shard_map.318.up_near), channel_id=1, source_target_pairs={{0,4},{4,0},{8,12},{12,8},{16,20},{20,16},{24,28},{28,24},{1,5},{5... | collective-permute-start | bytes 3145736 | tf_op jit(solution)/shard_map/ppermute | solution.py:65
  92.7 21.5 %collective-permute-start.30 = (bf16[512,1024]{1,0:T(8,128)(2,1)S(1)}, bf16[512,1024]{1,0:T(8,128)(2,1)S(1)}, u32[]{:S(2)}, u32[]{:S(2)}) collective-permute-start(bf16[512,1024]{1,0:T(8,128)(2,1)S(1)} %shard_map.321.down_near), channel_id=1, source_target_pairs={{0,8},{4,12},{8,0},{12,4},{16,24},{20,28},{24,16},{28,20},{1,9},{5... | collective-permute-start | bytes 3145736 | tf_op jit(solution)/shard_map/ppermute | solution.py:65
  102.2 10.5 %collective-permute-start.32 = (bf16[176,1024]{1,0:T(8,128)(2,1)S(1)}, bf16[176,1024]{1,0:T(8,128)(2,1)S(1)}, u32[]{:S(2)}, u32[]{:S(2)}) collective-permute-start(bf16[176,1024]{1,0:T(8,128)(2,1)S(1)} %get-tuple-element.526.x0), channel_id=1, source_target_pairs={{0,2},{1,3},{2,0},{3,1},{4,6},{5,7},{6,4},{7,5},{8,10},{9,11},{10,... | collective-permute-start | bytes 1081352 | tf_op jit(solution)/shard_map/ppermute | solution.py:65
  121.1 10.6 %collective-permute-start.35 = (bf16[176,1024]{1,0:T(8,128)(2,1)S(1)}, bf16[176,1024]{1,0:T(8,128)(2,1)S(1)}, u32[]{:S(2)}, u32[]{:S(2)}) collective-permute-start(bf16[176,1024]{1,0:T(8,128)(2,1)S(1)} %shard_map.328), channel_id=1, source_target_pairs={{0,2},{1,3},{2,0},{3,1},{4,6},{5,7},{6,4},{7,5},{8,10},{9,11},{10,... | collective-permute-start | bytes 1081352 | tf_op jit(solution)/shard_map/ppermute | solution.py:65
  148.2 10.6 %collective-permute-start.37 = (bf16[176,1024]{1,0:T(8,128)(2,1)S(1)}, bf16[176,1024]{1,0:T(8,128)(2,1)S(1)}, u32[]{:S(2)}, u32[]{:S(2)}) collective-permute-start(bf16[176,1024]{1,0:T(8,128)(2,1)S(1)} %get-tuple-element.577), channel_id=1, source_target_pairs={{0,1},{1,0},{2,3},{3,2},{4,5},{5,4},{6,7},{7,6},{8,9},{9,8},{10,11... | collective-permute-start | bytes 1081352 | tf_op jit(solution)/shard_map/ppermute | solution.py:65
  149.6 10.8 %collective-permute-start.41 = (bf16[176,1024]{1,0:T(8,128)(2,1)S(1)}, bf16[176,1024]{1,0:T(8,128)(2,1)S(1)}, u32[]{:S(2)}, u32[]{:S(2)}) collective-permute-start(bf16[176,1024]{1,0:T(8,128)(2,1)S(1)} %shard_map.333), channel_id=1, source_target_pairs={{0,2},{1,3},{2,0},{3,1},{4,6},{5,7},{6,4},{7,5},{8,10},{9,11},{10,... | collective-permute-start | bytes 1081352 | tf_op jit(solution)/shard_map/ppermute | solution.py:65
  154.5 25.4 %collective-permute-start.47 = (bf16[2,2,128,1024]{3,2,1,0:T(8,128)(2,1)S(1)}, bf16[2,2,128,1024]{3,2,1,0:T(8,128)(2,1)S(1)}, u32[]{:S(2)}, u32[]{:S(2)}) collective-permute-start(bf16[2,2,128,1024]{3,2,1,0:T(8,128)(2,1)S(1)} %bitcast.72), channel_id=1, source_target_pairs={{0,4},{4,0},{8,12},{12,8},{16,20},{20,16},{24,28},{28,24},{1,5},{5... | collective-permute-start | bytes 3145736 | tf_op jit(solution)/shard_map/ppermute | solution.py:65
  156.0 24.9 %collective-permute-start.46 = (bf16[2,2,128,1024]{3,2,1,0:T(8,128)(2,1)S(1)}, bf16[2,2,128,1024]{3,2,1,0:T(8,128)(2,1)S(1)}, u32[]{:S(2)}, u32[]{:S(2)}) collective-permute-start(bf16[2,2,128,1024]{3,2,1,0:T(8,128)(2,1)S(1)} %bitcast.71), channel_id=1, source_target_pairs={{0,8},{4,12},{8,0},{12,4},{16,24},{20,28},{24,16},{28,20},{1,9},{5... | collective-permute-start | bytes 3145736 | tf_op jit(solution)/shard_map/ppermute | solution.py:65
  176.4 20.5 %collective-permute-start.50 = (bf16[2,2,128,768]{3,2,1,0:T(8,128)(2,1)S(1)}, bf16[2,2,128,768]{3,2,1,0:T(8,128)(2,1)S(1)}, u32[]{:S(2)}, u32[]{:S(2)}) collective-permute-start(bf16[2,2,128,768]{3,2,1,0:T(8,128)(2,1)S(1)} %bitcast.74), channel_id=1, source_target_pairs={{0,4},{4,0},{8,12},{12,8},{16,20},{20,16},{24,28},{28,24},{1,5},{5... | collective-permute-start | bytes 2359304 | tf_op jit(solution)/shard_map/ppermute | solution.py:65
  177.9 11.2 %collective-permute-start.52 = (bf16[1024,256]{1,0:T(8,128)(2,1)S(1)}, bf16[1024,256]{1,0:T(8,128)(2,1)S(1)}, u32[]{:S(2)}, u32[]{:S(2)}) collective-permute-start(bf16[1024,256]{1,0:T(8,128)(2,1)S(1)} %get-tuple-element.633), channel_id=1, source_target_pairs={{0,1},{1,0},{2,3},{3,2},{4,5},{5,4},{6,7},{7,6},{8,9},{9,8},{10,11... | collective-permute-start | bytes 1572872 | tf_op jit(solution)/shard_map/ppermute | solution.py:65
  178.0 14.3 %collective-permute-start.53 = (bf16[1024,256]{1,0:T(8,128)(2,1)S(1)}, bf16[1024,256]{1,0:T(8,128)(2,1)S(1)}, u32[]{:S(2)}, u32[]{:S(2)}) collective-permute-start(bf16[1024,256]{1,0:T(8,128)(2,1)S(1)} %shard_map.342), channel_id=1, source_target_pairs={{0,2},{1,3},{2,0},{3,1},{4,6},{5,7},{6,4},{7,5},{8,10},{9,11},{10,... | collective-permute-start | bytes 1572872 | tf_op jit(solution)/shard_map/ppermute | solution.py:65
  181.0 12.8 %collective-permute-start.51 = (bf16[2,128,1024]{2,1,0:T(8,128)(2,1)S(1)}, bf16[2,128,1024]{2,1,0:T(8,128)(2,1)S(1)}, u32[]{:S(2)}, u32[]{:S(2)}) collective-permute-start(bf16[2,128,1024]{2,1,0:T(8,128)(2,1)S(1)} %shard_map.345), channel_id=1, source_target_pairs={{0,8},{4,12},{8,0},{12,4},{16,24},{20,28},{24,16},{28,20},{1,9},{5... | collective-permute-start | bytes 1572872 | tf_op jit(solution)/shard_map/ppermute | solution.py:65
  183.0 30.7 %collective-permute-start.57 = (bf16[2,128,1024]{2,1,0:T(8,128)(2,1)S(1)}, bf16[2,128,1024]{2,1,0:T(8,128)(2,1)S(1)}, u32[]{:S(2)}, u32[]{:S(2)}) collective-permute-start(bf16[2,128,1024]{2,1,0:T(8,128)(2,1)S(1)} %shard_map.346), channel_id=1, source_target_pairs={{0,4},{4,0},{8,12},{12,8},{16,20},{20,16},{24,28},{28,24},{1,5},{5... | collective-permute-start | bytes 1572872 | tf_op jit(solution)/shard_map/ppermute | solution.py:65
  196.9 14.7 %collective-permute-start.54 = (bf16[2,128,768]{2,1,0:T(8,128)(2,1)S(1)}, bf16[2,128,768]{2,1,0:T(8,128)(2,1)S(1)}, u32[]{:S(2)}, u32[]{:S(2)}) collective-permute-start(bf16[2,128,768]{2,1,0:T(8,128)(2,1)S(1)} %shard_map.352), channel_id=1, source_target_pairs={{0,8},{4,12},{8,0},{12,4},{16,24},{20,28},{24,16},{28,20},{1,9},{5... | collective-permute-start | bytes 1179656 | tf_op jit(solution)/shard_map/ppermute | solution.py:65
  198.8 14.9 %collective-permute-start.49 = (bf16[176,1024]{1,0:T(8,128)(2,1)S(1)}, bf16[176,1024]{1,0:T(8,128)(2,1)S(1)}, u32[]{:S(2)}, u32[]{:S(2)}) collective-permute-start(bf16[176,1024]{1,0:T(8,128)(2,1)S(1)} %get-tuple-element.679), channel_id=1, source_target_pairs={{0,1},{1,0},{2,3},{3,2},{4,5},{5,4},{6,7},{7,6},{8,9},{9,8},{10,11... | collective-permute-start | bytes 1081352 | tf_op jit(solution)/shard_map/ppermute | solution.py:65
  198.8 17.4 %collective-permute-start.58 = (bf16[2,2,128,384]{3,2,1,0:T(8,128)(2,1)S(1)}, bf16[2,2,128,384]{3,2,1,0:T(8,128)(2,1)S(1)}, u32[]{:S(2)}, u32[]{:S(2)}) collective-permute-start(bf16[2,2,128,384]{3,2,1,0:T(8,128)(2,1)S(1)} %shard_map.350), channel_id=1, source_target_pairs={{0,4},{4,0},{8,12},{12,8},{16,20},{20,16},{24,28},{28,24},{1,5},{5... | collective-permute-start | bytes 1179656 | tf_op jit(solution)/shard_map/ppermute | solution.py:65
  200.2 19.9 %collective-permute-start.56 = (bf16[128,1024]{1,0:T(8,128)(2,1)S(1)}, bf16[128,1024]{1,0:T(8,128)(2,1)S(1)}, u32[]{:S(2)}, u32[]{:S(2)}) collective-permute-start(bf16[128,1024]{1,0:T(8,128)(2,1)S(1)} %shard_map.351), channel_id=1, source_target_pairs={{0,16},{4,20},{8,24},{12,28},{16,0},{20,4},{24,8},{28,12},{1,17},{... | collective-permute-start | bytes 786440 | tf_op jit(solution)/shard_map/ppermute | solution.py:65
  211.7 12.0 %collective-permute-start.59 = (bf16[128,768]{1,0:T(8,128)(2,1)S(1)}, bf16[128,768]{1,0:T(8,128)(2,1)S(1)}, u32[]{:S(2)}, u32[]{:S(2)}) collective-permute-start(bf16[128,768]{1,0:T(8,128)(2,1)S(1)} %shard_map.353), channel_id=1, source_target_pairs={{0,16},{4,20},{8,24},{12,28},{16,0},{20,4},{24,8},{28,12},{1,17},{... | collective-permute-start | bytes 589832 | tf_op jit(solution)/shard_map/ppermute | solution.py:65
  213.6 14.5 %collective-permute-start.48 = (bf16[176,1024]{1,0:T(8,128)(2,1)S(1)}, bf16[176,1024]{1,0:T(8,128)(2,1)S(1)}, u32[]{:S(2)}, u32[]{:S(2)}) collective-permute-start(bf16[176,1024]{1,0:T(8,128)(2,1)S(1)} %get-tuple-element.677), channel_id=1, source_target_pairs={{0,1},{1,0},{2,3},{3,2},{4,5},{5,4},{6,7},{7,6},{8,9},{9,8},{10,11... | collective-permute-start | bytes 1081352 | tf_op jit(solution)/shard_map/ppermute | solution.py:65
  213.7 14.4 %collective-permute-start.55 = (bf16[176,1024]{1,0:T(8,128)(2,1)S(1)}, bf16[176,1024]{1,0:T(8,128)(2,1)S(1)}, u32[]{:S(2)}, u32[]{:S(2)}) collective-permute-start(bf16[176,1024]{1,0:T(8,128)(2,1)S(1)} %shard_map.354), channel_id=1, source_target_pairs={{0,2},{1,3},{2,0},{3,1},{4,6},{5,7},{6,4},{7,5},{8,10},{9,11},{10,... | collective-permute-start | bytes 1081352 | tf_op jit(solution)/shard_map/ppermute | solution.py:65
  224.8 17.9 %collective-permute-start.61 = (bf16[128,1024]{1,0:T(8,128)(2,1)S(1)}, bf16[128,1024]{1,0:T(8,128)(2,1)S(1)}, u32[]{:S(2)}, u32[]{:S(2)}) collective-permute-start(bf16[128,1024]{1,0:T(8,128)(2,1)S(1)} %shard_map.356), channel_id=1, source_target_pairs={{0,16},{4,20},{8,24},{12,28},{16,0},{20,4},{24,8},{28,12},{1,17},{... | collective-permute-start | bytes 786440 | tf_op jit(solution)/shard_map/ppermute | solution.py:65
  (52 other events, 381.6 us)

commit v4 on v3

--- a/solution.py
+++ b/solution.py
@@ -491,9 +491,17 @@
 
 def half_grad_kernel(near, left_ref, right_ref, out_ref):
     left = left_ref[:, : D // 2] if near else left_ref[:, D // 2 :]
-    for n in range(right_ref.shape[1] // TILE):
-        at = slice(n * TILE, (n + 1) * TILE)
+
+    def tile(n):
+        at = pl.ds(pl.multiple_of(n * TILE, TILE), TILE)
         out_ref[:, at] = dot_tn(left, right_ref[:, at]).astype(bf16)
+
+    steps = right_ref.shape[1] // TILE
+    if near:
+        pl.loop(0, steps)(tile)
+    else:
+        for n in range(steps):
+            tile(n)
 
 
 def normal_below(u):
@@ -1069,7 +1077,13 @@
         )
 
     s_up.take()
-    x_up = columns_back([s_up]).turn()
+    s_first.take()
+    x_up = columns_back([s_up, s_first]).turn()
+    s_second.take().send()
+    run.wait(s_down.other, s_second.other, meet_tok.far, x_up.other)
+    s_down.take()
+    s_second.take()
+    x_rest = columns_back([s_down, s_second])
     out_f = shape_of((1, SLOTS, D), f32)
     grad_tokens = run(
         lambda *ins: glue(
@@ -1080,17 +1094,10 @@
         ),
         d_resid_one, *meet_tok.terms(),
     )
-    run.wait(s_second.other, x_up.other)
-    s_second.take().send()
-    run.wait(s_down.other, s_second.other)
-    s_down.take()
-    s_first.take()
-    s_second.take()
-    x_rest = columns_back([s_down, s_first, s_second])
     x_rest.turn()
-    (grad_up,) = whole_rows(x_up, (1,), (hidden,), ())
-    grad_down, grad_qkv, grad_proj, *out = whole_rows(
-        x_rest, (1, 3, 1), (hidden, width, width), (1,) * 6 + (2, 6, 4)
+    grad_up, grad_qkv = whole_rows(x_up, (1, 3), (hidden, width), ())
+    grad_down, grad_proj, *out = whole_rows(
+        x_rest, (1, 1), (hidden, width), (1,) * 6 + (2, 6, 4)
     )
     out = [x.reshape(-1) for x in out]
     return (

time: 261 us -> 257 us (0.985); the launches traced: 258 us -> 257 us
  waiting for transfers between devices: 135 us -> 131 us
    ppermute x67, waiting for transfers between devices: 135 us -> 131 us  [swap(): lax.ppermute(x, axis, [(i, i ^ b) for i in range(lax.axis_size(axis))])]
  transfers between devices with their start and end apart: 67 -> 67, of which waited for: 36 -> 37; matrix products, arithmetic and copies ran while one was open for 1% -> 1% of each run, Pallas kernels for 19% -> 19%
where the time goes in v4:
time: 257 us
  waiting for transfers between devices  131 us (51%)
  Pallas kernels  60.3 us (23%)
  starting transfers between devices  57 us (22%)
  local copies, waits for them, and re-layouts  5.66 us (2%)
    ppermute x67, waiting for transfers between devices, swap(): lax.ppermute(x, axis, [(i, i ^ b) for i in range(lax.axis_size(axis))])  131 us
    ppermute x67, starting transfers between devices, swap(): lax.ppermute(x, axis, [(i, i ^ b) for i in range(lax.axis_size(axis))])  57 us
    pallas_call x70, Pallas kernels, call(): pl.pallas_call(kernel, in_specs=[pl.BlockSpec(memory_space=m) for m in sp...  56.2 us
    unnamed x35, local copies, waits for them, and re-layouts  5.29 us
  transfers between devices with their start and end apart: 67, of which 37 were waited for; matrix products, arithmetic and copies ran while one was open for 1% of the time, Pallas kernels for 19%

profile of v4, /device:TPU:0, one launch (start us, length us, event | category | flops | bytes accessed | tf_op | source)
XLA Modules:
  0.0 257.0 jit_solution(13280348098058904377)
XLA Ops:
  7.6 3.0 %collective-permute-start.3 = (bf16[2,32,1024]{2,1,0:T(8,128)(2,1)S(1)}, bf16[2,32,1024]{2,1,0:T(8,128)(2,1)S(1)}, u32[]{:S(2)}, u32[]{:S(2)}) collective-permute-start(bf16[2,32,1024]{2,1,0:T(8,128)(2,1)S(1)} %get-tuple-element.406), channel_id=1, source_target_pairs={{0,2},{1,3},{2,0},{3,1},{4,6},{5,7},{6,4},{7,5},{8,10},{9,11},{10,... | collective-permute-start | bytes 393224 | tf_op jit(solution)/shard_map/ppermute | solution.py:65
  11.9 2.4 collective-permute-done.3.other
  18.5 2.7 %collective-permute-start.5 = (bf16[128,1024]{1,0:T(8,128)(2,1)S(1)}, bf16[128,1024]{1,0:T(8,128)(2,1)S(1)}, u32[]{:S(2)}, u32[]{:S(2)}) collective-permute-start(bf16[128,1024]{1,0:T(8,128)(2,1)S(1)} %bitcast.69), channel_id=1, source_target_pairs={{0,16},{4,20},{8,24},{12,28},{16,0},{20,4},{24,8},{28,12},{1,17},{... | collective-permute-start | bytes 786440 | tf_op jit(solution)/shard_map/ppermute | solution.py:65
  21.7 3.1 %collective-permute-done.6.o = bf16[32,128]{1,0:T(8,128)(2,1)S(1)} collective-permute-done((bf16[32,128]{1,0:T(8,128)(2,1)S(1)}, bf16[32,128]{1,0:T(8,128)(2,1)S(1)}, u32[]{:S(2)}, u32[]{:S(2)}) %collective-permute-start.6) | collective-permute-done | bytes 8224 | tf_op jit(solution)/shard_map/ppermute | solution.py:65
  30.6 3.5 %collective-permute-done.9.o = bf16[128,128]{1,0:T(8,128)(2,1)S(1)} collective-permute-done((bf16[128,128]{1,0:T(8,128)(2,1)S(1)}, bf16[128,128]{1,0:T(8,128)(2,1)S(1)}, u32[]{:S(2)}, u32[]{:S(2)}) %collective-permute-start.9) | collective-permute-done | bytes 32800 | tf_op jit(solution)/shard_map/ppermute | solution.py:65
  35.2 3.3 %collective-permute-start.11 = (bf16[128,1024]{1,0:T(8,128)(2,1)S(1)}, bf16[128,1024]{1,0:T(8,128)(2,1)S(1)}, u32[]{:S(2)}, u32[]{:S(2)}) collective-permute-start(bf16[128,1024]{1,0:T(8,128)(2,1)S(1)} %bitcast.78), channel_id=1, source_target_pairs={{0,16},{4,20},{8,24},{12,28},{16,0},{20,4},{24,8},{28,12},{1,17},{... | collective-permute-start | bytes 786440 | tf_op jit(solution)/shard_map/ppermute | solution.py:65
  38.5 14.4 %collective-permute-done.14.o = bf16[256,128]{1,0:T(8,128)(2,1)S(1)} collective-permute-done((bf16[256,128]{1,0:T(8,128)(2,1)S(1)}, bf16[256,128]{1,0:T(8,128)(2,1)S(1)}, u32[]{:S(2)}, u32[]{:S(2)}) %collective-permute-start.14) | collective-permute-done | bytes 65568 | tf_op jit(solution)/shard_map/ppermute | solution.py:65
  58.9 4.1 %shard_map.315.bias_ref = f32[4,4,176,176]{3,2,1,0:T(8,128)S(1)} custom-call(bf16[4,16,256]{2,1,0:T(8,128)(2,1)S(1)} %shard_map.310.notes_ref, f32[12,256]{1,0:T(8,128)S(1)} %get-tuple-element.468.ext_ref), custom_call_target="tpu_custom_call" | custom-call | tf_op jit(solution)/shard_map/pallas_call | solution.py:243
  62.9 7.5 %collective-permute-done.16.o = bf16[128,1024]{1,0:T(8,128)(2,1)S(1)} collective-permute-done((bf16[128,1024]{1,0:T(8,128)(2,1)S(1)}, bf16[128,1024]{1,0:T(8,128)(2,1)S(1)}, u32[]{:S(2)}, u32[]{:S(2)}) %collective-permute-start.16) | collective-permute-done | bytes 262176 | tf_op jit(solution)/shard_map/ppermute | solution.py:65
  71.3 6.4 %collective-permute-done.19.rest_2_ = bf16[512,256]{1,0:T(8,128)(2,1)S(1)} collective-permute-done((bf16[512,256]{1,0:T(8,128)(2,1)S(1)}, bf16[512,256]{1,0:T(8,128)(2,1)S(1)}, u32[]{:S(2)}, u32[]{:S(2)}) %collective-permute-start.19) | collective-permute-done | bytes 262176 | tf_op jit(solution)/shard_map/ppermute | solution.py:65
  77.8 5.4 %collective-permute-done.17.o = bf16[256,1024]{1,0:T(8,128)(2,1)S(1)} collective-permute-done((bf16[256,1024]{1,0:T(8,128)(2,1)S(1)}, bf16[256,1024]{1,0:T(8,128)(2,1)S(1)}, u32[]{:S(2)}, u32[]{:S(2)}) %collective-permute-start.17) | collective-permute-done | bytes 524320 | tf_op jit(solution)/shard_map/ppermute | solution.py:65
  83.4 3.1 %shard_map.320 = (bf16[704,1024]{1,0:T(8,128)(2,1)S(1)}, bf16[704,768]{1,0:T(8,128)(2,1)S(1)}, f32[4,4,176,176]{3,2,1,0:T(8,128)S(1)}, bf16[2,176,256]{2,1,0:T(8,128)(2,1)S(1)}) custom-call(s32[2]{0:T(128)S(1)} %pad_add_fusion.at.at_ref, bf16[176,1024]{1,0:T(8,128)(2,1)S(1)} %collective-permute-done.12.refs_2_.d0, ...), custom_call_target="tpu_custom_call" | custom-call | tf_op jit(solution)/shard_map/pallas_call | solution.py:31
  89.1 3.6 %collective-permute-done.21.o = bf16[256,1024]{1,0:T(8,128)(2,1)S(1)} collective-permute-done((bf16[256,1024]{1,0:T(8,128)(2,1)S(1)}, bf16[256,1024]{1,0:T(8,128)(2,1)S(1)}, u32[]{:S(2)}, u32[]{:S(2)}) %collective-permute-start.21) | collective-permute-done | bytes 524320 | tf_op jit(solution)/shard_map/ppermute | solution.py:65
  95.0 3.1 %shard_map.322 = (bf16[704,1024]{1,0:T(8,128)(2,1)S(1)}, bf16[704,768]{1,0:T(8,128)(2,1)S(1)}, f32[4,4,176,176]{3,2,1,0:T(8,128)S(1)}, bf16[2,176,256]{2,1,0:T(8,128)(2,1)S(1)}) custom-call(s32[2]{0:T(128)S(1)} %pad_add_fusion.at.at_ref, ...), custom_call_target="tpu_custom_call", output_to_operand_aliasing={{0}: (7, {}), {1}: (8, {}), {2}: (9, {})} | custom-call | tf_op jit(solution)/shard_map/pallas_call | solution.py:31
  103.4 9.3 %collective-permute-done.32.x0 = bf16[176,1024]{1,0:T(8,128)(2,1)S(1)} collective-permute-done((bf16[176,1024]{1,0:T(8,128)(2,1)S(1)}, bf16[176,1024]{1,0:T(8,128)(2,1)S(1)}, u32[]{:S(2)}, u32[]{:S(2)}) %collective-permute-start.32) | collective-permute-done | bytes 360480 | tf_op jit(solution)/shard_map/ppermute | solution.py:65
  114.2 2.5 shard_map.326
  116.7 2.5 shard_map.327
  123.9 7.7 %collective-permute-done.35.got_y = bf16[176,1024]{1,0:T(8,128)(2,1)S(1)} collective-permute-done((bf16[176,1024]{1,0:T(8,128)(2,1)S(1)}, bf16[176,1024]{1,0:T(8,128)(2,1)S(1)}, u32[]{:S(2)}, u32[]{:S(2)}) %collective-permute-start.35) | collective-permute-done | bytes 360480 | tf_op jit(solution)/shard_map/ppermute | solution.py:65
  134.8 7.9 %collective-permute-done.38.g0 = bf16[176,1024]{1,0:T(8,128)(2,1)S(1)} collective-permute-done((bf16[176,1024]{1,0:T(8,128)(2,1)S(1)}, bf16[176,1024]{1,0:T(8,128)(2,1)S(1)}, u32[]{:S(2)}, u32[]{:S(2)}) %collective-permute-start.38) | collective-permute-done | bytes 360480 | tf_op jit(solution)/shard_map/ppermute | solution.py:65
  142.7 2.4 shard_map.331
  145.1 2.4 shard_map.332
  165.6 4.0 %shard_map.340 = (bf16[704,768]{1,0:T(8,128)(2,1)S(1)}, f32[4,768]{1,0:T(4,128)S(1)}, f32[3,128,512]{2,1,0:T(8,128)S(1)}) custom-call(bf16[704,768]{1,0:T(8,128)(2,1)S(1)} %get-tuple-element.648.qkv_ref, f32[4,4,176,176]{3,2,1,0:T(8,128)S(1)} %get-tuple-element.649.probs_ref, bf16[176,256]{1,0:T(8,128)(2,1)S(1)} %get-tuple-element.639.g0, ...), custom_call_target="tpu_custom_call" | custom-call | flops 10000000000 | tf_op jit(solution)/shard_map/pallas_call | solution.py:31
  170.9 4.1 %shard_map.343 = (bf16[704,768]{1,0:T(8,128)(2,1)S(1)}, f32[4,768]{1,0:T(4,128)S(1)}, f32[3,128,512]{2,1,0:T(8,128)S(1)}, f32[12,256]{1,0:T(8,128)S(1)}) custom-call(bf16[704,768]{1,0:T(8,128)(2,1)S(1)} %get-tuple-element.648.qkv_ref, ...), custom_call_target="tpu_custom_call", output_to_operand_aliasing={{0}: (5, {}), {1}: (6, {}), {2}: (7, {})} | custom-call | tf_op jit(solution)/shard_map/pallas_call | solution.py:31
  185.2 2.7 %shard_map.348 = bf16[1024,128]{1,0:T(8,128)(2,1)S(1)} custom-call(s32[2]{0:T(128)S(1)} %pad_add_fusion.at.at_ref, f32[12,256]{1,0:T(8,128)S(1)} %get-tuple-element.668.ext_ref, f32[4,768]{1,0:T(4,128)S(1)} %get-tuple-element.669.sums_ref, f32[2,1024]{1,0:T(2,128)S(1)} %get-tuple-element.670.up_ref, f32[3,1024]{1,0:T(4,128)S(1)} %get-tuple-element.671.one_ref, ...), custom_call_target="tpu_custom_call" | custom-call | tf_op jit(solution)/shard_map/pallas_call | solution.py:31
  191.9 2.5 collective-permute-done.51.refs_2_
  194.5 2.6 %collective-permute-done.50.refs_1_ = bf16[2,2,128,768]{3,2,1,0:T(8,128)(2,1)S(1)} collective-permute-done((bf16[2,2,128,768]{3,2,1,0:T(8,128)(2,1)S(1)}, bf16[2,2,128,768]{3,2,1,0:T(8,128)(2,1)S(1)}, u32[]{:S(2)}, u32[]{:S(2)}) %collective-permute-start.50) | collective-permute-done | bytes 786464 | tf_op jit(solution)/shard_map/ppermute | solution.py:65
  202.1 8.5 %collective-permute-done.54.refs_2_ = bf16[2,128,768]{2,1,0:T(8,128)(2,1)S(1)} collective-permute-done((bf16[2,128,768]{2,1,0:T(8,128)(2,1)S(1)}, bf16[2,128,768]{2,1,0:T(8,128)(2,1)S(1)}, u32[]{:S(2)}, u32[]{:S(2)}) %collective-permute-start.54) | collective-permute-done | bytes 393248 | tf_op jit(solution)/shard_map/ppermute | solution.py:65
  210.7 2.7 %collective-permute-start.59 = (bf16[128,768]{1,0:T(8,128)(2,1)S(1)}, bf16[128,768]{1,0:T(8,128)(2,1)S(1)}, u32[]{:S(2)}, u32[]{:S(2)}) collective-permute-start(bf16[128,768]{1,0:T(8,128)(2,1)S(1)} %shard_map.353), channel_id=1, source_target_pairs={{0,16},{4,20},{8,24},{12,28},{16,0},{20,4},{24,8},{28,12},{1,17},{... | collective-permute-start | bytes 589832 | tf_op jit(solution)/shard_map/ppermute | solution.py:65
  213.9 6.4 %collective-permute-done.57.refs_4_ = bf16[2,2,128,384]{3,2,1,0:T(8,128)(2,1)S(1)} collective-permute-done((bf16[2,2,128,384]{3,2,1,0:T(8,128)(2,1)S(1)}, bf16[2,2,128,384]{3,2,1,0:T(8,128)(2,1)S(1)}, u32[]{:S(2)}, u32[]{:S(2)}) %collective-permute-start.57) | collective-permute-done | bytes 393248 | tf_op jit(solution)/shard_map/ppermute | solution.py:65
  220.9 3.8 %collective-permute-done.59.refs_3_ = bf16[128,768]{1,0:T(8,128)(2,1)S(1)} collective-permute-done((bf16[128,768]{1,0:T(8,128)(2,1)S(1)}, bf16[128,768]{1,0:T(8,128)(2,1)S(1)}, u32[]{:S(2)}, u32[]{:S(2)}) %collective-permute-start.59) | collective-permute-done | bytes 196640 | tf_op jit(solution)/shard_map/ppermute | solution.py:65
  230.0 5.8 %collective-permute-done.61.refs_5_ = bf16[2,128,384]{2,1,0:T(8,128)(2,1)S(1)} collective-permute-done((bf16[2,128,384]{2,1,0:T(8,128)(2,1)S(1)}, bf16[2,128,384]{2,1,0:T(8,128)(2,1)S(1)}, u32[]{:S(2)}, u32[]{:S(2)}) %collective-permute-start.61) | collective-permute-done | bytes 196640 | tf_op jit(solution)/shard_map/ppermute | solution.py:65
  237.2 7.0 %collective-permute-done.60.refs_3_ = bf16[128,1024]{1,0:T(8,128)(2,1)S(1)} collective-permute-done((bf16[128,1024]{1,0:T(8,128)(2,1)S(1)}, bf16[128,1024]{1,0:T(8,128)(2,1)S(1)}, u32[]{:S(2)}, u32[]{:S(2)}) %collective-permute-start.60) | collective-permute-done | bytes 262176 | tf_op jit(solution)/shard_map/ppermute | solution.py:65
  (225 shorter events, 104.5 us)
Async XLA Ops:
  18.5 15.7 %collective-permute-start.5 = (bf16[128,1024]{1,0:T(8,128)(2,1)S(1)}, bf16[128,1024]{1,0:T(8,128)(2,1)S(1)}, u32[]{:S(2)}, u32[]{:S(2)}) collective-permute-start(bf16[128,1024]{1,0:T(8,128)(2,1)S(1)} %bitcast.69), channel_id=1, source_target_pairs={{0,16},{4,20},{8,24},{12,28},{16,0},{20,4},{24,8},{28,12},{1,17},{... | collective-permute-start | bytes 786440 | tf_op jit(solution)/shard_map/ppermute | solution.py:65
  34.2 20.9 %collective-permute-start.10 = (bf16[256,1024]{1,0:T(8,128)(2,1)S(1)}, bf16[256,1024]{1,0:T(8,128)(2,1)S(1)}, u32[]{:S(2)}, u32[]{:S(2)}) collective-permute-start(bf16[256,1024]{1,0:T(8,128)(2,1)S(1)} %shard_map.309.m), channel_id=1, source_target_pairs={{0,8},{4,12},{8,0},{12,4},{16,24},{20,28},{24,16},{28,20},{1,9},{5... | collective-permute-start | bytes 1572872 | tf_op jit(solution)/shard_map/ppermute | solution.py:65
  35.2 17.8 %collective-permute-start.11 = (bf16[128,1024]{1,0:T(8,128)(2,1)S(1)}, bf16[128,1024]{1,0:T(8,128)(2,1)S(1)}, u32[]{:S(2)}, u32[]{:S(2)}) collective-permute-start(bf16[128,1024]{1,0:T(8,128)(2,1)S(1)} %bitcast.78), channel_id=1, source_target_pairs={{0,16},{4,20},{8,24},{12,28},{16,0},{20,4},{24,8},{28,12},{1,17},{... | collective-permute-start | bytes 786440 | tf_op jit(solution)/shard_map/ppermute | solution.py:65
  38.5 14.5 %collective-permute-start.14 = (bf16[256,128]{1,0:T(8,128)(2,1)S(1)}, bf16[256,128]{1,0:T(8,128)(2,1)S(1)}, u32[]{:S(2)}, u32[]{:S(2)}) collective-permute-start(bf16[256,128]{1,0:T(8,128)(2,1)S(1)} %shard_map.308.m), channel_id=1, source_target_pairs={{0,16},{4,20},{8,24},{12,28},{16,0},{20,4},{24,8},{28,12},{1,17},{... | collective-permute-start | bytes 196616 | tf_op jit(solution)/shard_map/ppermute | solution.py:65
  55.2 28.0 %collective-permute-start.15 = (bf16[512,1024]{1,0:T(8,128)(2,1)S(1)}, bf16[512,1024]{1,0:T(8,128)(2,1)S(1)}, u32[]{:S(2)}, u32[]{:S(2)}) collective-permute-start(bf16[512,1024]{1,0:T(8,128)(2,1)S(1)} %shard_map.312.refs_0_.near_ref), channel_id=1, source_target_pairs={{0,4},{4,0},{8,12},{12,8},{16,20},{20,16},{24,28},{28,24},{1,5},{5... | collective-permute-start | bytes 3145736 | tf_op jit(solution)/shard_map/ppermute | solution.py:65
  56.8 13.6 %collective-permute-start.16 = (bf16[128,1024]{1,0:T(8,128)(2,1)S(1)}, bf16[128,1024]{1,0:T(8,128)(2,1)S(1)}, u32[]{:S(2)}, u32[]{:S(2)}) collective-permute-start(bf16[128,1024]{1,0:T(8,128)(2,1)S(1)} %bitcast.76), channel_id=1, source_target_pairs={{0,16},{4,20},{8,24},{12,28},{16,0},{20,4},{24,8},{28,12},{1,17},{... | collective-permute-start | bytes 786440 | tf_op jit(solution)/shard_map/ppermute | solution.py:65
  70.4 12.7 %collective-permute-start.17 = (bf16[256,1024]{1,0:T(8,128)(2,1)S(1)}, bf16[256,1024]{1,0:T(8,128)(2,1)S(1)}, u32[]{:S(2)}, u32[]{:S(2)}) collective-permute-start(bf16[256,1024]{1,0:T(8,128)(2,1)S(1)} %shard_map.316.m), channel_id=1, source_target_pairs={{0,8},{4,12},{8,0},{12,4},{16,24},{20,28},{24,16},{28,20},{1,9},{5... | collective-permute-start | bytes 1572872 | tf_op jit(solution)/shard_map/ppermute | solution.py:65
  71.0 21.7 %collective-permute-start.21 = (bf16[256,1024]{1,0:T(8,128)(2,1)S(1)}, bf16[256,1024]{1,0:T(8,128)(2,1)S(1)}, u32[]{:S(2)}, u32[]{:S(2)}) collective-permute-start(bf16[256,1024]{1,0:T(8,128)(2,1)S(1)} %shard_map.311.m), channel_id=1, source_target_pairs={{0,4},{4,0},{8,12},{12,8},{16,20},{20,16},{24,28},{28,24},{1,5},{5... | collective-permute-start | bytes 1572872 | tf_op jit(solution)/shard_map/ppermute | solution.py:65
  71.3 11.9 %collective-permute-start.18 = (bf16[512,256]{1,0:T(8,128)(2,1)S(1)}, bf16[512,256]{1,0:T(8,128)(2,1)S(1)}, u32[]{:S(2)}, u32[]{:S(2)}) collective-permute-start(bf16[512,256]{1,0:T(8,128)(2,1)S(1)} %shard_map.317.rest_0_), channel_id=1, source_target_pairs={{0,1},{1,0},{2,3},{3,2},{4,5},{5,4},{6,7},{7,6},{8,9},{9,8},{10,11... | collective-permute-start | bytes 786440 | tf_op jit(solution)/shard_map/ppermute | solution.py:65
  83.3 11.2 %collective-permute-start.26 = (bf16[512,256]{1,0:T(8,128)(2,1)S(1)}, bf16[512,256]{1,0:T(8,128)(2,1)S(1)}, u32[]{:S(2)}, u32[]{:S(2)}) collective-permute-start(bf16[512,256]{1,0:T(8,128)(2,1)S(1)} %shard_map.319.rest_4_), channel_id=1, source_target_pairs={{0,2},{1,3},{2,0},{3,1},{4,6},{5,7},{6,4},{7,5},{8,10},{9,11},{10,... | collective-permute-start | bytes 786440 | tf_op jit(solution)/shard_map/ppermute | solution.py:65
  86.5 11.6 %collective-permute-start.23 = (bf16[2,176,256]{2,1,0:T(8,128)(2,1)S(1)}, bf16[2,176,256]{2,1,0:T(8,128)(2,1)S(1)}, u32[]{:S(2)}, u32[]{:S(2)}) collective-permute-start(bf16[2,176,256]{2,1,0:T(8,128)(2,1)S(1)} %get-tuple-element.486), channel_id=1, source_target_pairs={{0,2},{1,3},{2,0},{3,1},{4,6},{5,7},{6,4},{7,5},{8,10},{9,11},{10,... | collective-permute-start | bytes 540680 | tf_op jit(solution)/shard_map/ppermute | solution.py:65
  88.5 24.7 %collective-permute-start.29 = (bf16[512,1024]{1,0:T(8,128)(2,1)S(1)}, bf16[512,1024]{1,0:T(8,128)(2,1)S(1)}, u32[]{:S(2)}, u32[]{:S(2)}) collective-permute-start(bf16[512,1024]{1,0:T(8,128)(2,1)S(1)} %shard_map.318.up_near), channel_id=1, source_target_pairs={{0,4},{4,0},{8,12},{12,8},{16,20},{20,16},{24,28},{28,24},{1,5},{5... | collective-permute-start | bytes 3145736 | tf_op jit(solution)/shard_map/ppermute | solution.py:65
  92.7 21.5 %collective-permute-start.30 = (bf16[512,1024]{1,0:T(8,128)(2,1)S(1)}, bf16[512,1024]{1,0:T(8,128)(2,1)S(1)}, u32[]{:S(2)}, u32[]{:S(2)}) collective-permute-start(bf16[512,1024]{1,0:T(8,128)(2,1)S(1)} %shard_map.321.down_near), channel_id=1, source_target_pairs={{0,8},{4,12},{8,0},{12,4},{16,24},{20,28},{24,16},{28,20},{1,9},{5... | collective-permute-start | bytes 3145736 | tf_op jit(solution)/shard_map/ppermute | solution.py:65
  121.1 10.6 %collective-permute-start.35 = (bf16[176,1024]{1,0:T(8,128)(2,1)S(1)}, bf16[176,1024]{1,0:T(8,128)(2,1)S(1)}, u32[]{:S(2)}, u32[]{:S(2)}) collective-permute-start(bf16[176,1024]{1,0:T(8,128)(2,1)S(1)} %shard_map.328), channel_id=1, source_target_pairs={{0,2},{1,3},{2,0},{3,1},{4,6},{5,7},{6,4},{7,5},{8,10},{9,11},{10,... | collective-permute-start | bytes 1081352 | tf_op jit(solution)/shard_map/ppermute | solution.py:65
  148.0 12.1 %collective-permute-start.37 = (bf16[176,1024]{1,0:T(8,128)(2,1)S(1)}, bf16[176,1024]{1,0:T(8,128)(2,1)S(1)}, u32[]{:S(2)}, u32[]{:S(2)}) collective-permute-start(bf16[176,1024]{1,0:T(8,128)(2,1)S(1)} %get-tuple-element.578), channel_id=1, source_target_pairs={{0,1},{1,0},{2,3},{3,2},{4,5},{5,4},{6,7},{7,6},{8,9},{9,8},{10,11... | collective-permute-start | bytes 1081352 | tf_op jit(solution)/shard_map/ppermute | solution.py:65
  149.4 10.8 %collective-permute-start.41 = (bf16[176,1024]{1,0:T(8,128)(2,1)S(1)}, bf16[176,1024]{1,0:T(8,128)(2,1)S(1)}, u32[]{:S(2)}, u32[]{:S(2)}) collective-permute-start(bf16[176,1024]{1,0:T(8,128)(2,1)S(1)} %shard_map.333), channel_id=1, source_target_pairs={{0,2},{1,3},{2,0},{3,1},{4,6},{5,7},{6,4},{7,5},{8,10},{9,11},{10,... | collective-permute-start | bytes 1081352 | tf_op jit(solution)/shard_map/ppermute | solution.py:65
  155.1 26.1 %collective-permute-start.47 = (bf16[2,2,128,1024]{3,2,1,0:T(8,128)(2,1)S(1)}, bf16[2,2,128,1024]{3,2,1,0:T(8,128)(2,1)S(1)}, u32[]{:S(2)}, u32[]{:S(2)}) collective-permute-start(bf16[2,2,128,1024]{3,2,1,0:T(8,128)(2,1)S(1)} %bitcast.72), channel_id=1, source_target_pairs={{0,4},{4,0},{8,12},{12,8},{16,20},{20,16},{24,28},{28,24},{1,5},{5... | collective-permute-start | bytes 3145736 | tf_op jit(solution)/shard_map/ppermute | solution.py:65
  156.6 24.9 %collective-permute-start.46 = (bf16[2,2,128,1024]{3,2,1,0:T(8,128)(2,1)S(1)}, bf16[2,2,128,1024]{3,2,1,0:T(8,128)(2,1)S(1)}, u32[]{:S(2)}, u32[]{:S(2)}) collective-permute-start(bf16[2,2,128,1024]{3,2,1,0:T(8,128)(2,1)S(1)} %bitcast.71), channel_id=1, source_target_pairs={{0,8},{4,12},{8,0},{12,4},{16,24},{20,28},{24,16},{28,20},{1,9},{5... | collective-permute-start | bytes 3145736 | tf_op jit(solution)/shard_map/ppermute | solution.py:65
  175.9 21.2 %collective-permute-start.50 = (bf16[2,2,128,768]{3,2,1,0:T(8,128)(2,1)S(1)}, bf16[2,2,128,768]{3,2,1,0:T(8,128)(2,1)S(1)}, u32[]{:S(2)}, u32[]{:S(2)}) collective-permute-start(bf16[2,2,128,768]{3,2,1,0:T(8,128)(2,1)S(1)} %bitcast.74), channel_id=1, source_target_pairs={{0,4},{4,0},{8,12},{12,8},{16,20},{20,16},{24,28},{28,24},{1,5},{5... | collective-permute-start | bytes 2359304 | tf_op jit(solution)/shard_map/ppermute | solution.py:65
  177.5 12.4 %collective-permute-start.52 = (bf16[1024,256]{1,0:T(8,128)(2,1)S(1)}, bf16[1024,256]{1,0:T(8,128)(2,1)S(1)}, u32[]{:S(2)}, u32[]{:S(2)}) collective-permute-start(bf16[1024,256]{1,0:T(8,128)(2,1)S(1)} %get-tuple-element.634), channel_id=1, source_target_pairs={{0,1},{1,0},{2,3},{3,2},{4,5},{5,4},{6,7},{7,6},{8,9},{9,8},{10,11... | collective-permute-start | bytes 1572872 | tf_op jit(solution)/shard_map/ppermute | solution.py:65
  177.6 14.3 %collective-permute-start.53 = (bf16[1024,256]{1,0:T(8,128)(2,1)S(1)}, bf16[1024,256]{1,0:T(8,128)(2,1)S(1)}, u32[]{:S(2)}, u32[]{:S(2)}) collective-permute-start(bf16[1024,256]{1,0:T(8,128)(2,1)S(1)} %shard_map.342), channel_id=1, source_target_pairs={{0,2},{1,3},{2,0},{3,1},{4,6},{5,7},{6,4},{7,5},{8,10},{9,11},{10,... | collective-permute-start | bytes 1572872 | tf_op jit(solution)/shard_map/ppermute | solution.py:65
  181.6 12.8 %collective-permute-start.51 = (bf16[2,128,1024]{2,1,0:T(8,128)(2,1)S(1)}, bf16[2,128,1024]{2,1,0:T(8,128)(2,1)S(1)}, u32[]{:S(2)}, u32[]{:S(2)}) collective-permute-start(bf16[2,128,1024]{2,1,0:T(8,128)(2,1)S(1)} %shard_map.345), channel_id=1, source_target_pairs={{0,8},{4,12},{8,0},{12,4},{16,24},{20,28},{24,16},{28,20},{1,9},{5... | collective-permute-start | bytes 1572872 | tf_op jit(solution)/shard_map/ppermute | solution.py:65
  197.2 13.4 %collective-permute-start.54 = (bf16[2,128,768]{2,1,0:T(8,128)(2,1)S(1)}, bf16[2,128,768]{2,1,0:T(8,128)(2,1)S(1)}, u32[]{:S(2)}, u32[]{:S(2)}) collective-permute-start(bf16[2,128,768]{2,1,0:T(8,128)(2,1)S(1)} %shard_map.352), channel_id=1, source_target_pairs={{0,8},{4,12},{8,0},{12,4},{16,24},{20,28},{24,16},{28,20},{1,9},{5... | collective-permute-start | bytes 1179656 | tf_op jit(solution)/shard_map/ppermute | solution.py:65
  199.0 14.9 %collective-permute-start.56 = (bf16[2,128,1024]{2,1,0:T(8,128)(2,1)S(1)}, bf16[2,128,1024]{2,1,0:T(8,128)(2,1)S(1)}, u32[]{:S(2)}, u32[]{:S(2)}) collective-permute-start(bf16[2,128,1024]{2,1,0:T(8,128)(2,1)S(1)} %shard_map.346), channel_id=1, source_target_pairs={{0,4},{4,0},{8,12},{12,8},{16,20},{20,16},{24,28},{28,24},{1,5},{5... | collective-permute-start | bytes 1572872 | tf_op jit(solution)/shard_map/ppermute | solution.py:65
  200.5 19.7 %collective-permute-start.57 = (bf16[2,2,128,384]{3,2,1,0:T(8,128)(2,1)S(1)}, bf16[2,2,128,384]{3,2,1,0:T(8,128)(2,1)S(1)}, u32[]{:S(2)}, u32[]{:S(2)}) collective-permute-start(bf16[2,2,128,384]{3,2,1,0:T(8,128)(2,1)S(1)} %shard_map.350), channel_id=1, source_target_pairs={{0,4},{4,0},{8,12},{12,8},{16,20},{20,16},{24,28},{28,24},{1,5},{5... | collective-permute-start | bytes 1179656 | tf_op jit(solution)/shard_map/ppermute | solution.py:65
  201.1 12.3 %collective-permute-start.49 = (bf16[176,1024]{1,0:T(8,128)(2,1)S(1)}, bf16[176,1024]{1,0:T(8,128)(2,1)S(1)}, u32[]{:S(2)}, u32[]{:S(2)}) collective-permute-start(bf16[176,1024]{1,0:T(8,128)(2,1)S(1)} %get-tuple-element.680), channel_id=1, source_target_pairs={{0,1},{1,0},{2,3},{3,2},{4,5},{5,4},{6,7},{7,6},{8,9},{9,8},{10,11... | collective-permute-start | bytes 1081352 | tf_op jit(solution)/shard_map/ppermute | solution.py:65
  201.1 19.9 %collective-permute-start.58 = (bf16[128,1024]{1,0:T(8,128)(2,1)S(1)}, bf16[128,1024]{1,0:T(8,128)(2,1)S(1)}, u32[]{:S(2)}, u32[]{:S(2)}) collective-permute-start(bf16[128,1024]{1,0:T(8,128)(2,1)S(1)} %shard_map.351), channel_id=1, source_target_pairs={{0,16},{4,20},{8,24},{12,28},{16,0},{20,4},{24,8},{28,12},{1,17},{... | collective-permute-start | bytes 786440 | tf_op jit(solution)/shard_map/ppermute | solution.py:65
  210.7 14.1 %collective-permute-start.59 = (bf16[128,768]{1,0:T(8,128)(2,1)S(1)}, bf16[128,768]{1,0:T(8,128)(2,1)S(1)}, u32[]{:S(2)}, u32[]{:S(2)}) collective-permute-start(bf16[128,768]{1,0:T(8,128)(2,1)S(1)} %shard_map.353), channel_id=1, source_target_pairs={{0,16},{4,20},{8,24},{12,28},{16,0},{20,4},{24,8},{28,12},{1,17},{... | collective-permute-start | bytes 589832 | tf_op jit(solution)/shard_map/ppermute | solution.py:65
  225.9 11.3 %collective-permute-start.55 = (bf16[176,1024]{1,0:T(8,128)(2,1)S(1)}, bf16[176,1024]{1,0:T(8,128)(2,1)S(1)}, u32[]{:S(2)}, u32[]{:S(2)}) collective-permute-start(bf16[176,1024]{1,0:T(8,128)(2,1)S(1)} %shard_map.354), channel_id=1, source_target_pairs={{0,2},{1,3},{2,0},{3,1},{4,6},{5,7},{6,4},{7,5},{8,10},{9,11},{10,... | collective-permute-start | bytes 1081352 | tf_op jit(solution)/shard_map/ppermute | solution.py:65
  226.4 17.8 %collective-permute-start.60 = (bf16[128,1024]{1,0:T(8,128)(2,1)S(1)}, bf16[128,1024]{1,0:T(8,128)(2,1)S(1)}, u32[]{:S(2)}, u32[]{:S(2)}) collective-permute-start(bf16[128,1024]{1,0:T(8,128)(2,1)S(1)} %shard_map.356), channel_id=1, source_target_pairs={{0,16},{4,20},{8,24},{12,28},{16,0},{20,4},{24,8},{28,12},{1,17},{... | collective-permute-start | bytes 786440 | tf_op jit(solution)/shard_map/ppermute | solution.py:65
  228.3 17.2 %collective-permute-start.64 = (bf16[2,32,1792]{2,1,0:T(8,128)(2,1)S(1)}, bf16[2,32,1792]{2,1,0:T(8,128)(2,1)S(1)}, u32[]{:S(2)}, u32[]{:S(2)}) collective-permute-start(bf16[2,32,1792]{2,1,0:T(8,128)(2,1)S(1)} %get-tuple-element.719), channel_id=1, source_target_pairs={{0,2},{1,3},{2,0},{3,1},{4,6},{5,7},{6,4},{7,5},{8,10},{9,11},{10,... | collective-permute-start | bytes 688136 | tf_op jit(solution)/shard_map/ppermute | solution.py:65
  230.0 16.5 %collective-permute-start.48 = (bf16[176,1024]{1,0:T(8,128)(2,1)S(1)}, bf16[176,1024]{1,0:T(8,128)(2,1)S(1)}, u32[]{:S(2)}, u32[]{:S(2)}) collective-permute-start(bf16[176,1024]{1,0:T(8,128)(2,1)S(1)} %get-tuple-element.678), channel_id=1, source_target_pairs={{0,1},{1,0},{2,3},{3,2},{4,5},{5,4},{6,7},{7,6},{8,9},{9,8},{10,11... | collective-permute-start | bytes 1081352 | tf_op jit(solution)/shard_map/ppermute | solution.py:65
  (52 other events, 381.4 us)

commit v5 on v4

--- a/solution.py
+++ b/solution.py
@@ -987,7 +987,7 @@
     d_qkv, d_sums, d_grid = run(
         lambda *ins: call(
             partial(attend_back_kernel, heads, (0, 1), False), ins,
-            [qkv_out, shape_of((tp, 3 * width), f32), grids], room, cost=10,
+            [qkv_out, shape_of((tp, 3 * width), f32), grids], room, cost=6,
         ),
         qkv, probs, a0, got_c, notes,
     )

time: 257 us -> 257 us (level)
  transfers between devices with their start and end apart: 67 -> 67, of which waited for: 37 -> 35; matrix products, arithmetic and copies ran while one was open for 1% -> 1% of each run, Pallas kernels for 19% -> 19%
where the time goes in v5:
time: 257 us; the launch traced here: 256 us
  waiting for transfers between devices  131 us (51%)
  Pallas kernels  60.2 us (23%)
  starting transfers between devices  56.2 us (22%)
  local copies, waits for them, and re-layouts  5.66 us (2%)
    ppermute x67, waiting for transfers between devices, swap(): lax.ppermute(x, axis, [(i, i ^ b) for i in range(lax.axis_size(axis))])  131 us
    ppermute x67, starting transfers between devices, swap(): lax.ppermute(x, axis, [(i, i ^ b) for i in range(lax.axis_size(axis))])  56.2 us
    pallas_call x70, Pallas kernels, call(): pl.pallas_call(kernel, in_specs=[pl.BlockSpec(memory_space=m) for m in sp...  56.2 us
    unnamed x35, local copies, waits for them, and re-layouts  5.29 us
  transfers between devices with their start and end apart: 67, of which 35 were waited for; matrix products, arithmetic and copies ran while one was open for 1% of the time, Pallas kernels for 19%

profile of v5, /device:TPU:0, one launch (start us, length us, event | category | flops | bytes accessed | tf_op | source)
XLA Modules:
  0.0 256.4 jit_solution(4387566240777615066)
XLA Ops:
  7.6 3.0 %collective-permute-start.3 = (bf16[2,32,1024]{2,1,0:T(8,128)(2,1)S(1)}, bf16[2,32,1024]{2,1,0:T(8,128)(2,1)S(1)}, u32[]{:S(2)}, u32[]{:S(2)}) collective-permute-start(bf16[2,32,1024]{2,1,0:T(8,128)(2,1)S(1)} %get-tuple-element.406), channel_id=1, source_target_pairs={{0,2},{1,3},{2,0},{3,1},{4,6},{5,7},{6,4},{7,5},{8,10},{9,11},{10,... | collective-permute-start | bytes 393224 | tf_op jit(solution)/shard_map/ppermute | solution.py:65
  11.9 2.4 collective-permute-done.3.other
  18.5 2.7 %collective-permute-start.5 = (bf16[128,1024]{1,0:T(8,128)(2,1)S(1)}, bf16[128,1024]{1,0:T(8,128)(2,1)S(1)}, u32[]{:S(2)}, u32[]{:S(2)}) collective-permute-start(bf16[128,1024]{1,0:T(8,128)(2,1)S(1)} %bitcast.69), channel_id=1, source_target_pairs={{0,16},{4,20},{8,24},{12,28},{16,0},{20,4},{24,8},{28,12},{1,17},{... | collective-permute-start | bytes 786440 | tf_op jit(solution)/shard_map/ppermute | solution.py:65
  21.7 3.1 %collective-permute-done.6.o = bf16[32,128]{1,0:T(8,128)(2,1)S(1)} collective-permute-done((bf16[32,128]{1,0:T(8,128)(2,1)S(1)}, bf16[32,128]{1,0:T(8,128)(2,1)S(1)}, u32[]{:S(2)}, u32[]{:S(2)}) %collective-permute-start.6) | collective-permute-done | bytes 8224 | tf_op jit(solution)/shard_map/ppermute | solution.py:65
  30.6 3.5 %collective-permute-done.9.o = bf16[128,128]{1,0:T(8,128)(2,1)S(1)} collective-permute-done((bf16[128,128]{1,0:T(8,128)(2,1)S(1)}, bf16[128,128]{1,0:T(8,128)(2,1)S(1)}, u32[]{:S(2)}, u32[]{:S(2)}) %collective-permute-start.9) | collective-permute-done | bytes 32800 | tf_op jit(solution)/shard_map/ppermute | solution.py:65
  35.2 3.3 %collective-permute-start.11 = (bf16[128,1024]{1,0:T(8,128)(2,1)S(1)}, bf16[128,1024]{1,0:T(8,128)(2,1)S(1)}, u32[]{:S(2)}, u32[]{:S(2)}) collective-permute-start(bf16[128,1024]{1,0:T(8,128)(2,1)S(1)} %bitcast.78), channel_id=1, source_target_pairs={{0,16},{4,20},{8,24},{12,28},{16,0},{20,4},{24,8},{28,12},{1,17},{... | collective-permute-start | bytes 786440 | tf_op jit(solution)/shard_map/ppermute | solution.py:65
  38.5 14.4 %collective-permute-done.14.o = bf16[256,128]{1,0:T(8,128)(2,1)S(1)} collective-permute-done((bf16[256,128]{1,0:T(8,128)(2,1)S(1)}, bf16[256,128]{1,0:T(8,128)(2,1)S(1)}, u32[]{:S(2)}, u32[]{:S(2)}) %collective-permute-start.14) | collective-permute-done | bytes 65568 | tf_op jit(solution)/shard_map/ppermute | solution.py:65
  58.9 4.1 %shard_map.315.bias_ref = f32[4,4,176,176]{3,2,1,0:T(8,128)S(1)} custom-call(bf16[4,16,256]{2,1,0:T(8,128)(2,1)S(1)} %shard_map.310.notes_ref, f32[12,256]{1,0:T(8,128)S(1)} %get-tuple-element.468.ext_ref), custom_call_target="tpu_custom_call" | custom-call | tf_op jit(solution)/shard_map/pallas_call | solution.py:243
  62.9 7.5 %collective-permute-done.16.o = bf16[128,1024]{1,0:T(8,128)(2,1)S(1)} collective-permute-done((bf16[128,1024]{1,0:T(8,128)(2,1)S(1)}, bf16[128,1024]{1,0:T(8,128)(2,1)S(1)}, u32[]{:S(2)}, u32[]{:S(2)}) %collective-permute-start.16) | collective-permute-done | bytes 262176 | tf_op jit(solution)/shard_map/ppermute | solution.py:65
  71.3 6.4 %collective-permute-done.19.rest_2_ = bf16[512,256]{1,0:T(8,128)(2,1)S(1)} collective-permute-done((bf16[512,256]{1,0:T(8,128)(2,1)S(1)}, bf16[512,256]{1,0:T(8,128)(2,1)S(1)}, u32[]{:S(2)}, u32[]{:S(2)}) %collective-permute-start.19) | collective-permute-done | bytes 262176 | tf_op jit(solution)/shard_map/ppermute | solution.py:65
  77.8 5.4 %collective-permute-done.17.o = bf16[256,1024]{1,0:T(8,128)(2,1)S(1)} collective-permute-done((bf16[256,1024]{1,0:T(8,128)(2,1)S(1)}, bf16[256,1024]{1,0:T(8,128)(2,1)S(1)}, u32[]{:S(2)}, u32[]{:S(2)}) %collective-permute-start.17) | collective-permute-done | bytes 524320 | tf_op jit(solution)/shard_map/ppermute | solution.py:65
  83.4 3.1 %shard_map.320 = (bf16[704,1024]{1,0:T(8,128)(2,1)S(1)}, bf16[704,768]{1,0:T(8,128)(2,1)S(1)}, f32[4,4,176,176]{3,2,1,0:T(8,128)S(1)}, bf16[2,176,256]{2,1,0:T(8,128)(2,1)S(1)}) custom-call(s32[2]{0:T(128)S(1)} %pad_add_fusion.at.at_ref, bf16[176,1024]{1,0:T(8,128)(2,1)S(1)} %collective-permute-done.12.refs_2_.d0, ...), custom_call_target="tpu_custom_call" | custom-call | tf_op jit(solution)/shard_map/pallas_call | solution.py:31
  89.1 3.6 %collective-permute-done.21.o = bf16[256,1024]{1,0:T(8,128)(2,1)S(1)} collective-permute-done((bf16[256,1024]{1,0:T(8,128)(2,1)S(1)}, bf16[256,1024]{1,0:T(8,128)(2,1)S(1)}, u32[]{:S(2)}, u32[]{:S(2)}) %collective-permute-start.21) | collective-permute-done | bytes 524320 | tf_op jit(solution)/shard_map/ppermute | solution.py:65
  95.0 3.1 %shard_map.322 = (bf16[704,1024]{1,0:T(8,128)(2,1)S(1)}, bf16[704,768]{1,0:T(8,128)(2,1)S(1)}, f32[4,4,176,176]{3,2,1,0:T(8,128)S(1)}, bf16[2,176,256]{2,1,0:T(8,128)(2,1)S(1)}) custom-call(s32[2]{0:T(128)S(1)} %pad_add_fusion.at.at_ref, ...), custom_call_target="tpu_custom_call", output_to_operand_aliasing={{0}: (7, {}), {1}: (8, {}), {2}: (9, {})} | custom-call | tf_op jit(solution)/shard_map/pallas_call | solution.py:31
  103.4 9.3 %collective-permute-done.32.x0 = bf16[176,1024]{1,0:T(8,128)(2,1)S(1)} collective-permute-done((bf16[176,1024]{1,0:T(8,128)(2,1)S(1)}, bf16[176,1024]{1,0:T(8,128)(2,1)S(1)}, u32[]{:S(2)}, u32[]{:S(2)}) %collective-permute-start.32) | collective-permute-done | bytes 360480 | tf_op jit(solution)/shard_map/ppermute | solution.py:65
  114.2 2.5 shard_map.326
  116.7 2.5 shard_map.327
  123.9 7.7 %collective-permute-done.35.got_y = bf16[176,1024]{1,0:T(8,128)(2,1)S(1)} collective-permute-done((bf16[176,1024]{1,0:T(8,128)(2,1)S(1)}, bf16[176,1024]{1,0:T(8,128)(2,1)S(1)}, u32[]{:S(2)}, u32[]{:S(2)}) %collective-permute-start.35) | collective-permute-done | bytes 360480 | tf_op jit(solution)/shard_map/ppermute | solution.py:65
  134.8 7.9 %collective-permute-done.38.g0 = bf16[176,1024]{1,0:T(8,128)(2,1)S(1)} collective-permute-done((bf16[176,1024]{1,0:T(8,128)(2,1)S(1)}, bf16[176,1024]{1,0:T(8,128)(2,1)S(1)}, u32[]{:S(2)}, u32[]{:S(2)}) %collective-permute-start.38) | collective-permute-done | bytes 360480 | tf_op jit(solution)/shard_map/ppermute | solution.py:65
  145.1 2.4 shard_map.332
  165.6 4.0 %shard_map.340 = (bf16[704,768]{1,0:T(8,128)(2,1)S(1)}, f32[4,768]{1,0:T(4,128)S(1)}, f32[3,128,512]{2,1,0:T(8,128)S(1)}) custom-call(bf16[704,768]{1,0:T(8,128)(2,1)S(1)} %get-tuple-element.648.qkv_ref, f32[4,4,176,176]{3,2,1,0:T(8,128)S(1)} %get-tuple-element.649.probs_ref, bf16[176,256]{1,0:T(8,128)(2,1)S(1)} %get-tuple-element.639.g0, ...), custom_call_target="tpu_custom_call" | custom-call | flops 6000000000 | tf_op jit(solution)/shard_map/pallas_call | solution.py:31
  170.9 4.1 %shard_map.343 = (bf16[704,768]{1,0:T(8,128)(2,1)S(1)}, f32[4,768]{1,0:T(4,128)S(1)}, f32[3,128,512]{2,1,0:T(8,128)S(1)}, f32[12,256]{1,0:T(8,128)S(1)}) custom-call(bf16[704,768]{1,0:T(8,128)(2,1)S(1)} %get-tuple-element.648.qkv_ref, ...), custom_call_target="tpu_custom_call", output_to_operand_aliasing={{0}: (5, {}), {1}: (6, {}), {2}: (7, {})} | custom-call | tf_op jit(solution)/shard_map/pallas_call | solution.py:31
  183.3 2.7 %shard_map.348 = bf16[1024,128]{1,0:T(8,128)(2,1)S(1)} custom-call(s32[2]{0:T(128)S(1)} %pad_add_fusion.at.at_ref, f32[12,256]{1,0:T(8,128)S(1)} %get-tuple-element.668.ext_ref, f32[4,768]{1,0:T(4,128)S(1)} %get-tuple-element.669.sums_ref, f32[2,1024]{1,0:T(2,128)S(1)} %get-tuple-element.670.up_ref, f32[3,1024]{1,0:T(4,128)S(1)} %get-tuple-element.671.one_ref, ...), custom_call_target="tpu_custom_call" | custom-call | tf_op jit(solution)/shard_map/pallas_call | solution.py:31
  188.1 3.7 %collective-permute-done.53 = bf16[1024,256]{1,0:T(8,128)(2,1)S(1)} collective-permute-done((bf16[1024,256]{1,0:T(8,128)(2,1)S(1)}, bf16[1024,256]{1,0:T(8,128)(2,1)S(1)}, u32[]{:S(2)}, u32[]{:S(2)}) %collective-permute-start.53) | collective-permute-done | bytes 524320 | tf_op jit(solution)/shard_map/ppermute | solution.py:65
  193.2 2.6 collective-permute-done.50.refs_1_
  200.8 9.1 %collective-permute-done.54.refs_2_ = bf16[2,128,768]{2,1,0:T(8,128)(2,1)S(1)} collective-permute-done((bf16[2,128,768]{2,1,0:T(8,128)(2,1)S(1)}, bf16[2,128,768]{2,1,0:T(8,128)(2,1)S(1)}, u32[]{:S(2)}, u32[]{:S(2)}) %collective-permute-start.54) | collective-permute-done | bytes 393248 | tf_op jit(solution)/shard_map/ppermute | solution.py:65
  209.9 2.7 %collective-permute-start.59 = (bf16[128,768]{1,0:T(8,128)(2,1)S(1)}, bf16[128,768]{1,0:T(8,128)(2,1)S(1)}, u32[]{:S(2)}, u32[]{:S(2)}) collective-permute-start(bf16[128,768]{1,0:T(8,128)(2,1)S(1)} %shard_map.353), channel_id=1, source_target_pairs={{0,16},{4,20},{8,24},{12,28},{16,0},{20,4},{24,8},{28,12},{1,17},{... | collective-permute-start | bytes 589832 | tf_op jit(solution)/shard_map/ppermute | solution.py:65
  212.7 6.5 %collective-permute-done.57.refs_4_ = bf16[2,2,128,384]{3,2,1,0:T(8,128)(2,1)S(1)} collective-permute-done((bf16[2,2,128,384]{3,2,1,0:T(8,128)(2,1)S(1)}, bf16[2,2,128,384]{3,2,1,0:T(8,128)(2,1)S(1)}, u32[]{:S(2)}, u32[]{:S(2)}) %collective-permute-start.57) | collective-permute-done | bytes 393248 | tf_op jit(solution)/shard_map/ppermute | solution.py:65
  219.6 3.8 %collective-permute-done.59.refs_3_ = bf16[128,768]{1,0:T(8,128)(2,1)S(1)} collective-permute-done((bf16[128,768]{1,0:T(8,128)(2,1)S(1)}, bf16[128,768]{1,0:T(8,128)(2,1)S(1)}, u32[]{:S(2)}, u32[]{:S(2)}) %collective-permute-start.59) | collective-permute-done | bytes 196640 | tf_op jit(solution)/shard_map/ppermute | solution.py:65
  228.6 6.6 %collective-permute-done.61.refs_5_ = bf16[2,128,384]{2,1,0:T(8,128)(2,1)S(1)} collective-permute-done((bf16[2,128,384]{2,1,0:T(8,128)(2,1)S(1)}, bf16[2,128,384]{2,1,0:T(8,128)(2,1)S(1)}, u32[]{:S(2)}, u32[]{:S(2)}) %collective-permute-start.61) | collective-permute-done | bytes 196640 | tf_op jit(solution)/shard_map/ppermute | solution.py:65
  235.8 7.8 %collective-permute-done.60.refs_3_ = bf16[128,1024]{1,0:T(8,128)(2,1)S(1)} collective-permute-done((bf16[128,1024]{1,0:T(8,128)(2,1)S(1)}, bf16[128,1024]{1,0:T(8,128)(2,1)S(1)}, u32[]{:S(2)}, u32[]{:S(2)}) %collective-permute-start.60) | collective-permute-done | bytes 262176 | tf_op jit(solution)/shard_map/ppermute | solution.py:65
  251.8 2.7 %collective-permute-done.66.other = bf16[2,32,1408]{2,1,0:T(8,128)(2,1)S(1)} collective-permute-done((bf16[2,32,1408]{2,1,0:T(8,128)(2,1)S(1)}, bf16[2,32,1408]{2,1,0:T(8,128)(2,1)S(1)}, u32[]{:S(2)}, u32[]{:S(2)}) %collective-permute-start.66) | collective-permute-done | bytes 180256 | tf_op jit(solution)/shard_map/ppermute | solution.py:65
  (225 shorter events, 100.1 us)
Async XLA Ops:
  18.5 15.7 %collective-permute-start.5 = (bf16[128,1024]{1,0:T(8,128)(2,1)S(1)}, bf16[128,1024]{1,0:T(8,128)(2,1)S(1)}, u32[]{:S(2)}, u32[]{:S(2)}) collective-permute-start(bf16[128,1024]{1,0:T(8,128)(2,1)S(1)} %bitcast.69), channel_id=1, source_target_pairs={{0,16},{4,20},{8,24},{12,28},{16,0},{20,4},{24,8},{28,12},{1,17},{... | collective-permute-start | bytes 786440 | tf_op jit(solution)/shard_map/ppermute | solution.py:65
  34.2 20.9 %collective-permute-start.10 = (bf16[256,1024]{1,0:T(8,128)(2,1)S(1)}, bf16[256,1024]{1,0:T(8,128)(2,1)S(1)}, u32[]{:S(2)}, u32[]{:S(2)}) collective-permute-start(bf16[256,1024]{1,0:T(8,128)(2,1)S(1)} %shard_map.309.m), channel_id=1, source_target_pairs={{0,8},{4,12},{8,0},{12,4},{16,24},{20,28},{24,16},{28,20},{1,9},{5... | collective-permute-start | bytes 1572872 | tf_op jit(solution)/shard_map/ppermute | solution.py:65
  35.2 17.8 %collective-permute-start.11 = (bf16[128,1024]{1,0:T(8,128)(2,1)S(1)}, bf16[128,1024]{1,0:T(8,128)(2,1)S(1)}, u32[]{:S(2)}, u32[]{:S(2)}) collective-permute-start(bf16[128,1024]{1,0:T(8,128)(2,1)S(1)} %bitcast.78), channel_id=1, source_target_pairs={{0,16},{4,20},{8,24},{12,28},{16,0},{20,4},{24,8},{28,12},{1,17},{... | collective-permute-start | bytes 786440 | tf_op jit(solution)/shard_map/ppermute | solution.py:65
  38.5 14.5 %collective-permute-start.14 = (bf16[256,128]{1,0:T(8,128)(2,1)S(1)}, bf16[256,128]{1,0:T(8,128)(2,1)S(1)}, u32[]{:S(2)}, u32[]{:S(2)}) collective-permute-start(bf16[256,128]{1,0:T(8,128)(2,1)S(1)} %shard_map.308.m), channel_id=1, source_target_pairs={{0,16},{4,20},{8,24},{12,28},{16,0},{20,4},{24,8},{28,12},{1,17},{... | collective-permute-start | bytes 196616 | tf_op jit(solution)/shard_map/ppermute | solution.py:65
  55.2 28.0 %collective-permute-start.15 = (bf16[512,1024]{1,0:T(8,128)(2,1)S(1)}, bf16[512,1024]{1,0:T(8,128)(2,1)S(1)}, u32[]{:S(2)}, u32[]{:S(2)}) collective-permute-start(bf16[512,1024]{1,0:T(8,128)(2,1)S(1)} %shard_map.312.refs_0_.near_ref), channel_id=1, source_target_pairs={{0,4},{4,0},{8,12},{12,8},{16,20},{20,16},{24,28},{28,24},{1,5},{5... | collective-permute-start | bytes 3145736 | tf_op jit(solution)/shard_map/ppermute | solution.py:65
  56.8 13.6 %collective-permute-start.16 = (bf16[128,1024]{1,0:T(8,128)(2,1)S(1)}, bf16[128,1024]{1,0:T(8,128)(2,1)S(1)}, u32[]{:S(2)}, u32[]{:S(2)}) collective-permute-start(bf16[128,1024]{1,0:T(8,128)(2,1)S(1)} %bitcast.76), channel_id=1, source_target_pairs={{0,16},{4,20},{8,24},{12,28},{16,0},{20,4},{24,8},{28,12},{1,17},{... | collective-permute-start | bytes 786440 | tf_op jit(solution)/shard_map/ppermute | solution.py:65
  70.4 12.7 %collective-permute-start.17 = (bf16[256,1024]{1,0:T(8,128)(2,1)S(1)}, bf16[256,1024]{1,0:T(8,128)(2,1)S(1)}, u32[]{:S(2)}, u32[]{:S(2)}) collective-permute-start(bf16[256,1024]{1,0:T(8,128)(2,1)S(1)} %shard_map.316.m), channel_id=1, source_target_pairs={{0,8},{4,12},{8,0},{12,4},{16,24},{20,28},{24,16},{28,20},{1,9},{5... | collective-permute-start | bytes 1572872 | tf_op jit(solution)/shard_map/ppermute | solution.py:65
  71.0 21.7 %collective-permute-start.21 = (bf16[256,1024]{1,0:T(8,128)(2,1)S(1)}, bf16[256,1024]{1,0:T(8,128)(2,1)S(1)}, u32[]{:S(2)}, u32[]{:S(2)}) collective-permute-start(bf16[256,1024]{1,0:T(8,128)(2,1)S(1)} %shard_map.311.m), channel_id=1, source_target_pairs={{0,4},{4,0},{8,12},{12,8},{16,20},{20,16},{24,28},{28,24},{1,5},{5... | collective-permute-start | bytes 1572872 | tf_op jit(solution)/shard_map/ppermute | solution.py:65
  71.3 11.9 %collective-permute-start.18 = (bf16[512,256]{1,0:T(8,128)(2,1)S(1)}, bf16[512,256]{1,0:T(8,128)(2,1)S(1)}, u32[]{:S(2)}, u32[]{:S(2)}) collective-permute-start(bf16[512,256]{1,0:T(8,128)(2,1)S(1)} %shard_map.317.rest_0_), channel_id=1, source_target_pairs={{0,1},{1,0},{2,3},{3,2},{4,5},{5,4},{6,7},{7,6},{8,9},{9,8},{10,11... | collective-permute-start | bytes 786440 | tf_op jit(solution)/shard_map/ppermute | solution.py:65
  83.3 11.2 %collective-permute-start.26 = (bf16[512,256]{1,0:T(8,128)(2,1)S(1)}, bf16[512,256]{1,0:T(8,128)(2,1)S(1)}, u32[]{:S(2)}, u32[]{:S(2)}) collective-permute-start(bf16[512,256]{1,0:T(8,128)(2,1)S(1)} %shard_map.319.rest_4_), channel_id=1, source_target_pairs={{0,2},{1,3},{2,0},{3,1},{4,6},{5,7},{6,4},{7,5},{8,10},{9,11},{10,... | collective-permute-start | bytes 786440 | tf_op jit(solution)/shard_map/ppermute | solution.py:65
  86.5 11.6 %collective-permute-start.23 = (bf16[2,176,256]{2,1,0:T(8,128)(2,1)S(1)}, bf16[2,176,256]{2,1,0:T(8,128)(2,1)S(1)}, u32[]{:S(2)}, u32[]{:S(2)}) collective-permute-start(bf16[2,176,256]{2,1,0:T(8,128)(2,1)S(1)} %get-tuple-element.486), channel_id=1, source_target_pairs={{0,2},{1,3},{2,0},{3,1},{4,6},{5,7},{6,4},{7,5},{8,10},{9,11},{10,... | collective-permute-start | bytes 540680 | tf_op jit(solution)/shard_map/ppermute | solution.py:65
  88.5 24.7 %collective-permute-start.29 = (bf16[512,1024]{1,0:T(8,128)(2,1)S(1)}, bf16[512,1024]{1,0:T(8,128)(2,1)S(1)}, u32[]{:S(2)}, u32[]{:S(2)}) collective-permute-start(bf16[512,1024]{1,0:T(8,128)(2,1)S(1)} %shard_map.318.up_near), channel_id=1, source_target_pairs={{0,4},{4,0},{8,12},{12,8},{16,20},{20,16},{24,28},{28,24},{1,5},{5... | collective-permute-start | bytes 3145736 | tf_op jit(solution)/shard_map/ppermute | solution.py:65
  92.7 21.5 %collective-permute-start.30 = (bf16[512,1024]{1,0:T(8,128)(2,1)S(1)}, bf16[512,1024]{1,0:T(8,128)(2,1)S(1)}, u32[]{:S(2)}, u32[]{:S(2)}) collective-permute-start(bf16[512,1024]{1,0:T(8,128)(2,1)S(1)} %shard_map.321.down_near), channel_id=1, source_target_pairs={{0,8},{4,12},{8,0},{12,4},{16,24},{20,28},{24,16},{28,20},{1,9},{5... | collective-permute-start | bytes 3145736 | tf_op jit(solution)/shard_map/ppermute | solution.py:65
  121.1 10.6 %collective-permute-start.35 = (bf16[176,1024]{1,0:T(8,128)(2,1)S(1)}, bf16[176,1024]{1,0:T(8,128)(2,1)S(1)}, u32[]{:S(2)}, u32[]{:S(2)}) collective-permute-start(bf16[176,1024]{1,0:T(8,128)(2,1)S(1)} %shard_map.328), channel_id=1, source_target_pairs={{0,2},{1,3},{2,0},{3,1},{4,6},{5,7},{6,4},{7,5},{8,10},{9,11},{10,... | collective-permute-start | bytes 1081352 | tf_op jit(solution)/shard_map/ppermute | solution.py:65
  148.0 12.1 %collective-permute-start.37 = (bf16[176,1024]{1,0:T(8,128)(2,1)S(1)}, bf16[176,1024]{1,0:T(8,128)(2,1)S(1)}, u32[]{:S(2)}, u32[]{:S(2)}) collective-permute-start(bf16[176,1024]{1,0:T(8,128)(2,1)S(1)} %get-tuple-element.578), channel_id=1, source_target_pairs={{0,1},{1,0},{2,3},{3,2},{4,5},{5,4},{6,7},{7,6},{8,9},{9,8},{10,11... | collective-permute-start | bytes 1081352 | tf_op jit(solution)/shard_map/ppermute | solution.py:65
  149.4 10.8 %collective-permute-start.41 = (bf16[176,1024]{1,0:T(8,128)(2,1)S(1)}, bf16[176,1024]{1,0:T(8,128)(2,1)S(1)}, u32[]{:S(2)}, u32[]{:S(2)}) collective-permute-start(bf16[176,1024]{1,0:T(8,128)(2,1)S(1)} %shard_map.333), channel_id=1, source_target_pairs={{0,2},{1,3},{2,0},{3,1},{4,6},{5,7},{6,4},{7,5},{8,10},{9,11},{10,... | collective-permute-start | bytes 1081352 | tf_op jit(solution)/shard_map/ppermute | solution.py:65
  153.2 25.6 %collective-permute-start.47 = (bf16[2,2,128,1024]{3,2,1,0:T(8,128)(2,1)S(1)}, bf16[2,2,128,1024]{3,2,1,0:T(8,128)(2,1)S(1)}, u32[]{:S(2)}, u32[]{:S(2)}) collective-permute-start(bf16[2,2,128,1024]{3,2,1,0:T(8,128)(2,1)S(1)} %bitcast.72), channel_id=1, source_target_pairs={{0,4},{4,0},{8,12},{12,8},{16,20},{20,16},{24,28},{28,24},{1,5},{5... | collective-permute-start | bytes 3145736 | tf_op jit(solution)/shard_map/ppermute | solution.py:65
  154.8 24.9 %collective-permute-start.46 = (bf16[2,2,128,1024]{3,2,1,0:T(8,128)(2,1)S(1)}, bf16[2,2,128,1024]{3,2,1,0:T(8,128)(2,1)S(1)}, u32[]{:S(2)}, u32[]{:S(2)}) collective-permute-start(bf16[2,2,128,1024]{3,2,1,0:T(8,128)(2,1)S(1)} %bitcast.71), channel_id=1, source_target_pairs={{0,8},{4,12},{8,0},{12,4},{16,24},{20,28},{24,16},{28,20},{1,9},{5... | collective-permute-start | bytes 3145736 | tf_op jit(solution)/shard_map/ppermute | solution.py:65
  175.9 19.9 %collective-permute-start.50 = (bf16[2,2,128,768]{3,2,1,0:T(8,128)(2,1)S(1)}, bf16[2,2,128,768]{3,2,1,0:T(8,128)(2,1)S(1)}, u32[]{:S(2)}, u32[]{:S(2)}) collective-permute-start(bf16[2,2,128,768]{3,2,1,0:T(8,128)(2,1)S(1)} %bitcast.74), channel_id=1, source_target_pairs={{0,4},{4,0},{8,12},{12,8},{16,20},{20,16},{24,28},{28,24},{1,5},{5... | collective-permute-start | bytes 2359304 | tf_op jit(solution)/shard_map/ppermute | solution.py:65
  177.5 10.6 %collective-permute-start.52 = (bf16[1024,256]{1,0:T(8,128)(2,1)S(1)}, bf16[1024,256]{1,0:T(8,128)(2,1)S(1)}, u32[]{:S(2)}, u32[]{:S(2)}) collective-permute-start(bf16[1024,256]{1,0:T(8,128)(2,1)S(1)} %get-tuple-element.634), channel_id=1, source_target_pairs={{0,1},{1,0},{2,3},{3,2},{4,5},{5,4},{6,7},{7,6},{8,9},{9,8},{10,11... | collective-permute-start | bytes 1572872 | tf_op jit(solution)/shard_map/ppermute | solution.py:65
  177.5 14.3 %collective-permute-start.53 = (bf16[1024,256]{1,0:T(8,128)(2,1)S(1)}, bf16[1024,256]{1,0:T(8,128)(2,1)S(1)}, u32[]{:S(2)}, u32[]{:S(2)}) collective-permute-start(bf16[1024,256]{1,0:T(8,128)(2,1)S(1)} %shard_map.342), channel_id=1, source_target_pairs={{0,2},{1,3},{2,0},{3,1},{4,6},{5,7},{6,4},{7,5},{8,10},{9,11},{10,... | collective-permute-start | bytes 1572872 | tf_op jit(solution)/shard_map/ppermute | solution.py:65
  179.8 13.3 %collective-permute-start.51 = (bf16[2,128,1024]{2,1,0:T(8,128)(2,1)S(1)}, bf16[2,128,1024]{2,1,0:T(8,128)(2,1)S(1)}, u32[]{:S(2)}, u32[]{:S(2)}) collective-permute-start(bf16[2,128,1024]{2,1,0:T(8,128)(2,1)S(1)} %shard_map.345), channel_id=1, source_target_pairs={{0,8},{4,12},{8,0},{12,4},{16,24},{20,28},{24,16},{28,20},{1,9},{5... | collective-permute-start | bytes 1572872 | tf_op jit(solution)/shard_map/ppermute | solution.py:65
  195.9 14.0 %collective-permute-start.54 = (bf16[2,128,768]{2,1,0:T(8,128)(2,1)S(1)}, bf16[2,128,768]{2,1,0:T(8,128)(2,1)S(1)}, u32[]{:S(2)}, u32[]{:S(2)}) collective-permute-start(bf16[2,128,768]{2,1,0:T(8,128)(2,1)S(1)} %shard_map.352), channel_id=1, source_target_pairs={{0,8},{4,12},{8,0},{12,4},{16,24},{20,28},{24,16},{28,20},{1,9},{5... | collective-permute-start | bytes 1179656 | tf_op jit(solution)/shard_map/ppermute | solution.py:65
  197.7 15.0 %collective-permute-start.56 = (bf16[2,128,1024]{2,1,0:T(8,128)(2,1)S(1)}, bf16[2,128,1024]{2,1,0:T(8,128)(2,1)S(1)}, u32[]{:S(2)}, u32[]{:S(2)}) collective-permute-start(bf16[2,128,1024]{2,1,0:T(8,128)(2,1)S(1)} %shard_map.346), channel_id=1, source_target_pairs={{0,4},{4,0},{8,12},{12,8},{16,20},{20,16},{24,28},{28,24},{1,5},{5... | collective-permute-start | bytes 1572872 | tf_op jit(solution)/shard_map/ppermute | solution.py:65
  199.2 20.0 %collective-permute-start.57 = (bf16[2,2,128,384]{3,2,1,0:T(8,128)(2,1)S(1)}, bf16[2,2,128,384]{3,2,1,0:T(8,128)(2,1)S(1)}, u32[]{:S(2)}, u32[]{:S(2)}) collective-permute-start(bf16[2,2,128,384]{3,2,1,0:T(8,128)(2,1)S(1)} %shard_map.350), channel_id=1, source_target_pairs={{0,4},{4,0},{8,12},{12,8},{16,20},{20,16},{24,28},{28,24},{1,5},{5... | collective-permute-start | bytes 1179656 | tf_op jit(solution)/shard_map/ppermute | solution.py:65
  199.7 12.9 %collective-permute-start.49 = (bf16[176,1024]{1,0:T(8,128)(2,1)S(1)}, bf16[176,1024]{1,0:T(8,128)(2,1)S(1)}, u32[]{:S(2)}, u32[]{:S(2)}) collective-permute-start(bf16[176,1024]{1,0:T(8,128)(2,1)S(1)} %get-tuple-element.680), channel_id=1, source_target_pairs={{0,1},{1,0},{2,3},{3,2},{4,5},{5,4},{6,7},{7,6},{8,9},{9,8},{10,11... | collective-permute-start | bytes 1081352 | tf_op jit(solution)/shard_map/ppermute | solution.py:65
  199.7 19.9 %collective-permute-start.58 = (bf16[128,1024]{1,0:T(8,128)(2,1)S(1)}, bf16[128,1024]{1,0:T(8,128)(2,1)S(1)}, u32[]{:S(2)}, u32[]{:S(2)}) collective-permute-start(bf16[128,1024]{1,0:T(8,128)(2,1)S(1)} %shard_map.351), channel_id=1, source_target_pairs={{0,16},{4,20},{8,24},{12,28},{16,0},{20,4},{24,8},{28,12},{1,17},{... | collective-permute-start | bytes 786440 | tf_op jit(solution)/shard_map/ppermute | solution.py:65
  209.9 13.5 %collective-permute-start.59 = (bf16[128,768]{1,0:T(8,128)(2,1)S(1)}, bf16[128,768]{1,0:T(8,128)(2,1)S(1)}, u32[]{:S(2)}, u32[]{:S(2)}) collective-permute-start(bf16[128,768]{1,0:T(8,128)(2,1)S(1)} %shard_map.353), channel_id=1, source_target_pairs={{0,16},{4,20},{8,24},{12,28},{16,0},{20,4},{24,8},{28,12},{1,17},{... | collective-permute-start | bytes 589832 | tf_op jit(solution)/shard_map/ppermute | solution.py:65
  224.5 11.3 %collective-permute-start.55 = (bf16[176,1024]{1,0:T(8,128)(2,1)S(1)}, bf16[176,1024]{1,0:T(8,128)(2,1)S(1)}, u32[]{:S(2)}, u32[]{:S(2)}) collective-permute-start(bf16[176,1024]{1,0:T(8,128)(2,1)S(1)} %shard_map.354), channel_id=1, source_target_pairs={{0,2},{1,3},{2,0},{3,1},{4,6},{5,7},{6,4},{7,5},{8,10},{9,11},{10,... | collective-permute-start | bytes 1081352 | tf_op jit(solution)/shard_map/ppermute | solution.py:65
  225.8 17.8 %collective-permute-start.60 = (bf16[128,1024]{1,0:T(8,128)(2,1)S(1)}, bf16[128,1024]{1,0:T(8,128)(2,1)S(1)}, u32[]{:S(2)}, u32[]{:S(2)}) collective-permute-start(bf16[128,1024]{1,0:T(8,128)(2,1)S(1)} %shard_map.356), channel_id=1, source_target_pairs={{0,16},{4,20},{8,24},{12,28},{16,0},{20,4},{24,8},{28,12},{1,17},{... | collective-permute-start | bytes 786440 | tf_op jit(solution)/shard_map/ppermute | solution.py:65
  227.7 17.2 %collective-permute-start.64 = (bf16[2,32,1792]{2,1,0:T(8,128)(2,1)S(1)}, bf16[2,32,1792]{2,1,0:T(8,128)(2,1)S(1)}, u32[]{:S(2)}, u32[]{:S(2)}) collective-permute-start(bf16[2,32,1792]{2,1,0:T(8,128)(2,1)S(1)} %get-tuple-element.719), channel_id=1, source_target_pairs={{0,2},{1,3},{2,0},{3,1},{4,6},{5,7},{6,4},{7,5},{8,10},{9,11},{10,... | collective-permute-start | bytes 688136 | tf_op jit(solution)/shard_map/ppermute | solution.py:65
  228.6 17.3 %collective-permute-start.48 = (bf16[176,1024]{1,0:T(8,128)(2,1)S(1)}, bf16[176,1024]{1,0:T(8,128)(2,1)S(1)}, u32[]{:S(2)}, u32[]{:S(2)}) collective-permute-start(bf16[176,1024]{1,0:T(8,128)(2,1)S(1)} %get-tuple-element.678), channel_id=1, source_target_pairs={{0,1},{1,0},{2,3},{3,2},{4,5},{5,4},{6,7},{7,6},{8,9},{9,8},{10,11... | collective-permute-start | bytes 1081352 | tf_op jit(solution)/shard_map/ppermute | solution.py:65
  (52 other events, 382.2 us)

commit v6 on v5

--- a/solution.py
+++ b/solution.py
@@ -957,8 +957,8 @@
         (made,) = run(lambda *ins: call(partial(half_grad_kernel, near), ins, [out]), left, right)
         return made
 
+    give = half_grad(d_ffn_group, act_low, False)
     meet.send()
-    give = half_grad(d_ffn_group, act_low, False)
     s_down = Scatter(run, (give,), "dp", X_Z, given=give).send()
     give = half_grad(normed_group, d_pre, False)
     s_up = Scatter(run, (give,), "dp", Z_X, given=give).send()

time: 257 us -> 257 us (level)
  no operation moved by 1% of the time
where the time goes in v6:
time: 257 us; the launch traced here: 256 us
  waiting for transfers between devices  131 us (51%)
  Pallas kernels  60.2 us (23%)
  starting transfers between devices  56.2 us (22%)
  local copies, waits for them, and re-layouts  5.66 us (2%)
    ppermute x67, waiting for transfers between devices, swap(): lax.ppermute(x, axis, [(i, i ^ b) for i in range(lax.axis_size(axis))])  131 us
    ppermute x67, starting transfers between devices, swap(): lax.ppermute(x, axis, [(i, i ^ b) for i in range(lax.axis_size(axis))])  56.2 us
    pallas_call x70, Pallas kernels, call(): pl.pallas_call(kernel, in_specs=[pl.BlockSpec(memory_space=m) for m in sp...  56.2 us
    unnamed x35, local copies, waits for them, and re-layouts  5.29 us
  transfers between devices with their start and end apart: 67, of which 35 were waited for; matrix products, arithmetic and copies ran while one was open for 1% of the time, Pallas kernels for 19%

profile of v6, /device:TPU:0, one launch (start us, length us, event | category | flops | bytes accessed | tf_op | source)
XLA Modules:
  0.0 256.4 jit_solution(11815249290498972987)
XLA Ops:
  7.6 3.0 %collective-permute-start.3 = (bf16[2,32,1024]{2,1,0:T(8,128)(2,1)S(1)}, bf16[2,32,1024]{2,1,0:T(8,128)(2,1)S(1)}, u32[]{:S(2)}, u32[]{:S(2)}) collective-permute-start(bf16[2,32,1024]{2,1,0:T(8,128)(2,1)S(1)} %get-tuple-element.406), channel_id=1, source_target_pairs={{0,2},{1,3},{2,0},{3,1},{4,6},{5,7},{6,4},{7,5},{8,10},{9,11},{10,... | collective-permute-start | bytes 393224 | tf_op jit(solution)/shard_map/ppermute | solution.py:65
  11.9 2.4 collective-permute-done.3.other
  18.5 2.7 %collective-permute-start.5 = (bf16[128,1024]{1,0:T(8,128)(2,1)S(1)}, bf16[128,1024]{1,0:T(8,128)(2,1)S(1)}, u32[]{:S(2)}, u32[]{:S(2)}) collective-permute-start(bf16[128,1024]{1,0:T(8,128)(2,1)S(1)} %bitcast.69), channel_id=1, source_target_pairs={{0,16},{4,20},{8,24},{12,28},{16,0},{20,4},{24,8},{28,12},{1,17},{... | collective-permute-start | bytes 786440 | tf_op jit(solution)/shard_map/ppermute | solution.py:65
  21.7 3.1 %collective-permute-done.6.o = bf16[32,128]{1,0:T(8,128)(2,1)S(1)} collective-permute-done((bf16[32,128]{1,0:T(8,128)(2,1)S(1)}, bf16[32,128]{1,0:T(8,128)(2,1)S(1)}, u32[]{:S(2)}, u32[]{:S(2)}) %collective-permute-start.6) | collective-permute-done | bytes 8224 | tf_op jit(solution)/shard_map/ppermute | solution.py:65
  30.6 3.5 %collective-permute-done.9.o = bf16[128,128]{1,0:T(8,128)(2,1)S(1)} collective-permute-done((bf16[128,128]{1,0:T(8,128)(2,1)S(1)}, bf16[128,128]{1,0:T(8,128)(2,1)S(1)}, u32[]{:S(2)}, u32[]{:S(2)}) %collective-permute-start.9) | collective-permute-done | bytes 32800 | tf_op jit(solution)/shard_map/ppermute | solution.py:65
  35.2 3.3 %collective-permute-start.11 = (bf16[128,1024]{1,0:T(8,128)(2,1)S(1)}, bf16[128,1024]{1,0:T(8,128)(2,1)S(1)}, u32[]{:S(2)}, u32[]{:S(2)}) collective-permute-start(bf16[128,1024]{1,0:T(8,128)(2,1)S(1)} %bitcast.78), channel_id=1, source_target_pairs={{0,16},{4,20},{8,24},{12,28},{16,0},{20,4},{24,8},{28,12},{1,17},{... | collective-permute-start | bytes 786440 | tf_op jit(solution)/shard_map/ppermute | solution.py:65
  38.5 14.4 %collective-permute-done.14.o = bf16[256,128]{1,0:T(8,128)(2,1)S(1)} collective-permute-done((bf16[256,128]{1,0:T(8,128)(2,1)S(1)}, bf16[256,128]{1,0:T(8,128)(2,1)S(1)}, u32[]{:S(2)}, u32[]{:S(2)}) %collective-permute-start.14) | collective-permute-done | bytes 65568 | tf_op jit(solution)/shard_map/ppermute | solution.py:65
  58.9 4.1 %shard_map.315.bias_ref = f32[4,4,176,176]{3,2,1,0:T(8,128)S(1)} custom-call(bf16[4,16,256]{2,1,0:T(8,128)(2,1)S(1)} %shard_map.310.notes_ref, f32[12,256]{1,0:T(8,128)S(1)} %get-tuple-element.468.ext_ref), custom_call_target="tpu_custom_call" | custom-call | tf_op jit(solution)/shard_map/pallas_call | solution.py:243
  62.9 7.5 %collective-permute-done.16.o = bf16[128,1024]{1,0:T(8,128)(2,1)S(1)} collective-permute-done((bf16[128,1024]{1,0:T(8,128)(2,1)S(1)}, bf16[128,1024]{1,0:T(8,128)(2,1)S(1)}, u32[]{:S(2)}, u32[]{:S(2)}) %collective-permute-start.16) | collective-permute-done | bytes 262176 | tf_op jit(solution)/shard_map/ppermute | solution.py:65
  71.3 6.4 %collective-permute-done.19.rest_2_ = bf16[512,256]{1,0:T(8,128)(2,1)S(1)} collective-permute-done((bf16[512,256]{1,0:T(8,128)(2,1)S(1)}, bf16[512,256]{1,0:T(8,128)(2,1)S(1)}, u32[]{:S(2)}, u32[]{:S(2)}) %collective-permute-start.19) | collective-permute-done | bytes 262176 | tf_op jit(solution)/shard_map/ppermute | solution.py:65
  77.8 5.4 %collective-permute-done.17.o = bf16[256,1024]{1,0:T(8,128)(2,1)S(1)} collective-permute-done((bf16[256,1024]{1,0:T(8,128)(2,1)S(1)}, bf16[256,1024]{1,0:T(8,128)(2,1)S(1)}, u32[]{:S(2)}, u32[]{:S(2)}) %collective-permute-start.17) | collective-permute-done | bytes 524320 | tf_op jit(solution)/shard_map/ppermute | solution.py:65
  83.4 3.1 %shard_map.320 = (bf16[704,1024]{1,0:T(8,128)(2,1)S(1)}, bf16[704,768]{1,0:T(8,128)(2,1)S(1)}, f32[4,4,176,176]{3,2,1,0:T(8,128)S(1)}, bf16[2,176,256]{2,1,0:T(8,128)(2,1)S(1)}) custom-call(s32[2]{0:T(128)S(1)} %pad_add_fusion.at.at_ref, bf16[176,1024]{1,0:T(8,128)(2,1)S(1)} %collective-permute-done.12.refs_2_.d0, ...), custom_call_target="tpu_custom_call" | custom-call | tf_op jit(solution)/shard_map/pallas_call | solution.py:31
  89.1 3.6 %collective-permute-done.21.o = bf16[256,1024]{1,0:T(8,128)(2,1)S(1)} collective-permute-done((bf16[256,1024]{1,0:T(8,128)(2,1)S(1)}, bf16[256,1024]{1,0:T(8,128)(2,1)S(1)}, u32[]{:S(2)}, u32[]{:S(2)}) %collective-permute-start.21) | collective-permute-done | bytes 524320 | tf_op jit(solution)/shard_map/ppermute | solution.py:65
  95.0 3.1 %shard_map.322 = (bf16[704,1024]{1,0:T(8,128)(2,1)S(1)}, bf16[704,768]{1,0:T(8,128)(2,1)S(1)}, f32[4,4,176,176]{3,2,1,0:T(8,128)S(1)}, bf16[2,176,256]{2,1,0:T(8,128)(2,1)S(1)}) custom-call(s32[2]{0:T(128)S(1)} %pad_add_fusion.at.at_ref, ...), custom_call_target="tpu_custom_call", output_to_operand_aliasing={{0}: (7, {}), {1}: (8, {}), {2}: (9, {})} | custom-call | tf_op jit(solution)/shard_map/pallas_call | solution.py:31
  103.4 9.3 %collective-permute-done.32.x0 = bf16[176,1024]{1,0:T(8,128)(2,1)S(1)} collective-permute-done((bf16[176,1024]{1,0:T(8,128)(2,1)S(1)}, bf16[176,1024]{1,0:T(8,128)(2,1)S(1)}, u32[]{:S(2)}, u32[]{:S(2)}) %collective-permute-start.32) | collective-permute-done | bytes 360480 | tf_op jit(solution)/shard_map/ppermute | solution.py:65
  114.2 2.5 shard_map.326
  116.7 2.5 shard_map.327
  123.9 7.7 %collective-permute-done.35.got_y = bf16[176,1024]{1,0:T(8,128)(2,1)S(1)} collective-permute-done((bf16[176,1024]{1,0:T(8,128)(2,1)S(1)}, bf16[176,1024]{1,0:T(8,128)(2,1)S(1)}, u32[]{:S(2)}, u32[]{:S(2)}) %collective-permute-start.35) | collective-permute-done | bytes 360480 | tf_op jit(solution)/shard_map/ppermute | solution.py:65
  134.8 7.9 %collective-permute-done.38.g0 = bf16[176,1024]{1,0:T(8,128)(2,1)S(1)} collective-permute-done((bf16[176,1024]{1,0:T(8,128)(2,1)S(1)}, bf16[176,1024]{1,0:T(8,128)(2,1)S(1)}, u32[]{:S(2)}, u32[]{:S(2)}) %collective-permute-start.38) | collective-permute-done | bytes 360480 | tf_op jit(solution)/shard_map/ppermute | solution.py:65
  145.1 2.4 shard_map.332
  165.6 4.0 %shard_map.340 = (bf16[704,768]{1,0:T(8,128)(2,1)S(1)}, f32[4,768]{1,0:T(4,128)S(1)}, f32[3,128,512]{2,1,0:T(8,128)S(1)}) custom-call(bf16[704,768]{1,0:T(8,128)(2,1)S(1)} %get-tuple-element.648.qkv_ref, f32[4,4,176,176]{3,2,1,0:T(8,128)S(1)} %get-tuple-element.649.probs_ref, bf16[176,256]{1,0:T(8,128)(2,1)S(1)} %get-tuple-element.639.g0, ...), custom_call_target="tpu_custom_call" | custom-call | flops 6000000000 | tf_op jit(solution)/shard_map/pallas_call | solution.py:31
  170.9 4.1 %shard_map.343 = (bf16[704,768]{1,0:T(8,128)(2,1)S(1)}, f32[4,768]{1,0:T(4,128)S(1)}, f32[3,128,512]{2,1,0:T(8,128)S(1)}, f32[12,256]{1,0:T(8,128)S(1)}) custom-call(bf16[704,768]{1,0:T(8,128)(2,1)S(1)} %get-tuple-element.648.qkv_ref, ...), custom_call_target="tpu_custom_call", output_to_operand_aliasing={{0}: (5, {}), {1}: (6, {}), {2}: (7, {})} | custom-call | tf_op jit(solution)/shard_map/pallas_call | solution.py:31
  182.5 2.7 %shard_map.348 = bf16[1024,128]{1,0:T(8,128)(2,1)S(1)} custom-call(s32[2]{0:T(128)S(1)} %pad_add_fusion.at.at_ref, f32[12,256]{1,0:T(8,128)S(1)} %get-tuple-element.668.ext_ref, f32[4,768]{1,0:T(4,128)S(1)} %get-tuple-element.669.sums_ref, f32[2,1024]{1,0:T(2,128)S(1)} %get-tuple-element.670.up_ref, f32[3,1024]{1,0:T(4,128)S(1)} %get-tuple-element.671.one_ref, ...), custom_call_target="tpu_custom_call" | custom-call | tf_op jit(solution)/shard_map/pallas_call | solution.py:31
  187.3 4.5 %collective-permute-done.53 = bf16[1024,256]{1,0:T(8,128)(2,1)S(1)} collective-permute-done((bf16[1024,256]{1,0:T(8,128)(2,1)S(1)}, bf16[1024,256]{1,0:T(8,128)(2,1)S(1)}, u32[]{:S(2)}, u32[]{:S(2)}) %collective-permute-start.53) | collective-permute-done | bytes 524320 | tf_op jit(solution)/shard_map/ppermute | solution.py:65
  193.2 2.6 collective-permute-done.50.refs_1_
  200.8 9.1 %collective-permute-done.54.refs_2_ = bf16[2,128,768]{2,1,0:T(8,128)(2,1)S(1)} collective-permute-done((bf16[2,128,768]{2,1,0:T(8,128)(2,1)S(1)}, bf16[2,128,768]{2,1,0:T(8,128)(2,1)S(1)}, u32[]{:S(2)}, u32[]{:S(2)}) %collective-permute-start.54) | collective-permute-done | bytes 393248 | tf_op jit(solution)/shard_map/ppermute | solution.py:65
  209.9 2.7 %collective-permute-start.59 = (bf16[128,768]{1,0:T(8,128)(2,1)S(1)}, bf16[128,768]{1,0:T(8,128)(2,1)S(1)}, u32[]{:S(2)}, u32[]{:S(2)}) collective-permute-start(bf16[128,768]{1,0:T(8,128)(2,1)S(1)} %shard_map.353), channel_id=1, source_target_pairs={{0,16},{4,20},{8,24},{12,28},{16,0},{20,4},{24,8},{28,12},{1,17},{... | collective-permute-start | bytes 589832 | tf_op jit(solution)/shard_map/ppermute | solution.py:65
  212.7 6.5 %collective-permute-done.57.refs_4_ = bf16[2,2,128,384]{3,2,1,0:T(8,128)(2,1)S(1)} collective-permute-done((bf16[2,2,128,384]{3,2,1,0:T(8,128)(2,1)S(1)}, bf16[2,2,128,384]{3,2,1,0:T(8,128)(2,1)S(1)}, u32[]{:S(2)}, u32[]{:S(2)}) %collective-permute-start.57) | collective-permute-done | bytes 393248 | tf_op jit(solution)/shard_map/ppermute | solution.py:65
  219.6 3.8 %collective-permute-done.59.refs_3_ = bf16[128,768]{1,0:T(8,128)(2,1)S(1)} collective-permute-done((bf16[128,768]{1,0:T(8,128)(2,1)S(1)}, bf16[128,768]{1,0:T(8,128)(2,1)S(1)}, u32[]{:S(2)}, u32[]{:S(2)}) %collective-permute-start.59) | collective-permute-done | bytes 196640 | tf_op jit(solution)/shard_map/ppermute | solution.py:65
  228.6 6.6 %collective-permute-done.61.refs_5_ = bf16[2,128,384]{2,1,0:T(8,128)(2,1)S(1)} collective-permute-done((bf16[2,128,384]{2,1,0:T(8,128)(2,1)S(1)}, bf16[2,128,384]{2,1,0:T(8,128)(2,1)S(1)}, u32[]{:S(2)}, u32[]{:S(2)}) %collective-permute-start.61) | collective-permute-done | bytes 196640 | tf_op jit(solution)/shard_map/ppermute | solution.py:65
  235.8 7.8 %collective-permute-done.60.refs_3_ = bf16[128,1024]{1,0:T(8,128)(2,1)S(1)} collective-permute-done((bf16[128,1024]{1,0:T(8,128)(2,1)S(1)}, bf16[128,1024]{1,0:T(8,128)(2,1)S(1)}, u32[]{:S(2)}, u32[]{:S(2)}) %collective-permute-start.60) | collective-permute-done | bytes 262176 | tf_op jit(solution)/shard_map/ppermute | solution.py:65
  251.8 2.7 %collective-permute-done.66.other = bf16[2,32,1408]{2,1,0:T(8,128)(2,1)S(1)} collective-permute-done((bf16[2,32,1408]{2,1,0:T(8,128)(2,1)S(1)}, bf16[2,32,1408]{2,1,0:T(8,128)(2,1)S(1)}, u32[]{:S(2)}, u32[]{:S(2)}) %collective-permute-start.66) | collective-permute-done | bytes 180256 | tf_op jit(solution)/shard_map/ppermute | solution.py:65
  (225 shorter events, 99.3 us)
Async XLA Ops:
  18.5 15.7 %collective-permute-start.5 = (bf16[128,1024]{1,0:T(8,128)(2,1)S(1)}, bf16[128,1024]{1,0:T(8,128)(2,1)S(1)}, u32[]{:S(2)}, u32[]{:S(2)}) collective-permute-start(bf16[128,1024]{1,0:T(8,128)(2,1)S(1)} %bitcast.69), channel_id=1, source_target_pairs={{0,16},{4,20},{8,24},{12,28},{16,0},{20,4},{24,8},{28,12},{1,17},{... | collective-permute-start | bytes 786440 | tf_op jit(solution)/shard_map/ppermute | solution.py:65
  34.2 20.9 %collective-permute-start.10 = (bf16[256,1024]{1,0:T(8,128)(2,1)S(1)}, bf16[256,1024]{1,0:T(8,128)(2,1)S(1)}, u32[]{:S(2)}, u32[]{:S(2)}) collective-permute-start(bf16[256,1024]{1,0:T(8,128)(2,1)S(1)} %shard_map.309.m), channel_id=1, source_target_pairs={{0,8},{4,12},{8,0},{12,4},{16,24},{20,28},{24,16},{28,20},{1,9},{5... | collective-permute-start | bytes 1572872 | tf_op jit(solution)/shard_map/ppermute | solution.py:65
  35.2 17.8 %collective-permute-start.11 = (bf16[128,1024]{1,0:T(8,128)(2,1)S(1)}, bf16[128,1024]{1,0:T(8,128)(2,1)S(1)}, u32[]{:S(2)}, u32[]{:S(2)}) collective-permute-start(bf16[128,1024]{1,0:T(8,128)(2,1)S(1)} %bitcast.78), channel_id=1, source_target_pairs={{0,16},{4,20},{8,24},{12,28},{16,0},{20,4},{24,8},{28,12},{1,17},{... | collective-permute-start | bytes 786440 | tf_op jit(solution)/shard_map/ppermute | solution.py:65
  38.5 14.5 %collective-permute-start.14 = (bf16[256,128]{1,0:T(8,128)(2,1)S(1)}, bf16[256,128]{1,0:T(8,128)(2,1)S(1)}, u32[]{:S(2)}, u32[]{:S(2)}) collective-permute-start(bf16[256,128]{1,0:T(8,128)(2,1)S(1)} %shard_map.308.m), channel_id=1, source_target_pairs={{0,16},{4,20},{8,24},{12,28},{16,0},{20,4},{24,8},{28,12},{1,17},{... | collective-permute-start | bytes 196616 | tf_op jit(solution)/shard_map/ppermute | solution.py:65
  55.2 28.0 %collective-permute-start.15 = (bf16[512,1024]{1,0:T(8,128)(2,1)S(1)}, bf16[512,1024]{1,0:T(8,128)(2,1)S(1)}, u32[]{:S(2)}, u32[]{:S(2)}) collective-permute-start(bf16[512,1024]{1,0:T(8,128)(2,1)S(1)} %shard_map.312.refs_0_.near_ref), channel_id=1, source_target_pairs={{0,4},{4,0},{8,12},{12,8},{16,20},{20,16},{24,28},{28,24},{1,5},{5... | collective-permute-start | bytes 3145736 | tf_op jit(solution)/shard_map/ppermute | solution.py:65
  56.8 13.6 %collective-permute-start.16 = (bf16[128,1024]{1,0:T(8,128)(2,1)S(1)}, bf16[128,1024]{1,0:T(8,128)(2,1)S(1)}, u32[]{:S(2)}, u32[]{:S(2)}) collective-permute-start(bf16[128,1024]{1,0:T(8,128)(2,1)S(1)} %bitcast.76), channel_id=1, source_target_pairs={{0,16},{4,20},{8,24},{12,28},{16,0},{20,4},{24,8},{28,12},{1,17},{... | collective-permute-start | bytes 786440 | tf_op jit(solution)/shard_map/ppermute | solution.py:65
  70.4 12.7 %collective-permute-start.17 = (bf16[256,1024]{1,0:T(8,128)(2,1)S(1)}, bf16[256,1024]{1,0:T(8,128)(2,1)S(1)}, u32[]{:S(2)}, u32[]{:S(2)}) collective-permute-start(bf16[256,1024]{1,0:T(8,128)(2,1)S(1)} %shard_map.316.m), channel_id=1, source_target_pairs={{0,8},{4,12},{8,0},{12,4},{16,24},{20,28},{24,16},{28,20},{1,9},{5... | collective-permute-start | bytes 1572872 | tf_op jit(solution)/shard_map/ppermute | solution.py:65
  71.0 21.7 %collective-permute-start.21 = (bf16[256,1024]{1,0:T(8,128)(2,1)S(1)}, bf16[256,1024]{1,0:T(8,128)(2,1)S(1)}, u32[]{:S(2)}, u32[]{:S(2)}) collective-permute-start(bf16[256,1024]{1,0:T(8,128)(2,1)S(1)} %shard_map.311.m), channel_id=1, source_target_pairs={{0,4},{4,0},{8,12},{12,8},{16,20},{20,16},{24,28},{28,24},{1,5},{5... | collective-permute-start | bytes 1572872 | tf_op jit(solution)/shard_map/ppermute | solution.py:65
  71.3 11.9 %collective-permute-start.18 = (bf16[512,256]{1,0:T(8,128)(2,1)S(1)}, bf16[512,256]{1,0:T(8,128)(2,1)S(1)}, u32[]{:S(2)}, u32[]{:S(2)}) collective-permute-start(bf16[512,256]{1,0:T(8,128)(2,1)S(1)} %shard_map.317.rest_0_), channel_id=1, source_target_pairs={{0,1},{1,0},{2,3},{3,2},{4,5},{5,4},{6,7},{7,6},{8,9},{9,8},{10,11... | collective-permute-start | bytes 786440 | tf_op jit(solution)/shard_map/ppermute | solution.py:65
  83.3 11.2 %collective-permute-start.26 = (bf16[512,256]{1,0:T(8,128)(2,1)S(1)}, bf16[512,256]{1,0:T(8,128)(2,1)S(1)}, u32[]{:S(2)}, u32[]{:S(2)}) collective-permute-start(bf16[512,256]{1,0:T(8,128)(2,1)S(1)} %shard_map.319.rest_4_), channel_id=1, source_target_pairs={{0,2},{1,3},{2,0},{3,1},{4,6},{5,7},{6,4},{7,5},{8,10},{9,11},{10,... | collective-permute-start | bytes 786440 | tf_op jit(solution)/shard_map/ppermute | solution.py:65
  86.5 11.6 %collective-permute-start.23 = (bf16[2,176,256]{2,1,0:T(8,128)(2,1)S(1)}, bf16[2,176,256]{2,1,0:T(8,128)(2,1)S(1)}, u32[]{:S(2)}, u32[]{:S(2)}) collective-permute-start(bf16[2,176,256]{2,1,0:T(8,128)(2,1)S(1)} %get-tuple-element.486), channel_id=1, source_target_pairs={{0,2},{1,3},{2,0},{3,1},{4,6},{5,7},{6,4},{7,5},{8,10},{9,11},{10,... | collective-permute-start | bytes 540680 | tf_op jit(solution)/shard_map/ppermute | solution.py:65
  88.5 24.7 %collective-permute-start.29 = (bf16[512,1024]{1,0:T(8,128)(2,1)S(1)}, bf16[512,1024]{1,0:T(8,128)(2,1)S(1)}, u32[]{:S(2)}, u32[]{:S(2)}) collective-permute-start(bf16[512,1024]{1,0:T(8,128)(2,1)S(1)} %shard_map.318.up_near), channel_id=1, source_target_pairs={{0,4},{4,0},{8,12},{12,8},{16,20},{20,16},{24,28},{28,24},{1,5},{5... | collective-permute-start | bytes 3145736 | tf_op jit(solution)/shard_map/ppermute | solution.py:65
  92.7 21.5 %collective-permute-start.30 = (bf16[512,1024]{1,0:T(8,128)(2,1)S(1)}, bf16[512,1024]{1,0:T(8,128)(2,1)S(1)}, u32[]{:S(2)}, u32[]{:S(2)}) collective-permute-start(bf16[512,1024]{1,0:T(8,128)(2,1)S(1)} %shard_map.321.down_near), channel_id=1, source_target_pairs={{0,8},{4,12},{8,0},{12,4},{16,24},{20,28},{24,16},{28,20},{1,9},{5... | collective-permute-start | bytes 3145736 | tf_op jit(solution)/shard_map/ppermute | solution.py:65
  102.2 10.5 %collective-permute-start.32 = (bf16[176,1024]{1,0:T(8,128)(2,1)S(1)}, bf16[176,1024]{1,0:T(8,128)(2,1)S(1)}, u32[]{:S(2)}, u32[]{:S(2)}) collective-permute-start(bf16[176,1024]{1,0:T(8,128)(2,1)S(1)} %get-tuple-element.527.x0), channel_id=1, source_target_pairs={{0,2},{1,3},{2,0},{3,1},{4,6},{5,7},{6,4},{7,5},{8,10},{9,11},{10,... | collective-permute-start | bytes 1081352 | tf_op jit(solution)/shard_map/ppermute | solution.py:65
  121.1 10.6 %collective-permute-start.35 = (bf16[176,1024]{1,0:T(8,128)(2,1)S(1)}, bf16[176,1024]{1,0:T(8,128)(2,1)S(1)}, u32[]{:S(2)}, u32[]{:S(2)}) collective-permute-start(bf16[176,1024]{1,0:T(8,128)(2,1)S(1)} %shard_map.328), channel_id=1, source_target_pairs={{0,2},{1,3},{2,0},{3,1},{4,6},{5,7},{6,4},{7,5},{8,10},{9,11},{10,... | collective-permute-start | bytes 1081352 | tf_op jit(solution)/shard_map/ppermute | solution.py:65
  148.0 11.1 %collective-permute-start.37 = (bf16[176,1024]{1,0:T(8,128)(2,1)S(1)}, bf16[176,1024]{1,0:T(8,128)(2,1)S(1)}, u32[]{:S(2)}, u32[]{:S(2)}) collective-permute-start(bf16[176,1024]{1,0:T(8,128)(2,1)S(1)} %get-tuple-element.578), channel_id=1, source_target_pairs={{0,1},{1,0},{2,3},{3,2},{4,5},{5,4},{6,7},{7,6},{8,9},{9,8},{10,11... | collective-permute-start | bytes 1081352 | tf_op jit(solution)/shard_map/ppermute | solution.py:65
  149.4 10.8 %collective-permute-start.41 = (bf16[176,1024]{1,0:T(8,128)(2,1)S(1)}, bf16[176,1024]{1,0:T(8,128)(2,1)S(1)}, u32[]{:S(2)}, u32[]{:S(2)}) collective-permute-start(bf16[176,1024]{1,0:T(8,128)(2,1)S(1)} %shard_map.334), channel_id=1, source_target_pairs={{0,2},{1,3},{2,0},{3,1},{4,6},{5,7},{6,4},{7,5},{8,10},{9,11},{10,... | collective-permute-start | bytes 1081352 | tf_op jit(solution)/shard_map/ppermute | solution.py:65
  151.2 27.7 %collective-permute-start.46 = (bf16[2,2,128,1024]{3,2,1,0:T(8,128)(2,1)S(1)}, bf16[2,2,128,1024]{3,2,1,0:T(8,128)(2,1)S(1)}, u32[]{:S(2)}, u32[]{:S(2)}) collective-permute-start(bf16[2,2,128,1024]{3,2,1,0:T(8,128)(2,1)S(1)} %bitcast.71), channel_id=1, source_target_pairs={{0,8},{4,12},{8,0},{12,4},{16,24},{20,28},{24,16},{28,20},{1,9},{5... | collective-permute-start | bytes 3145736 | tf_op jit(solution)/shard_map/ppermute | solution.py:65
  154.0 24.9 %collective-permute-start.47 = (bf16[2,2,128,1024]{3,2,1,0:T(8,128)(2,1)S(1)}, bf16[2,2,128,1024]{3,2,1,0:T(8,128)(2,1)S(1)}, u32[]{:S(2)}, u32[]{:S(2)}) collective-permute-start(bf16[2,2,128,1024]{3,2,1,0:T(8,128)(2,1)S(1)} %bitcast.72), channel_id=1, source_target_pairs={{0,4},{4,0},{8,12},{12,8},{16,20},{20,16},{24,28},{28,24},{1,5},{5... | collective-permute-start | bytes 3145736 | tf_op jit(solution)/shard_map/ppermute | solution.py:65
  175.9 19.9 %collective-permute-start.50 = (bf16[2,2,128,768]{3,2,1,0:T(8,128)(2,1)S(1)}, bf16[2,2,128,768]{3,2,1,0:T(8,128)(2,1)S(1)}, u32[]{:S(2)}, u32[]{:S(2)}) collective-permute-start(bf16[2,2,128,768]{3,2,1,0:T(8,128)(2,1)S(1)} %bitcast.74), channel_id=1, source_target_pairs={{0,4},{4,0},{8,12},{12,8},{16,20},{20,16},{24,28},{28,24},{1,5},{5... | collective-permute-start | bytes 2359304 | tf_op jit(solution)/shard_map/ppermute | solution.py:65
  177.5 14.3 %collective-permute-start.53 = (bf16[1024,256]{1,0:T(8,128)(2,1)S(1)}, bf16[1024,256]{1,0:T(8,128)(2,1)S(1)}, u32[]{:S(2)}, u32[]{:S(2)}) collective-permute-start(bf16[1024,256]{1,0:T(8,128)(2,1)S(1)} %shard_map.342), channel_id=1, source_target_pairs={{0,2},{1,3},{2,0},{3,1},{4,6},{5,7},{6,4},{7,5},{8,10},{9,11},{10,... | collective-permute-start | bytes 1572872 | tf_op jit(solution)/shard_map/ppermute | solution.py:65
  179.0 14.1 %collective-permute-start.51 = (bf16[2,128,1024]{2,1,0:T(8,128)(2,1)S(1)}, bf16[2,128,1024]{2,1,0:T(8,128)(2,1)S(1)}, u32[]{:S(2)}, u32[]{:S(2)}) collective-permute-start(bf16[2,128,1024]{2,1,0:T(8,128)(2,1)S(1)} %shard_map.345), channel_id=1, source_target_pairs={{0,8},{4,12},{8,0},{12,4},{16,24},{20,28},{24,16},{28,20},{1,9},{5... | collective-permute-start | bytes 1572872 | tf_op jit(solution)/shard_map/ppermute | solution.py:65
  195.9 14.0 %collective-permute-start.54 = (bf16[2,128,768]{2,1,0:T(8,128)(2,1)S(1)}, bf16[2,128,768]{2,1,0:T(8,128)(2,1)S(1)}, u32[]{:S(2)}, u32[]{:S(2)}) collective-permute-start(bf16[2,128,768]{2,1,0:T(8,128)(2,1)S(1)} %shard_map.352), channel_id=1, source_target_pairs={{0,8},{4,12},{8,0},{12,4},{16,24},{20,28},{24,16},{28,20},{1,9},{5... | collective-permute-start | bytes 1179656 | tf_op jit(solution)/shard_map/ppermute | solution.py:65
  197.7 15.0 %collective-permute-start.56 = (bf16[2,128,1024]{2,1,0:T(8,128)(2,1)S(1)}, bf16[2,128,1024]{2,1,0:T(8,128)(2,1)S(1)}, u32[]{:S(2)}, u32[]{:S(2)}) collective-permute-start(bf16[2,128,1024]{2,1,0:T(8,128)(2,1)S(1)} %shard_map.346), channel_id=1, source_target_pairs={{0,4},{4,0},{8,12},{12,8},{16,20},{20,16},{24,28},{28,24},{1,5},{5... | collective-permute-start | bytes 1572872 | tf_op jit(solution)/shard_map/ppermute | solution.py:65
  199.2 20.0 %collective-permute-start.57 = (bf16[2,2,128,384]{3,2,1,0:T(8,128)(2,1)S(1)}, bf16[2,2,128,384]{3,2,1,0:T(8,128)(2,1)S(1)}, u32[]{:S(2)}, u32[]{:S(2)}) collective-permute-start(bf16[2,2,128,384]{3,2,1,0:T(8,128)(2,1)S(1)} %shard_map.350), channel_id=1, source_target_pairs={{0,4},{4,0},{8,12},{12,8},{16,20},{20,16},{24,28},{28,24},{1,5},{5... | collective-permute-start | bytes 1179656 | tf_op jit(solution)/shard_map/ppermute | solution.py:65
  199.7 12.9 %collective-permute-start.49 = (bf16[176,1024]{1,0:T(8,128)(2,1)S(1)}, bf16[176,1024]{1,0:T(8,128)(2,1)S(1)}, u32[]{:S(2)}, u32[]{:S(2)}) collective-permute-start(bf16[176,1024]{1,0:T(8,128)(2,1)S(1)} %get-tuple-element.680), channel_id=1, source_target_pairs={{0,1},{1,0},{2,3},{3,2},{4,5},{5,4},{6,7},{7,6},{8,9},{9,8},{10,11... | collective-permute-start | bytes 1081352 | tf_op jit(solution)/shard_map/ppermute | solution.py:65
  199.7 19.9 %collective-permute-start.58 = (bf16[128,1024]{1,0:T(8,128)(2,1)S(1)}, bf16[128,1024]{1,0:T(8,128)(2,1)S(1)}, u32[]{:S(2)}, u32[]{:S(2)}) collective-permute-start(bf16[128,1024]{1,0:T(8,128)(2,1)S(1)} %shard_map.351), channel_id=1, source_target_pairs={{0,16},{4,20},{8,24},{12,28},{16,0},{20,4},{24,8},{28,12},{1,17},{... | collective-permute-start | bytes 786440 | tf_op jit(solution)/shard_map/ppermute | solution.py:65
  209.9 13.5 %collective-permute-start.59 = (bf16[128,768]{1,0:T(8,128)(2,1)S(1)}, bf16[128,768]{1,0:T(8,128)(2,1)S(1)}, u32[]{:S(2)}, u32[]{:S(2)}) collective-permute-start(bf16[128,768]{1,0:T(8,128)(2,1)S(1)} %shard_map.353), channel_id=1, source_target_pairs={{0,16},{4,20},{8,24},{12,28},{16,0},{20,4},{24,8},{28,12},{1,17},{... | collective-permute-start | bytes 589832 | tf_op jit(solution)/shard_map/ppermute | solution.py:65
  224.5 11.3 %collective-permute-start.55 = (bf16[176,1024]{1,0:T(8,128)(2,1)S(1)}, bf16[176,1024]{1,0:T(8,128)(2,1)S(1)}, u32[]{:S(2)}, u32[]{:S(2)}) collective-permute-start(bf16[176,1024]{1,0:T(8,128)(2,1)S(1)} %shard_map.354), channel_id=1, source_target_pairs={{0,2},{1,3},{2,0},{3,1},{4,6},{5,7},{6,4},{7,5},{8,10},{9,11},{10,... | collective-permute-start | bytes 1081352 | tf_op jit(solution)/shard_map/ppermute | solution.py:65
  225.8 17.8 %collective-permute-start.60 = (bf16[128,1024]{1,0:T(8,128)(2,1)S(1)}, bf16[128,1024]{1,0:T(8,128)(2,1)S(1)}, u32[]{:S(2)}, u32[]{:S(2)}) collective-permute-start(bf16[128,1024]{1,0:T(8,128)(2,1)S(1)} %shard_map.356), channel_id=1, source_target_pairs={{0,16},{4,20},{8,24},{12,28},{16,0},{20,4},{24,8},{28,12},{1,17},{... | collective-permute-start | bytes 786440 | tf_op jit(solution)/shard_map/ppermute | solution.py:65
  227.7 17.2 %collective-permute-start.64 = (bf16[2,32,1792]{2,1,0:T(8,128)(2,1)S(1)}, bf16[2,32,1792]{2,1,0:T(8,128)(2,1)S(1)}, u32[]{:S(2)}, u32[]{:S(2)}) collective-permute-start(bf16[2,32,1792]{2,1,0:T(8,128)(2,1)S(1)} %get-tuple-element.719), channel_id=1, source_target_pairs={{0,2},{1,3},{2,0},{3,1},{4,6},{5,7},{6,4},{7,5},{8,10},{9,11},{10,... | collective-permute-start | bytes 688136 | tf_op jit(solution)/shard_map/ppermute | solution.py:65
  228.6 17.3 %collective-permute-start.48 = (bf16[176,1024]{1,0:T(8,128)(2,1)S(1)}, bf16[176,1024]{1,0:T(8,128)(2,1)S(1)}, u32[]{:S(2)}, u32[]{:S(2)}) collective-permute-start(bf16[176,1024]{1,0:T(8,128)(2,1)S(1)} %get-tuple-element.678), channel_id=1, source_target_pairs={{0,1},{1,0},{2,3},{3,2},{4,5},{5,4},{6,7},{7,6},{8,9},{9,8},{10,11... | collective-permute-start | bytes 1081352 | tf_op jit(solution)/shard_map/ppermute | solution.py:65
  (52 other events, 381.5 us)
